TPU v7x, 32 devices: a whole 2x2x4 slice. The times are simulated.
32 devices in a mesh: dp: 8 (over y, x, core), tensor: 4 (over z).
Axes of the slice: x: 2, y: 2, z: 4, core: 2. Of those that a mesh axis runs over, the one named last changes fastest.
Arguments:
- activations: bfloat16 [16, 1024, 1024], P('dp', 'tensor'), may hold values from -6 to 6
- cotangent: bfloat16 [16, 1024, 1024], P('dp', 'tensor'), may hold values from -6 to 6
- attn_gain: float32 [1024], replicated, may hold values from 0.5 to 1.5
- attn_shift: float32 [1024], replicated, may hold values from -2 to 2
- qkv_weight: bfloat16 [1024, 3072], P('dp', 'tensor'), may hold values from -0.1875 to 0.1875
- qkv_bias: float32 [3072], P('tensor'), may hold values from -3 to 3
- out_weight: bfloat16 [1024, 1024], P('dp', 'tensor'), may hold values from -3.5 to 3.5
- out_bias: float32 [1024], replicated, may hold values from -2 to 2
- mlp_gain: float32 [1024], replicated, may hold values from 0.5 to 1.5
- mlp_shift: float32 [1024], replicated, may hold values from -2 to 2
- fc1_weight: bfloat16 [1024, 4096], P('dp', 'tensor'), may hold values from -0.1875 to 0.1875
- fc1_bias: float32 [4096], P('tensor'), may hold values from -3 to 3
- fc2_weight: bfloat16 [1024, 4096], P('dp', 'tensor'), may hold values from -0.09375 to 0.09375
- fc2_bias: float32 [1024], replicated, may hold values from -2 to 2
Outputs:
- output: bfloat16 [16, 1024, 1024], P('dp', 'tensor')
- input_grad: float32 [16, 1024, 1024], P('dp', 'tensor')
- grad_attn_gain: float32 [1024], replicated
- grad_attn_shift: float32 [1024], replicated
- grad_qkv_weight: float32 [1024, 3072], P('dp', 'tensor')
- grad_qkv_bias: float32 [3072], P('tensor')
- grad_out_weight: float32 [1024, 1024], P('dp', 'tensor')
- grad_out_bias: float32 [1024], replicated
- grad_mlp_gain: float32 [1024], replicated
- grad_mlp_shift: float32 [1024], replicated
- grad_fc1_weight: float32 [1024, 4096], P('dp', 'tensor')
- grad_fc1_bias: float32 [4096], P('tensor')
- grad_fc2_weight: float32 [1024, 4096], P('dp', 'tensor')
- grad_fc2_bias: float32 [1024], replicated
All inputs are finite; a program needn't handle non-finite values.
Results may differ from a plain program's by a relative error of at most 0.02.
Values may be sent and summed in bfloat16 or wider, within the bound.
No kernel may reach another device: no remote copies, remote signals or barrier semaphores. Data moves between devices by JAX's collectives and lax.ppermute only.
A program may use at most 192 MiB of HBM per device.

v0:
```python
import math

import jax
import jax.numpy as jnp
from jax import lax
from jax.experimental import pallas as pl
from jax.experimental.pallas import tpu as pltpu
from jax.sharding import PartitionSpec as P

HD = 64
GRID = 16


def norm_rows(values, gain_vec, shift_vec):
    row_mean = jnp.mean(values, axis=-1, keepdims=True)
    centred = values - row_mean
    variance = jnp.mean(centred * centred, axis=-1, keepdims=True)
    return centred * lax.rsqrt(variance + 1e-06) * gain_vec + shift_vec


def rotary_tables(length):
    section = 2 * (HD // 3 // 2)
    half = section // 2
    position = jnp.arange(length)
    frame = (position // (GRID * GRID)).astype(jnp.float32)
    row_pos = (position // GRID % GRID).astype(jnp.float32)
    col_pos = (position % GRID).astype(jnp.float32)
    omega = 1.0 / 10000.0 ** (jnp.arange(half).astype(jnp.float32) / half)
    pieces = [
        jnp.repeat(coordinate[:, None] * omega[None, :], 2, axis=1)
        for coordinate in (frame, row_pos, col_pos)
    ]
    pieces.append(jnp.zeros((length, HD - 3 * section), jnp.float32))
    angles = jnp.concatenate(pieces, axis=1)
    parity = jnp.where(jnp.arange(HD) % 2 == 0, -1.0, 1.0).astype(jnp.float32)
    return (jnp.cos(angles), jnp.sin(angles) * parity)


def pair_swap(values):
    shape = values.shape
    paired = values.reshape(shape[:-1] + (shape[-1] // 2, 2))
    return paired[..., ::-1].reshape(shape)


def contract(left, right, left_dim, right_dim):
    return lax.dot_general(
        left, right, (((left_dim,), (right_dim,)), ((), ())), preferred_element_type=jnp.float32
    )


def exact_gelu(values):
    return jax.nn.gelu(values, approximate=False)


def body(
    activations,
    cotangent,
    attn_gain,
    attn_shift,
    qkv_weight,
    qkv_bias,
    out_weight,
    out_bias,
    mlp_gain,
    mlp_shift,
    fc1_weight,
    fc1_bias,
    fc2_weight,
    fc2_bias,
):
    tensor_size = lax.axis_size("tensor")
    tensor_rank = lax.axis_index("tensor")
    row_count = activations.shape[1]
    width = activations.shape[2]
    length = row_count * tensor_size
    block_rows = min(512, length)
    block_count = length // block_rows
    local_heads = qkv_weight.shape[1] // (3 * HD)
    packed_cols = qkv_weight.shape[1]
    unit_cols = fc1_weight.shape[1]
    factor = 1.0 / math.sqrt(HD)
    cosine, sine = rotary_tables(length)
    cosine = cosine[:, None, :]
    sine = sine[:, None, :]

    def rotate(values):
        return values * cosine + pair_swap(values) * sine

    def rotate_back(values):
        return values * cosine + pair_swap(values * sine)

    def fetch():
        gathered = (
            lax.all_gather(qkv_weight, "dp", axis=0, tiled=True),
            lax.all_gather(out_weight, "dp", axis=0, tiled=True),
            lax.all_gather(fc1_weight, "dp", axis=0, tiled=True),
            lax.all_gather(fc2_weight, "dp", axis=0, tiled=True),
        )
        return (gathered, gathered)

    def seq_gather(values):
        return lax.all_gather(values, "tensor", axis=0, tiled=True)

    def part_sum(values):
        return lax.psum_scatter(
            values.astype(jnp.bfloat16), "tensor", scatter_dimension=0, tiled=True
        ).astype(jnp.float32)

    def grad_gather(values):
        return lax.all_gather(values, "tensor", axis=0, tiled=True)

    def grad_sum(values):
        return lax.psum_scatter(
            values.astype(jnp.bfloat16), "tensor", scatter_dimension=0, tiled=True
        ).astype(jnp.float32)

    def forward(inputs, weights):
        (weight_qkv, weight_out, weight_up, weight_down), (
            whole_qkv,
            whole_out,
            whole_up,
            whole_down,
        ) = weights
        first_all = seq_gather(norm_rows(inputs, attn_gain, attn_shift).astype(jnp.bfloat16))
        packed = (
            jnp.dot(first_all, weight_qkv, preferred_element_type=jnp.float32) + qkv_bias
        ).reshape(length, local_heads, 3, HD)
        query = rotate(packed[:, :, 0]).astype(jnp.bfloat16)
        key_all = rotate(packed[:, :, 1]).astype(jnp.bfloat16)
        value_all = packed[:, :, 2].astype(jnp.bfloat16)
        outputs = []
        log_sums = []
        for block in range(block_count):
            query_block = query[block * block_rows : (block + 1) * block_rows]
            scores = (
                jnp.einsum("qhd,khd->hqk", query_block, key_all, preferred_element_type=jnp.float32)
                * factor
            )
            row_max = jnp.max(scores, axis=-1, keepdims=True)
            expo = jnp.exp(scores - row_max)
            row_total = jnp.sum(expo, axis=-1, keepdims=True)
            weights_low = (expo / row_total).astype(jnp.bfloat16)
            outputs.append(
                jnp.einsum(
                    "hqk,khd->qhd", weights_low, value_all, preferred_element_type=jnp.float32
                )
            )
            log_sums.append(row_max + jnp.log(row_total))
        heads_out = (
            jnp.concatenate(outputs, axis=0).reshape(length, local_heads * HD).astype(jnp.bfloat16)
        )
        log_total = jnp.concatenate(log_sums, axis=1)
        attended = part_sum(contract(heads_out, weight_out, 1, 1))
        resid = inputs + attended + out_bias
        second_all = seq_gather(norm_rows(resid, mlp_gain, mlp_shift).astype(jnp.bfloat16))
        hidden = jnp.dot(second_all, weight_up, preferred_element_type=jnp.float32) + fc1_bias
        act = exact_gelu(hidden).astype(jnp.bfloat16)
        branch = part_sum(contract(act, weight_down, 1, 1))
        result = resid + branch + fc2_bias
        kept = (
            first_all,
            query,
            key_all,
            value_all,
            log_total,
            heads_out,
            heads_out,
            resid,
            second_all,
            hidden,
            act,
        )
        return (result, kept)

    def backward(inputs, grad_low, kept, weights):
        (weight_qkv, weight_out, weight_up, weight_down), (
            whole_qkv,
            whole_out,
            whole_up,
            whole_down,
        ) = weights
        (
            first_all,
            query,
            key_all,
            value_all,
            log_total,
            heads_out,
            heads_rows,
            resid,
            second_all,
            hidden,
            act,
        ) = kept
        grad_top = grad_low.astype(jnp.float32)
        grad_fc2_bias = jnp.sum(grad_top, axis=0)
        grad_all = grad_gather(grad_low)
        grad_fc2_weight = contract(grad_all, act, 0, 0)
        grad_act = jnp.dot(grad_all, weight_down, preferred_element_type=jnp.float32)
        gelu_pull = jax.vjp(exact_gelu, hidden)[1]
        grad_hidden = gelu_pull(grad_act)[0].astype(jnp.bfloat16)
        grad_fc1_bias = jnp.sum(grad_hidden, axis=0, dtype=jnp.float32)
        grad_fc1_weight = contract(second_all, grad_hidden, 0, 0)
        grad_second = grad_sum(contract(grad_hidden, weight_up, 1, 1))
        second_pull = jax.vjp(norm_rows, resid, mlp_gain, mlp_shift)[1]
        grad_resid_norm, grad_mlp_gain, grad_mlp_shift = second_pull(grad_second)
        grad_resid = grad_top + grad_resid_norm
        grad_out_bias = jnp.sum(grad_resid, axis=0)
        resid_low = grad_resid.astype(jnp.bfloat16)
        resid_all = grad_gather(resid_low)
        grad_out_weight = contract(resid_all, heads_out, 0, 0)
        grad_heads = jnp.dot(resid_all, weight_out, preferred_element_type=jnp.float32).astype(
            jnp.bfloat16
        )
        grad_heads = grad_heads.reshape(length, local_heads, HD)
        grad_key = jnp.zeros((length, local_heads, HD), jnp.float32)
        grad_value = jnp.zeros((length, local_heads, HD), jnp.float32)
        query_grads = []
        for block in range(block_count):
            lower = block * block_rows
            upper = lower + block_rows
            query_block = query[lower:upper]
            grad_block = grad_heads[lower:upper]
            scores = (
                jnp.einsum("qhd,khd->hqk", query_block, key_all, preferred_element_type=jnp.float32)
                * factor
            )
            probs = jnp.exp(scores - log_total[:, lower:upper])
            grad_value = grad_value + jnp.einsum(
                "hqk,qhd->khd",
                probs.astype(jnp.bfloat16),
                grad_block,
                preferred_element_type=jnp.float32,
            )
            grad_probs = jnp.einsum(
                "qhd,khd->hqk", grad_block, value_all, preferred_element_type=jnp.float32
            )
            grad_scores = (
                probs * (grad_probs - jnp.sum(probs * grad_probs, axis=-1, keepdims=True))
            ).astype(jnp.bfloat16)
            query_grads.append(
                jnp.einsum("hqk,khd->qhd", grad_scores, key_all, preferred_element_type=jnp.float32)
                * factor
            )
            grad_key = (
                grad_key
                + jnp.einsum(
                    "hqk,qhd->khd", grad_scores, query_block, preferred_element_type=jnp.float32
                )
                * factor
            )
        grad_query = jnp.concatenate(query_grads, axis=0)
        grad_packed = jnp.stack(
            [rotate_back(grad_query), rotate_back(grad_key), grad_value], axis=2
        )
        grad_packed = grad_packed.reshape(length, packed_cols).astype(jnp.bfloat16)
        grad_qkv_bias = jnp.sum(grad_packed, axis=0, dtype=jnp.float32)
        grad_qkv_weight = contract(first_all, grad_packed, 0, 0)
        grad_first = grad_sum(contract(grad_packed, weight_qkv, 1, 1))
        first_pull = jax.vjp(norm_rows, inputs, attn_gain, attn_shift)[1]
        grad_input_norm, grad_attn_gain, grad_attn_shift = first_pull(grad_first)
        input_grad = grad_resid + grad_input_norm
        grads = (
            grad_attn_gain,
            grad_attn_shift,
            grad_qkv_weight,
            grad_qkv_bias,
            grad_out_weight,
            grad_out_bias,
            grad_mlp_gain,
            grad_mlp_shift,
            grad_fc1_weight,
            grad_fc1_bias,
            grad_fc2_weight,
            grad_fc2_bias,
        )
        return (input_grad, grads)

    def per_clip(totals, inputs_pair):
        clip_in, clip_grad = inputs_pair
        forward_weights = fetch()
        result, kept = forward(clip_in.astype(jnp.float32), forward_weights)
        backward_weights = fetch()
        input_grad, grads = backward(clip_in.astype(jnp.float32), clip_grad, kept, backward_weights)
        totals = tuple((left + right for left, right in zip(totals, grads)))
        return (totals, (result.astype(jnp.bfloat16), input_grad))

    out_cols = local_heads * HD
    start_totals = (
        jnp.zeros((width,), jnp.float32),
        jnp.zeros((width,), jnp.float32),
        jnp.zeros((width, packed_cols), jnp.float32),
        jnp.zeros((packed_cols,), jnp.float32),
        jnp.zeros((width, out_cols), jnp.float32),
        jnp.zeros((width,), jnp.float32),
        jnp.zeros((width,), jnp.float32),
        jnp.zeros((width,), jnp.float32),
        jnp.zeros((width, unit_cols), jnp.float32),
        jnp.zeros((unit_cols,), jnp.float32),
        jnp.zeros((width, unit_cols), jnp.float32),
        jnp.zeros((width,), jnp.float32),
    )
    totals, (output, input_grad) = lax.scan(per_clip, start_totals, (activations, cotangent))
    out_grad = totals[4]
    weight_sums = (
        lax.psum_scatter(
            totals[2].astype(jnp.bfloat16), "dp", scatter_dimension=0, tiled=True
        ).astype(jnp.float32),
        lax.psum_scatter(
            out_grad.astype(jnp.bfloat16), "dp", scatter_dimension=0, tiled=True
        ).astype(jnp.float32),
        lax.psum_scatter(
            totals[8].astype(jnp.bfloat16), "dp", scatter_dimension=0, tiled=True
        ).astype(jnp.float32),
        lax.psum_scatter(
            totals[10].astype(jnp.bfloat16), "dp", scatter_dimension=0, tiled=True
        ).astype(jnp.float32),
    )
    qkv_place = lax.dynamic_update_slice_in_dim(
        jnp.zeros((packed_cols * tensor_size,), jnp.float32),
        totals[3],
        tensor_rank * packed_cols,
        0,
    )
    unit_place = lax.dynamic_update_slice_in_dim(
        jnp.zeros((unit_cols * tensor_size,), jnp.float32), totals[9], tensor_rank * unit_cols, 0
    )
    summed = lax.psum(
        (totals[0], totals[1], qkv_place, totals[5], totals[6], totals[7], unit_place, totals[11]),
        ("dp", "tensor"),
    )
    grad_qkv_bias = lax.dynamic_slice_in_dim(summed[2], tensor_rank * packed_cols, packed_cols, 0)
    grad_fc1_bias = lax.dynamic_slice_in_dim(summed[6], tensor_rank * unit_cols, unit_cols, 0)
    return (
        output,
        input_grad,
        summed[0],
        summed[1],
        weight_sums[0],
        grad_qkv_bias,
        weight_sums[1],
        summed[3],
        summed[4],
        summed[5],
        weight_sums[2],
        grad_fc1_bias,
        weight_sums[3],
        summed[7],
    )


def lane_swap(values):
    even = lax.broadcasted_iota(jnp.int32, values.shape, 1) % 2 == 0
    return jnp.where(even, pltpu.roll(values, 127, 1), pltpu.roll(values, 1, 1))


def attend_kernel(first_ref, weight_ref, bias_ref, cos_ref, sin_ref, qkv_ref, heads_ref, turned_ref, log_ref):
    low = jnp.bfloat16
    packed = jnp.dot(first_ref[...], weight_ref[...], preferred_element_type=jnp.float32) + bias_ref[...]
    cosine, sine = cos_ref[...], sin_ref[...]

    def rotate(values):
        return values * cosine + lane_swap(values) * sine

    query = (rotate(packed[:, :128]).astype(low).astype(jnp.float32) * 0.125).astype(low)
    key = rotate(packed[:, 128:256]).astype(low)
    value = packed[:, 256:]
    qkv_ref[:, :128] = query
    qkv_ref[:, 128:256] = key
    qkv_ref[:, 256:] = value.astype(low)
    value = jnp.transpose(value).astype(low)
    first_head = lax.broadcasted_iota(jnp.int32, key.shape, 1) < HD
    for head in range(2):
        mine = slice(head * HD, (head + 1) * HD)
        key_here = jnp.where(first_head == (head == 0), key, jnp.zeros_like(key))
        scores = contract(key_here, query, 1, 1)
        top = jnp.max(scores, axis=0, keepdims=True)
        expo = jnp.exp(scores - top)
        total = jnp.sum(expo, axis=0, keepdims=True)
        summed = jnp.dot(value[mine], expo.astype(low), preferred_element_type=jnp.float32)
        turned_ref[0, mine] = summed / total
        log_ref[0, head : head + 1] = top + jnp.log(total)
    heads_ref[...] = jnp.transpose(turned_ref[0]).astype(low)


def attend(first, weight, bias, cosine, sine):
    length, width = first.shape
    pairs = weight.shape[1] // 384
    return pl.pallas_call(
        attend_kernel,
        grid=(pairs,),
        in_specs=[
            pl.BlockSpec((length, width), lambda i: (0, 0)),
            pl.BlockSpec((width, 384), lambda i: (0, i)),
            pl.BlockSpec((1, 384), lambda i: (0, i)),
            pl.BlockSpec((length, 128), lambda i: (0, 0)),
            pl.BlockSpec((length, 128), lambda i: (0, 0)),
        ],
        out_specs=[
            pl.BlockSpec((length, 384), lambda i: (0, i)),
            pl.BlockSpec((length, 128), lambda i: (0, i)),
            pl.BlockSpec((1, 128, length), lambda i: (i, 0, 0)),
            pl.BlockSpec((1, 2, length), lambda i: (i, 0, 0)),
        ],
        out_shape=[
            jax.ShapeDtypeStruct((length, 384 * pairs), jnp.bfloat16),
            jax.ShapeDtypeStruct((length, 128 * pairs), jnp.bfloat16),
            jax.ShapeDtypeStruct((pairs, 128, length), jnp.float32),
            jax.ShapeDtypeStruct((pairs, 2, length), jnp.float32),
        ],
        name="attend",
    )(first, weight, bias.reshape(1, -1), cosine, sine)


def attend_back_kernel(qkv_ref, grad_ref, turned_ref, log_ref, cos_ref, sin_ref, out_ref, bias_ref):
    low = jnp.bfloat16
    query = qkv_ref[:, :128]
    key = qkv_ref[:, 128:256]
    value = qkv_ref[:, 256:]
    grad = grad_ref[...]
    key_turned = jnp.transpose(key.astype(jnp.float32)).astype(low)
    product = jnp.transpose(grad.astype(jnp.float32)) * turned_ref[0]
    first_head = lax.broadcasted_iota(jnp.int32, key.shape, 1) < HD
    zero = jnp.zeros_like(key)
    query_grads, key_grads, value_grads = [], [], []
    for head in range(2):
        mine = slice(head * HD, (head + 1) * HD)
        here = first_head == (head == 0)
        delta = jnp.sum(product[mine], axis=0, keepdims=True)
        scores = contract(jnp.where(here, key, zero), query, 1, 1)
        probs = jnp.exp(scores - log_ref[0, head : head + 1])
        grad_probs = contract(jnp.where(here, value, zero), grad, 1, 1)
        grad_scores = (probs * (grad_probs - delta)).astype(low)
        value_grads.append(jnp.dot(probs.astype(low), grad, preferred_element_type=jnp.float32))
        key_grads.append(jnp.dot(grad_scores, query, preferred_element_type=jnp.float32))
        query_grads.append(jnp.dot(key_turned[mine], grad_scores, preferred_element_type=jnp.float32))
    cosine, sine = cos_ref[...], sin_ref[...]

    def rotate_back(values):
        return values * cosine + lane_swap(values * sine)

    parts = [
        rotate_back(jnp.transpose(jnp.concatenate(query_grads, axis=0)) * 0.125),
        rotate_back(jnp.where(first_head, key_grads[0], key_grads[1])),
        jnp.where(first_head, value_grads[0], value_grads[1]),
    ]
    for at, part in enumerate(parts):
        part = part.astype(low)
        out_ref[:, at * 128 : (at + 1) * 128] = part
        bias_ref[:, at * 128 : (at + 1) * 128] = jnp.sum(part.astype(jnp.float32), axis=0, keepdims=True)


def attend_back(qkv, grad, turned, logs, cosine, sine):
    length = qkv.shape[0]
    pairs = qkv.shape[1] // 384
    return pl.pallas_call(
        attend_back_kernel,
        grid=(pairs,),
        in_specs=[
            pl.BlockSpec((length, 384), lambda i: (0, i)),
            pl.BlockSpec((length, 128), lambda i: (0, i)),
            pl.BlockSpec((1, 128, length), lambda i: (i, 0, 0)),
            pl.BlockSpec((1, 2, length), lambda i: (i, 0, 0)),
            pl.BlockSpec((length, 128), lambda i: (0, 0)),
            pl.BlockSpec((length, 128), lambda i: (0, 0)),
        ],
        out_specs=[
            pl.BlockSpec((length, 384), lambda i: (0, i)),
            pl.BlockSpec((1, 384), lambda i: (0, i)),
        ],
        out_shape=[
            jax.ShapeDtypeStruct((length, 384 * pairs), jnp.bfloat16),
            jax.ShapeDtypeStruct((1, 384 * pairs), jnp.float32),
        ],
        name="attend_back",
    )(qkv, grad, turned, logs, cosine, sine)


def assemble_kernel(place_ref, own_ref, x_ref, y_ref, even_ref, odd_ref, *out_refs):
    rows = even_ref.shape[0]
    start = 0
    for out_ref in out_refs:
        cols = slice(start, start + out_ref.shape[1])
        start += out_ref.shape[1]
        for at, ref in enumerate((own_ref, x_ref, y_ref)):
            out_ref[pl.ds(pl.multiple_of((at ^ place_ref[0]) * 2 * rows, 2 * rows), 2 * rows)] = ref[:, cols]
        last = (3 ^ place_ref[0]) * 2 * rows
        out_ref[pl.ds(pl.multiple_of(last, rows), rows)] = even_ref[:, cols]
        out_ref[pl.ds(pl.multiple_of(last + rows, rows), rows)] = odd_ref[:, cols]


def assemble(place, pieces, widths):
    rows = pieces[3].shape[0]
    total = sum(widths)
    return pl.pallas_call(
        assemble_kernel,
        grid_spec=pltpu.PrefetchScalarGridSpec(
            num_scalar_prefetch=1,
            grid=(4,),
            in_specs=[pl.BlockSpec((item.shape[0], total), lambda i, place: (0, i)) for item in pieces],
            out_specs=[pl.BlockSpec((8 * rows, cols), lambda i, place: (0, i)) for cols in widths],
        ),
        out_shape=[jax.ShapeDtypeStruct((8 * rows, 4 * cols), jnp.bfloat16) for cols in widths],
        name="assemble",
    )(place, *pieces)


def deal_kernel(place_ref, *refs):
    in_refs, out_refs = refs[:-4], refs[-4:]
    rows = out_refs[0].shape[1]
    start = 0
    for ref in in_refs:
        cols = slice(start, start + ref.shape[1])
        start += ref.shape[1]
        for half, kept_ref, sent_ref, bit in ((0, out_refs[0], out_refs[1], 2), (1, out_refs[2], out_refs[3], 1)):
            for out_ref, from_bit in ((kept_ref, 0), (sent_ref, bit)):
                for at in range(2):
                    block = (at * (3 - bit) + from_bit) ^ place_ref[0]
                    first_row = pl.multiple_of((2 * block + half) * rows, rows)
                    out_ref[at, :, cols] = ref[pl.ds(first_row, rows)]


def deal(place, grads):
    rows = grads[0].shape[0] // 8
    widths = [item.shape[1] // 4 for item in grads]
    total = sum(widths)
    return pl.pallas_call(
        deal_kernel,
        grid_spec=pltpu.PrefetchScalarGridSpec(
            num_scalar_prefetch=1,
            grid=(4,),
            in_specs=[pl.BlockSpec((8 * rows, cols), lambda i, place: (0, i)) for cols in widths],
            out_specs=[pl.BlockSpec((2, rows, total), lambda i, place: (0, 0, i))] * 4,
        ),
        out_shape=[jax.ShapeDtypeStruct((2, rows, 4 * total), jnp.bfloat16)] * 4,
        name="deal",
    )(place, *grads)


def after(values, earlier):
    return lax.optimization_barrier((values, earlier))[0]


EVERY = ("y", "x", "core", "tensor")


def one_clip_per_chip(mesh):
    return mesh.shape["dp"] == 8 and mesh.shape["tensor"] == 4


def swap(values, axis, bit=1):
    return lax.ppermute(values, axis, [(i, i ^ bit) for i in range(4 if axis == "tensor" else 2)])


def clip_routes(back):
    routes = []
    for turn in range(2):
        pairs = []
        for column in range(4):
            for core in range(2):
                for place in range(4):
                    source = (2 * column + core) * 4 + place
                    target = (2 * column + place // 2) * 4 + 2 * core + (turn ^ (place % 2))
                    pairs.append((target, source) if back else (source, target))
        routes.append(pairs)
    return routes


def pick(flag, first, second):
    return jnp.where(flag, second, first)


def to_clips(values):
    odd = lax.axis_index("tensor") % 2 == 1
    arrived = []
    for turn, pairs in enumerate(clip_routes(False)):
        sent = pick(odd, values[turn], values[1 - turn])
        arrived.append(lax.ppermute(sent, EVERY, pairs))
    return jnp.concatenate(
        [pick(odd, arrived[0], arrived[1]), pick(odd, arrived[1], arrived[0])], axis=0
    )


def from_clips(values):
    odd = lax.axis_index("tensor") % 2 == 1
    rows = values.shape[0] // 2
    arrived = []
    for turn, pairs in enumerate(clip_routes(True)):
        sent = pick(odd, values[turn * rows : (turn + 1) * rows], values[(1 - turn) * rows : (2 - turn) * rows])
        arrived.append(lax.ppermute(sent, EVERY, pairs))
    return jnp.stack([pick(odd, arrived[0], arrived[1]), pick(odd, arrived[1], arrived[0])])


def three_parts(values):
    high = lax.reduce_precision(values, 8, 7)
    rest = values - high
    middle = lax.reduce_precision(rest, 8, 7)
    low = rest - middle
    return jnp.stack([high, middle, low]).astype(jnp.bfloat16)


def clip_body(
    activations,
    cotangent,
    attn_gain,
    attn_shift,
    qkv_weight,
    qkv_bias,
    out_weight,
    out_bias,
    mlp_gain,
    mlp_shift,
    fc1_weight,
    fc1_bias,
    fc2_weight,
    fc2_bias,
):
    core, at_x, at_y, at_z = (lax.axis_index(name) for name in ("core", "x", "y", "tensor"))
    place = (2 * at_y + at_x).astype(jnp.int32).reshape(1)
    width = activations.shape[2]
    length = activations.shape[1] * 4
    half_rows = length // 2
    own_rows = qkv_weight.shape[0]
    half_heads = qkv_weight.shape[1] // (6 * HD)
    qkv_cols = half_heads * 3 * HD
    out_cols = out_weight.shape[1] // 2
    unit_cols = fc1_weight.shape[1] // 2
    low = jnp.bfloat16

    def first_half(values):
        return lax.slice_in_dim(values, 0, values.shape[-1] // 2, axis=values.ndim - 1)

    def second_half(values):
        return lax.slice_in_dim(values, values.shape[-1] // 2, values.shape[-1], axis=values.ndim - 1)

    def own_half(values):
        return pick(core == 1, first_half(values), second_half(values))

    def other_half(values):
        return pick(core == 1, second_half(values), first_half(values))

    def by_kind(values):
        lead = values.shape[:-1]
        split = values.reshape(lead + (2, half_heads, 3, HD))
        return jnp.swapaxes(split, -3, -2).reshape(values.shape)

    def by_head(values):
        lead = values.shape[:-1]
        split = values.reshape(lead + (2, 3, half_heads, HD))
        return jnp.swapaxes(split, -3, -2).reshape(values.shape)

    columns = (by_kind(qkv_weight), out_weight, fc1_weight, fc2_weight)
    mine = jnp.concatenate([own_half(item) for item in columns], axis=1)
    theirs = swap(jnp.concatenate([other_half(item) for item in columns], axis=1), "core")
    held = jnp.concatenate([pick(core == 1, mine, theirs), pick(core == 1, theirs, mine)], axis=0)

    def along_z(own):
        one = swap(own, "tensor", 1)
        two = swap(own, "tensor", 2)
        return [own, one, two, swap(two, "tensor", 1)]

    def over_plane(blocks):
        own = jnp.concatenate(blocks, axis=1)
        from_x, from_y = swap(own, "x"), swap(own, "y")
        return own, from_x, from_y, swap(from_y[:own_rows], "x"), swap(from_x[own_rows:], "y")

    lines = jnp.concatenate([own_half(by_kind(qkv_bias)), own_half(fc1_bias)])
    lines = jnp.pad(three_parts(lines), ((0, 0), (0, 3 * qkv_cols - lines.shape[0]))).reshape(9, qkv_cols)
    blocks = along_z(jnp.concatenate([held[:, :qkv_cols], lines, jnp.zeros((7, qkv_cols), low)], axis=0))
    tokens = to_clips(activations).astype(jnp.float32)
    lines = jnp.stack([item[2 * own_rows : 2 * own_rows + 9] for item in blocks])
    lines = lines.astype(jnp.float32).reshape(4, 3, 3 * qkv_cols).sum(axis=1)
    bias_qkv = lines[:, :qkv_cols].reshape(-1)
    bias_up = lines[:, qkv_cols : qkv_cols + unit_cols].reshape(-1)
    pieces = over_plane([item[: 2 * own_rows] for item in blocks])
    (weight_qkv,) = assemble(place, pieces, [qkv_cols])

    blocks = along_z(after(held[:, qkv_cols : qkv_cols + out_cols + unit_cols], blocks[3]))
    blocks[0] = after(blocks[0], pieces[2])
    pieces = over_plane(blocks)
    weight_out, weight_up = assemble(place, pieces, [out_cols, unit_cols])

    blocks = along_z(after(held[:, qkv_cols + out_cols + unit_cols :], blocks[3]))
    blocks[0] = after(blocks[0], pieces[2])
    grad_own = to_clips(after(cotangent, blocks[3]))
    (weight_down,) = assemble(place, over_plane(blocks), [unit_cols])

    def both_halves(values):
        other = swap(values, "core")
        return jnp.concatenate([pick(core == 1, values, other), pick(core == 1, other, values)], axis=0)

    def part_sum(values):
        halves = values.reshape((2, half_rows) + values.shape[1:])
        sent = pick(core == 1, halves[1], halves[0]).astype(low)
        return pick(core == 1, halves[0], halves[1]) + swap(sent, "core").astype(jnp.float32)

    cosine, sine = (jnp.concatenate([item, item], axis=1) for item in rotary_tables(length))

    first_all = both_halves(norm_rows(tokens, attn_gain, attn_shift).astype(low))
    qkv, heads_out, turned, log_total = attend(first_all, weight_qkv, bias_qkv, cosine, sine)
    resid = tokens + part_sum(contract(heads_out, weight_out, 1, 1)) + out_bias
    second_all = both_halves(norm_rows(resid, mlp_gain, mlp_shift).astype(low))
    hidden = jnp.dot(second_all, weight_up, preferred_element_type=jnp.float32) + bias_up
    act = exact_gelu(hidden).astype(low)
    result = resid + part_sum(contract(act, weight_down, 1, 1)) + fc2_bias
    output = from_clips(result.astype(low))

    def to_core(total):
        kept = pick(core == 1, total[0], total[1])
        came = swap(pick(core == 1, total[1], total[0]), "core")
        return jnp.concatenate(
            [pick(core == 1, kept, came), pick(core == 1, came, kept)], axis=-1
        ).astype(jnp.float32)

    def over_plane_back(grads, waits):
        kept_even, sent_even, kept_odd, sent_odd = deal(place, [item.astype(low) for item in grads])
        even = kept_even + after(swap(sent_even, "y"), waits[0])
        odd = kept_odd + after(swap(sent_odd, "x"), waits[0])
        even = even[0] + after(swap(even[1], "x"), waits[1])
        odd = odd[0] + after(swap(odd[1], "y"), waits[1])
        return jnp.concatenate([even, odd])

    def along_z_back(total, wait):
        cols = total.shape[1] // 4
        own, one, two, three = (total[:, at * cols : (at + 1) * cols] for at in range(4))
        one = swap(one, "tensor", 1)
        two = swap(two + after(swap(three, "tensor", 1), wait), "tensor", 2)
        return to_core((own + one + two).reshape(2, own_rows, cols))

    grad_top = grad_own.astype(jnp.float32)
    grad_all = both_halves(grad_own)
    sum_fc2_bias = jnp.sum(grad_top, axis=0)
    grad_fc2 = contract(grad_all, act, 0, 0)
    grad_act = jnp.dot(grad_all, weight_down, preferred_element_type=jnp.float32)
    grad_hidden = jax.vjp(exact_gelu, hidden)[1](grad_act)[0].astype(low)
    sum_fc1_bias = jnp.sum(grad_hidden, axis=0, dtype=jnp.float32)
    grad_fc1 = contract(second_all, grad_hidden, 0, 0)
    grad_second_part = contract(grad_hidden, weight_up, 1, 1)
    grad_second = part_sum(grad_second_part)
    second_pull = jax.vjp(norm_rows, resid, mlp_gain, mlp_shift)[1]
    grad_resid_norm, sum_mlp_gain, sum_mlp_shift = second_pull(grad_second)
    grad_resid = grad_top + grad_resid_norm
    sum_out_bias = jnp.sum(grad_resid, axis=0)
    resid_all = both_halves(grad_resid.astype(low))
    grad_out = contract(resid_all, heads_out, 0, 0)
    grad_heads = jnp.dot(resid_all, weight_out, preferred_element_type=jnp.float32).astype(low)
    grad_packed, sum_qkv_bias = attend_back(qkv, grad_heads, turned, log_total, cosine, sine)
    grad_qkv = contract(first_all, grad_packed, 0, 0)
    grad_first_part = contract(grad_packed, weight_qkv, 1, 1)
    grad_first = part_sum(grad_first_part)
    first_pull = jax.vjp(norm_rows, tokens, attn_gain, attn_shift)[1]
    grad_input_norm, sum_attn_gain, sum_attn_shift = first_pull(grad_first)
    input_grad = from_clips((grad_resid + grad_input_norm).astype(low)).astype(jnp.float32)

    total = over_plane_back([grad_fc2], [grad_second_part, grad_packed])
    grad_fc2_weight = along_z_back(total, grad_first_part)
    total = over_plane_back([grad_out, grad_fc1], [grad_packed, grad_first_part])
    both_weights = along_z_back(total, grad_first)
    cuts = both_weights.shape[1] // 2
    both_weights = [both_weights[:, :cuts], both_weights[:, cuts:]]
    grad_out_weight = jnp.concatenate([item[:, :out_cols] for item in both_weights], axis=1)
    grad_fc1_weight = jnp.concatenate([item[:, out_cols:] for item in both_weights], axis=1)
    total = over_plane_back([grad_qkv], [grad_first_part, grad_first])
    grad_qkv_weight = by_head(along_z_back(total, grad_first))

    def by_core(values):
        none = jnp.zeros_like(values)
        return [pick(core == 1, values, none), pick(core == 1, none, values)]

    def by_owner(values, cols):
        first, second, third, fourth = (values.reshape(-1)[at * cols : (at + 1) * cols] for at in range(4))
        odd = at_z % 2 == 1
        first, second = pick(odd, first, second), pick(odd, second, first)
        third, fourth = pick(odd, third, fourth), pick(odd, fourth, third)
        lower, upper = jnp.concatenate([first, second]), jnp.concatenate([third, fourth])
        far = at_z // 2 == 1
        return jnp.concatenate([pick(far, lower, upper), pick(far, upper, lower)])

    sums = [sum_attn_gain, sum_attn_shift, sum_out_bias, sum_mlp_gain, sum_mlp_shift, sum_fc2_bias]
    sums = jnp.concatenate(sums + by_core(by_owner(sum_qkv_bias, qkv_cols)) + by_core(by_owner(sum_fc1_bias, unit_cols)))
    for axis, bit in (("core", 1), ("x", 1), ("y", 1), ("tensor", 1), ("tensor", 2)):
        sums = sums + swap(sums, axis, bit)
    vectors = sums[: 6 * width].reshape(6, width)
    qkv_sums = sums[6 * width : 6 * width + 8 * qkv_cols].reshape(2, 4, qkv_cols)
    unit_sums = sums[6 * width + 8 * qkv_cols :].reshape(2, 4, unit_cols)

    def own_place(values):
        return lax.dynamic_index_in_dim(values, at_z, 1, keepdims=False).reshape(-1)

    return (
        output,
        input_grad,
        vectors[0],
        vectors[1],
        grad_qkv_weight,
        by_head(own_place(qkv_sums)),
        grad_out_weight,
        vectors[2],
        vectors[3],
        vectors[4],
        grad_fc1_weight,
        own_place(unit_sums),
        grad_fc2_weight,
        vectors[5],
    )


def solution(mesh):
    if one_clip_per_chip(mesh):
        plan, rows = clip_body, ("y", "x", "core")
        mesh = jax.sharding.Mesh(mesh.devices.reshape(2, 2, 2, 4), EVERY)
    else:
        plan, rows = body, "dp"
    tokens, matrix, columns = P(rows, "tensor", None), P(rows, "tensor"), P("tensor")
    params = (P(), P(), matrix, columns, matrix, P(), P(), P(), matrix, columns, matrix, P())
    both = (tokens, tokens) + params
    return jax.shard_map(plan, mesh=mesh, in_specs=both, out_specs=both, check_vma=False)
```

profile of v0, /device:TPU:1, one launch (start us, length us, event | category | flops | bytes accessed | tf_op | source)
XLA Modules:
  0.0 576.4 jit_solution(18332055900095711987)
XLA Ops:
  16.1 15.7 %collective-permute-done.5 = bf16[272,384]{1,0:T(8,128)(2,1)S(1)} collective-permute-done((bf16[272,384]{1,0:T(8,128)(2,1)}, bf16[272,384]{1,0:T(8,128)(2,1)S(1)}, u32[]{:S(2)}, u32[]{:S(2)}) %collective-permute-start.5) | collective-permute-done | bytes 208928 | tf_op jit(solution)/shard_map/ppermute | solution.py:552
  31.8 8.5 %collective-permute-start.6 = (bf16[272,384]{1,0:T(8,128)(2,1)S(1)}, bf16[272,384]{1,0:T(8,128)(2,1)S(1)}, u32[]{:S(2)}, u32[]{:S(2)}) collective-permute-start(bf16[272,384]{1,0:T(8,128)(2,1)S(1)} %collective-permute-done.5), channel_id=1, source_target_pairs={{0,1},{1,0},{2,3},{3,2},{4,5},{5,4},{6,7},{7,6},{8,9},{9,8},{10,11... | collective-permute-start | bytes 626696 | tf_op jit(solution)/shard_map/ppermute | solution.py:552
  54.0 13.7 %collective-permute-done.12 = bf16[256,640]{1,0:T(8,128)(2,1)S(1)} collective-permute-done((bf16[256,640]{1,0:T(8,128)(2,1)S(1)}, bf16[256,640]{1,0:T(8,128)(2,1)S(1)}, u32[]{:S(2)}, u32[]{:S(2)}) %collective-permute-start.12) | collective-permute-done | bytes 327712 | tf_op jit(solution)/shard_map/ppermute | solution.py:552
  70.2 6.2 %collective-permute-done.13 = bf16[256,640]{1,0:T(8,128)(2,1)S(1)} collective-permute-done((bf16[256,640]{1,0:T(8,128)(2,1)S(1)}, bf16[256,640]{1,0:T(8,128)(2,1)S(1)}, u32[]{:S(2)}, u32[]{:S(2)}) %collective-permute-start.13) | collective-permute-done | bytes 327712 | tf_op jit(solution)/shard_map/ppermute | solution.py:552
  89.8 11.9 %collective-permute-done.21 = bf16[256,512]{1,0:T(8,128)(2,1)} collective-permute-done((bf16[256,512]{1,0:T(8,128)(2,1)}, bf16[256,512]{1,0:T(8,128)(2,1)}, u32[]{:S(2)}, u32[]{:S(2)}) %collective-permute-start.21) | collective-permute-done | bytes 262176 | tf_op jit(solution)/shard_map/ppermute | solution.py:552
  113.6 9.6 %collective-permute-done.7.x_ref = bf16[256,1536]{1,0:T(8,128)(2,1)} collective-permute-done((bf16[256,1536]{1,0:T(8,128)(2,1)}, bf16[256,1536]{1,0:T(8,128)(2,1)}, u32[]{:S(2)}, u32[]{:S(2)}) %collective-permute-start.7) | collective-permute-done | bytes 786464 | tf_op jit(solution)/shard_map/ppermute | solution.py:552
  127.3 6.5 %collective-permute-start.30 = (bf16[256,1024]{1,0:T(8,128)(2,1)S(1)}, bf16[256,1024]{1,0:T(8,128)(2,1)S(1)}, u32[]{:S(2)}, u32[]{:S(2)}) collective-permute-start(bf16[256,1024]{1,0:T(8,128)(2,1)S(1)} %get-tuple-element.179), channel_id=1, source_target_pairs={{0,1},{1,0},{2,5},{3,4},{4,3},{5,2},{6,7},{7,6},{8,9},{9,8},{10,13... | collective-permute-start | bytes 1572872 | tf_op jit(solution)/shard_map/ppermute | solution.py:578
  133.8 11.8 %collective-permute-done.9.even_ref = bf16[128,1536]{1,0:T(8,128)(2,1)S(1)} collective-permute-done((bf16[128,1536]{1,0:T(8,128)(2,1)S(1)}, bf16[128,1536]{1,0:T(8,128)(2,1)S(1)}, u32[]{:S(2)}, u32[]{:S(2)}) %collective-permute-start.9) | collective-permute-done | bytes 393248 | tf_op jit(solution)/shard_map/ppermute | solution.py:552
  154.6 20.4 %attend.1 = (bf16[1024,1536]{1,0:T(8,128)(2,1)}, bf16[1024,512]{1,0:T(8,128)(2,1)}, f32[4,128,1024]{2,1,0:T(8,128)}, f32[4,2,1024]{2,1,0:T(2,128)}) custom-call(bf16[1024,1024]{1,0:T(8,128)(2,1)} %pad_maximum_fusion.first_ref, bf16[1024,1536]{1,0:T(8,128)(2,1)} %assemble.3.weight_ref, f32[1,1536]{1,0:T(1,128)} %bitcast.102, ...), custom_call_target="tpu_custom_call" | custom-call | tf_op jit(solution)/shard_map/attend/pallas_call | solution.py:389
  202.3 16.8 %collective-permute-done.24.y_ref = bf16[256,2048]{1,0:T(8,128)(2,1)} collective-permute-done((bf16[256,2048]{1,0:T(8,128)(2,1)}, bf16[256,2048]{1,0:T(8,128)(2,1)}, u32[]{:S(2)}, u32[]{:S(2)}) %collective-permute-start.24) | collective-permute-done | bytes 1048608 | tf_op jit(solution)/shard_map/ppermute | solution.py:552
  241.1 25.3 %multiply_convert_fusion = (bf16[1024,2048]{1,0:T(8,128)(2,1)S(1)}, f32[1024,2048]{1,0:T(8,128)}, f32[1024,2048]{1,0:T(8,128)}) fusion(f32[2048]{0:T(1024)S(1)} %bitcast.105, bf16[1024,2048]{1,0:T(8,128)(2,1)S(1)} %copy-done.63, bf16[512,1024]{1,0:T(8,128)(2,1)S(1)} %get-tuple-element.166, bf16[512,1024]{1,0:T(8,128)(2,1)S(1)} %get-tuple-element.165), kind=kOutput, calls=%fused_computation.4 | convolution fusion | flops 4437573632 | bytes 27271168 | tf_op jit(solution)/shard_map/dot_general | solution.py:703
  271.0 6.3 %convolution_convert_fusion.1.refs_0_ = bf16[1024,2048]{1,0:T(8,128)(2,1)} fusion(bf16[1024,2048]{1,0:T(8,128)(2,1)S(1)} %get-tuple-element.153, bf16[512,1024]{1,0:T(8,128)(2,1)S(1)} %copy-done.34, bf16[512,1024]{1,0:T(8,128)(2,1)S(1)} %copy-done.33), kind=kOutput, calls=%fused_computation.19 | convolution fusion | flops 4301258752 | bytes 10485760 | tf_op jit(solution)/shard_map/dot_general | solution.py:46
  277.3 13.4 %convert_reduce_fusion = (f32[2048]{0:T(1024)S(1)}, bf16[1024,2048]{1,0:T(8,128)(2,1)}) fusion(f32[1024,2048]{1,0:T(8,128)} %get-tuple-element.154, bf16[1024,2048]{1,0:T(8,128)(2,1)S(1)} %copy-done.17, bf16[512,1024]{1,0:T(8,128)(2,1)S(1)} %copy-done.34, bf16[512,1024]{1,0:T(8,128)(2,1)S(1)} %copy-done.33, f32[1024,2048]{1,0:T(8,128)} %get-tuple-element.233, ...), kind=kOutput, calls=%fused_computation.2 | convolution fusion | flops 4334811136 | bytes 27279360 | tf_op jit(solution)/shard_map/dot_general | solution.py:734
  290.7 6.8 %fusion.90 = f32[1024,1024]{1,0:T(8,128)S(1)} fusion(bf16[1024,2048]{1,0:T(8,128)(2,1)} %get-tuple-element.235, bf16[1024,2048]{1,0:T(8,128)(2,1)S(1)} %copy-done.63), kind=kOutput, calls=%fused_computation.300 | convolution fusion | flops 4294967296 | bytes 12582912 | tf_op jit(solution)/shard_map/dot_general | solution.py:46
  303.9 6.3 %convolution_convert_fusion.2.refs_1_ = bf16[1024,2048]{1,0:T(8,128)(2,1)} fusion(bf16[1024,2048]{1,0:T(8,128)(2,1)S(1)} %copy-done.66, bf16[512,1024]{1,0:T(8,128)(2,1)S(1)} %get-tuple-element.166, bf16[512,1024]{1,0:T(8,128)(2,1)S(1)} %get-tuple-element.165), kind=kOutput, calls=%fused_computation.20 | convolution fusion | flops 4301258752 | bytes 10485760 | tf_op jit(solution)/shard_map/dot_general | solution.py:46
  322.9 15.8 %collective-permute-done.59 = bf16[2,128,2048]{2,1,0:T(8,128)(2,1)S(1)} collective-permute-done((bf16[2,128,2048]{2,1,0:T(8,128)(2,1)}, bf16[2,128,2048]{2,1,0:T(8,128)(2,1)S(1)}, u32[]{:S(2)}, u32[]{:S(2)}) %collective-permute-start.59) | collective-permute-done | bytes 1048608 | tf_op jit(solution)/shard_map/ppermute | solution.py:552
  354.0 11.3 %collective-permute-done.29 = bf16[256,1024]{1,0:T(8,128)(2,1)S(1)} collective-permute-done((bf16[256,1024]{1,0:T(8,128)(2,1)S(1)}, bf16[256,1024]{1,0:T(8,128)(2,1)S(1)}, u32[]{:S(2)}, u32[]{:S(2)}) %collective-permute-start.29) | collective-permute-done | bytes 524320 | tf_op jit(solution)/shard_map/ppermute | solution.py:590
  370.3 25.9 %attend_back.1 = (bf16[1024,1536]{1,0:T(8,128)(2,1)}, f32[1,1536]{1,0:T(1,128)}) custom-call(bf16[1024,1536]{1,0:T(8,128)(2,1)} %get-tuple-element.62.qkv_ref, bf16[1024,512]{1,0:T(8,128)(2,1)} %convolution_convert_fusion.4.grad_ref, f32[4,128,1024]{2,1,0:T(8,128)} %get-tuple-element.63.turned_ref, f32[4,2,1024]{2,1,0:T(2,128)} %get-tuple-element.64.log_ref, ...), custom_call_target="tpu_custom_call" | custom-call | tf_op jit(solution)/shard_map/attend_back/pallas_call | solution.py:456
  396.2 8.4 %fusion.91 = f32[1024,1024]{1,0:T(8,128)} fusion(bf16[1024,1536]{1,0:T(8,128)(2,1)} %get-tuple-element.65, bf16[1024,1536]{1,0:T(8,128)(2,1)} %assemble.3.weight_ref), kind=kOutput, calls=%fused_computation.301 | convolution fusion | flops 3221225472 | bytes 10485760 | tf_op jit(solution)/shard_map/dot_general | solution.py:46
  425.7 12.7 %collective-permute-done.65 = bf16[256,512]{1,0:T(8,128)(2,1)S(1)} collective-permute-done((bf16[256,512]{1,0:T(8,128)(2,1)S(1)}, bf16[256,512]{1,0:T(8,128)(2,1)S(1)}, u32[]{:S(2)}, u32[]{:S(2)}) %collective-permute-start.65) | collective-permute-done | bytes 262176 | tf_op jit(solution)/shard_map/ppermute | solution.py:552
  450.6 8.6 %collective-permute-done.45 = bf16[2,128,1536]{2,1,0:T(8,128)(2,1)} collective-permute-done((bf16[2,128,1536]{2,1,0:T(8,128)(2,1)}, bf16[2,128,1536]{2,1,0:T(8,128)(2,1)}, u32[]{:S(2)}, u32[]{:S(2)}) %collective-permute-start.45) | collective-permute-done | bytes 786464 | tf_op jit(solution)/shard_map/ppermute | solution.py:552
  467.9 29.0 %collective-permute-done.39 = f32[13312]{0:T(1024)S(1)} collective-permute-done((f32[13312]{0:T(1024)S(1)}, f32[13312]{0:T(1024)S(1)}, u32[]{:S(2)}, u32[]{:S(2)}) %collective-permute-start.39) | collective-permute-done | bytes 53280 | tf_op jit(solution)/shard_map/ppermute | solution.py:552
  506.9 9.5 %collective-permute-done.41 = f32[13312]{0:T(1024)S(1)} collective-permute-done((f32[13312]{0:T(1024)S(1)}, f32[13312]{0:T(1024)S(1)}, u32[]{:S(2)}, u32[]{:S(2)}) %collective-permute-start.41) | collective-permute-done | bytes 53280 | tf_op jit(solution)/shard_map/ppermute | solution.py:552
  564.2 9.1 %collective-permute-start.58 = (bf16[128,640]{1,0:T(8,128)(2,1)S(1)}, bf16[128,640]{1,0:T(8,128)(2,1)S(1)}, u32[]{:S(2)}, u32[]{:S(2)}) collective-permute-start(bf16[128,640]{1,0:T(8,128)(2,1)S(1)} %broadcast_select_fusion.21), channel_id=1, source_target_pairs={{0,4},{4,0},{1,5},{5,1},{2,6},{6,2},{3,7},{7,3},{8,12},{12,8},{9,1... | collective-permute-start | bytes 491528 | tf_op jit(solution)/shard_map/ppermute | solution.py:552
  (451 shorter events, 264.5 us)
Async XLA Ops:
  4.1 42.4 %collective-permute-start = (bf16[256,1024]{1,0:T(8,128)(2,1)}, bf16[256,1024]{1,0:T(8,128)(2,1)S(1)}, u32[]{:S(2)}, u32[]{:S(2)}) collective-permute-start(bf16[256,1024]{1,0:T(8,128)(2,1)} %get-tuple-element.187), channel_id=1, source_target_pairs={{0,1},{1,0},{2,5},{3,4},{4,3},{5,2},{6,7},{7,6},{8,9},{9,8},{10,13... | collective-permute-start | bytes 1572872 | tf_op jit(solution)/shard_map/ppermute | solution.py:578
  8.8 37.7 %collective-permute-start.1 = (bf16[256,1024]{1,0:T(8,128)(2,1)S(1)}, bf16[256,1024]{1,0:T(8,128)(2,1)}, u32[]{:S(2)}, u32[]{:S(2)}) collective-permute-start(bf16[256,1024]{1,0:T(8,128)(2,1)S(1)} %get-tuple-element.188), channel_id=1, source_target_pairs={{0,0},{1,1},{2,4},{3,5},{4,2},{5,3},{6,6},{7,7},{8,8},{9,9},{10,12... | collective-permute-start | bytes 1572872 | tf_op jit(solution)/shard_map/ppermute | solution.py:578
  77.4 32.2 %collective-permute-start.14 = (bf16[256,2560]{1,0:T(8,128)(2,1)}, bf16[256,2560]{1,0:T(8,128)(2,1)}, u32[]{:S(2)}, u32[]{:S(2)}) collective-permute-start(bf16[256,2560]{1,0:T(8,128)(2,1)} %constant_dynamic-update-slice_fusion.own_ref), channel_id=1, source_target_pairs={{0,8},{8,0},{1,9},{9,1},{2,10},{10,2},{3,11},{11,3},{4,12},{12,4},... | collective-permute-start | bytes 3932168 | tf_op jit(solution)/shard_map/ppermute | solution.py:552
  79.1 32.8 %collective-permute-start.2 = (bf16[512,1024]{1,0:T(8,128)(2,1)S(1)}, bf16[512,1024]{1,0:T(8,128)(2,1)}, u32[]{:S(2)}, u32[]{:S(2)}) collective-permute-start(bf16[512,1024]{1,0:T(8,128)(2,1)S(1)} %fusion.13), channel_id=1, source_target_pairs={{0,4},{4,0},{1,5},{5,1},{2,6},{6,2},{3,7},{7,3},{8,12},{12,8},{9,1... | collective-permute-start | bytes 3145736 | tf_op jit(solution)/shard_map/ppermute | solution.py:552
  85.8 37.4 %collective-permute-start.7 = (bf16[256,1536]{1,0:T(8,128)(2,1)}, bf16[256,1536]{1,0:T(8,128)(2,1)}, u32[]{:S(2)}, u32[]{:S(2)}) collective-permute-start(bf16[256,1536]{1,0:T(8,128)(2,1)} %pad_maximum_fusion.15.own_ref), channel_id=1, source_target_pairs={{0,8},{8,0},{1,9},{9,1},{2,10},{10,2},{3,11},{11,3},{4,12},{12,4},... | collective-permute-start | bytes 2359304 | tf_op jit(solution)/shard_map/ppermute | solution.py:552
  108.4 66.6 %collective-permute-start.16 = (bf16[128,2560]{1,0:T(8,128)(2,1)}, bf16[128,2560]{1,0:T(8,128)(2,1)}, u32[]{:S(2)}, u32[]{:S(2)}) collective-permute-start(bf16[128,2560]{1,0:T(8,128)(2,1)} %slice.462), channel_id=1, source_target_pairs={{0,8},{8,0},{1,9},{9,1},{2,10},{10,2},{3,11},{11,3},{4,12},{12,4},... | collective-permute-start | bytes 1966088 | tf_op jit(solution)/shard_map/ppermute | solution.py:552
  111.6 63.4 %collective-permute-start.17 = (bf16[128,2560]{1,0:T(8,128)(2,1)}, bf16[128,2560]{1,0:T(8,128)(2,1)}, u32[]{:S(2)}, u32[]{:S(2)}) collective-permute-start(bf16[128,2560]{1,0:T(8,128)(2,1)} %slice.463), channel_id=1, source_target_pairs={{0,16},{16,0},{1,17},{17,1},{2,18},{18,2},{3,19},{19,3},{4,20},{20... | collective-permute-start | bytes 1966088 | tf_op jit(solution)/shard_map/ppermute | solution.py:552
  113.3 32.3 %collective-permute-start.9 = (bf16[128,1536]{1,0:T(8,128)(2,1)S(1)}, bf16[128,1536]{1,0:T(8,128)(2,1)S(1)}, u32[]{:S(2)}, u32[]{:S(2)}) collective-permute-start(bf16[128,1536]{1,0:T(8,128)(2,1)S(1)} %slice.456), channel_id=1, source_target_pairs={{0,8},{8,0},{1,9},{9,1},{2,10},{10,2},{3,11},{11,3},{4,12},{12,4},... | collective-permute-start | bytes 1179656 | tf_op jit(solution)/shard_map/ppermute | solution.py:552
  127.3 57.6 %collective-permute-start.30 = (bf16[256,1024]{1,0:T(8,128)(2,1)S(1)}, bf16[256,1024]{1,0:T(8,128)(2,1)S(1)}, u32[]{:S(2)}, u32[]{:S(2)}) collective-permute-start(bf16[256,1024]{1,0:T(8,128)(2,1)S(1)} %get-tuple-element.179), channel_id=1, source_target_pairs={{0,1},{1,0},{2,5},{3,4},{4,3},{5,2},{6,7},{7,6},{8,9},{9,8},{10,13... | collective-permute-start | bytes 1572872 | tf_op jit(solution)/shard_map/ppermute | solution.py:578
  145.6 39.2 %collective-permute-start.31 = (bf16[256,1024]{1,0:T(8,128)(2,1)S(1)}, bf16[256,1024]{1,0:T(8,128)(2,1)S(1)}, u32[]{:S(2)}, u32[]{:S(2)}) collective-permute-start(bf16[256,1024]{1,0:T(8,128)(2,1)S(1)} %get-tuple-element.180), channel_id=1, source_target_pairs={{0,0},{1,1},{2,4},{3,5},{4,2},{5,3},{6,6},{7,7},{8,8},{9,9},{10,12... | collective-permute-start | bytes 1572872 | tf_op jit(solution)/shard_map/ppermute | solution.py:578
  186.2 38.4 %collective-permute-start.32 = (bf16[512,1024]{1,0:T(8,128)(2,1)}, bf16[512,1024]{1,0:T(8,128)(2,1)}, u32[]{:S(2)}, u32[]{:S(2)}) collective-permute-start(bf16[512,1024]{1,0:T(8,128)(2,1)} %pad_maximum_fusion.14), channel_id=1, source_target_pairs={{0,4},{4,0},{1,5},{5,1},{2,6},{6,2},{3,7},{7,3},{8,12},{12,8},{9,1... | collective-permute-start | bytes 3145736 | tf_op jit(solution)/shard_map/ppermute | solution.py:552
  200.5 38.1 %collective-permute-start.19 = (bf16[512,1024]{1,0:T(8,128)(2,1)}, bf16[512,1024]{1,0:T(8,128)(2,1)}, u32[]{:S(2)}, u32[]{:S(2)}) collective-permute-start(bf16[512,1024]{1,0:T(8,128)(2,1)} %add_convert_fusion.3), channel_id=1, source_target_pairs={{0,4},{4,0},{1,5},{5,1},{2,6},{6,2},{3,7},{7,3},{8,12},{12,8},{9,1... | collective-permute-start | bytes 3145736 | tf_op jit(solution)/shard_map/ppermute | solution.py:552
  316.2 30.8 %collective-permute-start.61 = (bf16[2,128,2048]{2,1,0:T(8,128)(2,1)}, bf16[2,128,2048]{2,1,0:T(8,128)(2,1)S(1)}, u32[]{:S(2)}, u32[]{:S(2)}) collective-permute-start(bf16[2,128,2048]{2,1,0:T(8,128)(2,1)} %get-tuple-element.90), channel_id=1, source_target_pairs={{0,8},{8,0},{1,9},{9,1},{2,10},{10,2},{3,11},{11,3},{4,12},{12,4},... | collective-permute-start | bytes 3145736 | tf_op jit(solution)/shard_map/ppermute | solution.py:552
  346.8 62.9 %collective-permute-start.60 = (bf16[128,2048]{1,0:T(8,128)(2,1)}, bf16[128,2048]{1,0:T(8,128)(2,1)}, u32[]{:S(2)}, u32[]{:S(2)}) collective-permute-start(bf16[128,2048]{1,0:T(8,128)(2,1)} %slice_bitcast_fusion.6), channel_id=1, source_target_pairs={{0,8},{8,0},{1,9},{9,1},{2,10},{10,2},{3,11},{11,3},{4,12},{12,4},... | collective-permute-start | bytes 1572872 | tf_op jit(solution)/shard_map/ppermute | solution.py:552
  348.3 61.3 %collective-permute-start.62 = (bf16[128,2048]{1,0:T(8,128)(2,1)}, bf16[128,2048]{1,0:T(8,128)(2,1)S(1)}, u32[]{:S(2)}, u32[]{:S(2)}) collective-permute-start(bf16[128,2048]{1,0:T(8,128)(2,1)} %slice_bitcast_fusion.4), channel_id=1, source_target_pairs={{0,16},{16,0},{1,17},{17,1},{2,18},{18,2},{3,19},{19,3},{4,20},{20... | collective-permute-start | bytes 1572872 | tf_op jit(solution)/shard_map/ppermute | solution.py:552
  417.4 31.3 %collective-permute-start.43 = (bf16[2,128,1536]{2,1,0:T(8,128)(2,1)}, bf16[2,128,1536]{2,1,0:T(8,128)(2,1)}, u32[]{:S(2)}, u32[]{:S(2)}) collective-permute-start(bf16[2,128,1536]{2,1,0:T(8,128)(2,1)} %get-tuple-element.68), channel_id=1, source_target_pairs={{0,16},{16,0},{1,17},{17,1},{2,18},{18,2},{3,19},{19,3},{4,20},{20... | collective-permute-start | bytes 2359304 | tf_op jit(solution)/shard_map/ppermute | solution.py:552
  446.3 72.0 %collective-permute-start.51 = (bf16[2,128,2560]{2,1,0:T(8,128)(2,1)}, bf16[2,128,2560]{2,1,0:T(8,128)(2,1)S(1)}, u32[]{:S(2)}, u32[]{:S(2)}) collective-permute-start(bf16[2,128,2560]{2,1,0:T(8,128)(2,1)} %get-tuple-element.77), channel_id=1, source_target_pairs={{0,16},{16,0},{1,17},{17,1},{2,18},{18,2},{3,19},{19,3},{4,20},{20... | collective-permute-start | bytes 3932168 | tf_op jit(solution)/shard_map/ppermute | solution.py:552
  446.6 73.1 %collective-permute-start.53 = (bf16[2,128,2560]{2,1,0:T(8,128)(2,1)}, bf16[2,128,2560]{2,1,0:T(8,128)(2,1)S(1)}, u32[]{:S(2)}, u32[]{:S(2)}) collective-permute-start(bf16[2,128,2560]{2,1,0:T(8,128)(2,1)} %get-tuple-element.81), channel_id=1, source_target_pairs={{0,8},{8,0},{1,9},{9,1},{2,10},{10,2},{3,11},{11,3},{4,12},{12,4},... | collective-permute-start | bytes 3932168 | tf_op jit(solution)/shard_map/ppermute | solution.py:552
  450.3 49.3 %collective-permute-start.44 = (bf16[128,1536]{1,0:T(8,128)(2,1)S(1)}, bf16[128,1536]{1,0:T(8,128)(2,1)S(1)}, u32[]{:S(2)}, u32[]{:S(2)}) collective-permute-start(bf16[128,1536]{1,0:T(8,128)(2,1)S(1)} %slice_bitcast_fusion.10), channel_id=1, source_target_pairs={{0,8},{8,0},{1,9},{9,1},{2,10},{10,2},{3,11},{11,3},{4,12},{12,4},... | collective-permute-start | bytes 1179656 | tf_op jit(solution)/shard_map/ppermute | solution.py:552
  460.7 37.0 %collective-permute-start.46 = (bf16[128,1536]{1,0:T(8,128)(2,1)S(1)}, bf16[128,1536]{1,0:T(8,128)(2,1)S(1)}, u32[]{:S(2)}, u32[]{:S(2)}) collective-permute-start(bf16[128,1536]{1,0:T(8,128)(2,1)S(1)} %slice_bitcast_fusion.8), channel_id=1, source_target_pairs={{0,16},{16,0},{1,17},{17,1},{2,18},{18,2},{3,19},{19,3},{4,20},{20... | collective-permute-start | bytes 1179656 | tf_op jit(solution)/shard_map/ppermute | solution.py:552
  466.5 30.4 %collective-permute-start.39 = (f32[13312]{0:T(1024)S(1)}, f32[13312]{0:T(1024)S(1)}, u32[]{:S(2)}, u32[]{:S(2)}) collective-permute-start(f32[13312]{0:T(1024)S(1)} %add.251), channel_id=1, source_target_pairs={{0,8},{8,0},{1,9},{9,1},{2,10},{10,2},{3,11},{11,3},{4,12},{12,4},... | collective-permute-start | bytes 159752 | tf_op jit(solution)/shard_map/ppermute | solution.py:552
  496.8 48.2 %collective-permute-start.36 = (bf16[256,1024]{1,0:T(8,128)(2,1)}, bf16[256,1024]{1,0:T(8,128)(2,1)}, u32[]{:S(2)}, u32[]{:S(2)}) collective-permute-start(bf16[256,1024]{1,0:T(8,128)(2,1)} %get-tuple-element.175), channel_id=1, source_target_pairs={{1,0},{0,1},{5,2},{4,3},{3,4},{2,5},{7,6},{6,7},{9,8},{8,9},{13,10... | collective-permute-start | bytes 1572872 | tf_op jit(solution)/shard_map/ppermute | solution.py:590
  497.7 47.3 %collective-permute-start.37 = (bf16[256,1024]{1,0:T(8,128)(2,1)}, bf16[256,1024]{1,0:T(8,128)(2,1)}, u32[]{:S(2)}, u32[]{:S(2)}) collective-permute-start(bf16[256,1024]{1,0:T(8,128)(2,1)} %get-tuple-element.176), channel_id=1, source_target_pairs={{0,0},{1,1},{4,2},{5,3},{2,4},{3,5},{6,6},{7,7},{8,8},{9,9},{12,10... | collective-permute-start | bytes 1572872 | tf_op jit(solution)/shard_map/ppermute | solution.py:590
  516.4 39.8 %collective-permute-start.47 = (bf16[256,384]{1,0:T(8,128)(2,1)}, bf16[256,384]{1,0:T(8,128)(2,1)}, u32[]{:S(2)}, u32[]{:S(2)}) collective-permute-start(bf16[256,384]{1,0:T(8,128)(2,1)} %get-tuple-element.189), channel_id=1, source_target_pairs={{0,1},{1,0},{2,3},{3,2},{4,5},{5,4},{6,7},{7,6},{8,9},{9,8},{10,11... | collective-permute-start | bytes 589832 | tf_op jit(solution)/shard_map/ppermute | solution.py:552
  (112 other events, 1640.4 us)
where the time goes:
time: 585 us; the launch traced here: 576 us
  waiting for transfers between devices  217 us (37%)
  starting transfers between devices  101 us (17%)
  matrix products  85 us (15%)
  Pallas kernels  75.8 us (13%)
  other arithmetic  58.1 us (10%)
  local copies, waits for them, and re-layouts  36.9 us (6%)
    ppermute x59, waiting for transfers between devices, swap(): lax.ppermute(values, axis, [(i, i ^ bit) for i in range(4 if axis == 'ten...  201 us
    ppermute x59, starting transfers between devices, swap(): lax.ppermute(values, axis, [(i, i ^ bit) for i in range(4 if axis == 'ten...  75.1 us
    dot_general x8, matrix products, contract(): lax.dot_general(left, right, (((left_dim,), (right_dim,)), ((), ())), pre...  44.1 us
    pallas_call x1, Pallas kernels, attend_back(): pl.pallas_call(attend_back_kernel, grid=(pairs,), in_specs=[pl.BlockSpec(...  25.9 us
    dot_general x1, matrix products, clip_body(): jnp.dot(second_all, weight_up, preferred_element_type=jnp.float32) + bias_up  25.3 us
    pallas_call x1, Pallas kernels, attend(): pl.pallas_call(attend_kernel, grid=(pairs,), in_specs=[pl.BlockSpec((leng...  20.4 us
    ppermute x4, starting transfers between devices, to_clips(): arrived.append(lax.ppermute(sent, EVERY, pairs))  17.7 us
    unnamed x154, local copies, waits for them, and re-layouts  16 us
  transfers between devices with their start and end apart: 67, of which 27 were waited for; matrix products, arithmetic and copies ran while one was open for 19% of the time, Pallas kernels for 13%

commit v1 on v0

--- a/solution.py
+++ b/solution.py
@@ -408,6 +408,7 @@
             jax.ShapeDtypeStruct((pairs, 128, length), jnp.float32),
             jax.ShapeDtypeStruct((pairs, 2, length), jnp.float32),
         ],
+        cost_estimate=pl.CostEstimate(flops=2 * 10**10, transcendentals=0, bytes_accessed=16 * 2**20),
         name="attend",
     )(first, weight, bias.reshape(1, -1), cosine, sine)
 
@@ -472,6 +473,7 @@
             jax.ShapeDtypeStruct((length, 384 * pairs), jnp.bfloat16),
             jax.ShapeDtypeStruct((1, 384 * pairs), jnp.float32),
         ],
+        cost_estimate=pl.CostEstimate(flops=27 * 10**9, transcendentals=0, bytes_accessed=16 * 2**20),
         name="attend_back",
     )(qkv, grad, turned, logs, cosine, sine)
 
@@ -501,6 +503,7 @@
             out_specs=[pl.BlockSpec((8 * rows, cols), lambda i, place: (0, i)) for cols in widths],
         ),
         out_shape=[jax.ShapeDtypeStruct((8 * rows, 4 * cols), jnp.bfloat16) for cols in widths],
+        cost_estimate=pl.CostEstimate(flops=0, transcendentals=0, bytes_accessed=16 * 2**20),
         name="assemble",
     )(place, *pieces)
 
@@ -533,6 +536,7 @@
             out_specs=[pl.BlockSpec((2, rows, total), lambda i, place: (0, 0, i))] * 4,
         ),
         out_shape=[jax.ShapeDtypeStruct((2, rows, 4 * total), jnp.bfloat16)] * 4,
+        cost_estimate=pl.CostEstimate(flops=0, transcendentals=0, bytes_accessed=16 * 2**20),
         name="deal",
     )(place, *grads)
 
@@ -654,20 +658,23 @@
     theirs = swap(jnp.concatenate([other_half(item) for item in columns], axis=1), "core")
     held = jnp.concatenate([pick(core == 1, mine, theirs), pick(core == 1, theirs, mine)], axis=0)
 
-    def along_z(own):
+    def along_z(own, wait=None):
         one = swap(own, "tensor", 1)
         two = swap(own, "tensor", 2)
+        two = two if wait is None else after(two, wait)
         return [own, one, two, swap(two, "tensor", 1)]
 
-    def over_plane(blocks):
+    def over_plane(blocks, wait=None):
         own = jnp.concatenate(blocks, axis=1)
         from_x, from_y = swap(own, "x"), swap(own, "y")
+        if wait is not None:
+            from_x, from_y = after((from_x, from_y), wait)
         return own, from_x, from_y, swap(from_y[:own_rows], "x"), swap(from_x[own_rows:], "y")
 
     lines = jnp.concatenate([own_half(by_kind(qkv_bias)), own_half(fc1_bias)])
     lines = jnp.pad(three_parts(lines), ((0, 0), (0, 3 * qkv_cols - lines.shape[0]))).reshape(9, qkv_cols)
     blocks = along_z(jnp.concatenate([held[:, :qkv_cols], lines, jnp.zeros((7, qkv_cols), low)], axis=0))
-    tokens = to_clips(activations).astype(jnp.float32)
+    tokens = to_clips(after(activations, blocks[2])).astype(jnp.float32)
     lines = jnp.stack([item[2 * own_rows : 2 * own_rows + 9] for item in blocks])
     lines = lines.astype(jnp.float32).reshape(4, 3, 3 * qkv_cols).sum(axis=1)
     bias_qkv = lines[:, :qkv_cols].reshape(-1)
@@ -675,16 +682,6 @@
     pieces = over_plane([item[: 2 * own_rows] for item in blocks])
     (weight_qkv,) = assemble(place, pieces, [qkv_cols])
 
-    blocks = along_z(after(held[:, qkv_cols : qkv_cols + out_cols + unit_cols], blocks[3]))
-    blocks[0] = after(blocks[0], pieces[2])
-    pieces = over_plane(blocks)
-    weight_out, weight_up = assemble(place, pieces, [out_cols, unit_cols])
-
-    blocks = along_z(after(held[:, qkv_cols + out_cols + unit_cols :], blocks[3]))
-    blocks[0] = after(blocks[0], pieces[2])
-    grad_own = to_clips(after(cotangent, blocks[3]))
-    (weight_down,) = assemble(place, over_plane(blocks), [unit_cols])
-
     def both_halves(values):
         other = swap(values, "core")
         return jnp.concatenate([pick(core == 1, values, other), pick(core == 1, other, values)], axis=0)
@@ -698,10 +695,25 @@
 
     first_all = both_halves(norm_rows(tokens, attn_gain, attn_shift).astype(low))
     qkv, heads_out, turned, log_total = attend(first_all, weight_qkv, bias_qkv, cosine, sine)
+
+    own = after(held[:, qkv_cols : qkv_cols + out_cols + unit_cols], (blocks[3], tokens))
+    blocks = along_z(own, pieces[1:3])
+    blocks[0] = after(blocks[0], pieces[3:])
+    pieces = over_plane(blocks, heads_out)
+    weight_out, weight_up = assemble(place, pieces, [out_cols, unit_cols])
     resid = tokens + part_sum(contract(heads_out, weight_out, 1, 1)) + out_bias
     second_all = both_halves(norm_rows(resid, mlp_gain, mlp_shift).astype(low))
-    hidden = jnp.dot(second_all, weight_up, preferred_element_type=jnp.float32) + bias_up
+
+    own = after(held[:, qkv_cols + out_cols + unit_cols :], blocks[3])
+    blocks = along_z(own, heads_out)
+    blocks[0] = after(blocks[0], pieces[3:])
+    pieces = over_plane(blocks, second_all)
+    grad_own = to_clips(after(cotangent, blocks[3]))
+
+    hidden = jnp.dot(after(second_all, pieces[1:3]), weight_up, preferred_element_type=jnp.float32) + bias_up
     act = exact_gelu(hidden).astype(low)
+    pieces = pieces[:3] + after(pieces[3:], act)
+    (weight_down,) = assemble(place, pieces, [unit_cols])
     result = resid + part_sum(contract(act, weight_down, 1, 1)) + fc2_bias
     output = from_clips(result.astype(low))
 
@@ -712,56 +724,63 @@
             [pick(core == 1, kept, came), pick(core == 1, came, kept)], axis=-1
         ).astype(jnp.float32)
 
-    def over_plane_back(grads, waits):
-        kept_even, sent_even, kept_odd, sent_odd = deal(place, [item.astype(low) for item in grads])
-        even = kept_even + after(swap(sent_even, "y"), waits[0])
-        odd = kept_odd + after(swap(sent_odd, "x"), waits[0])
-        even = even[0] + after(swap(even[1], "x"), waits[1])
-        odd = odd[0] + after(swap(odd[1], "y"), waits[1])
-        return jnp.concatenate([even, odd])
-
-    def along_z_back(total, wait):
+    def dealt(*grads):
+        return deal(place, [item.astype(low) for item in grads])
+
+    def first_back(parts, wait):
+        kept_even, sent_even, kept_odd, sent_odd = parts
+        came = after((swap(sent_even, "y"), swap(sent_odd, "x")), wait)
+        return kept_even + came[0], kept_odd + came[1]
+
+    def second_back(even, odd, wait):
+        came = after((swap(even[1], "x"), swap(odd[1], "y")), wait)
+        return jnp.concatenate([even[0] + came[0], odd[0] + came[1]])
+
+    def along_z_back(total, wait, later):
         cols = total.shape[1] // 4
         own, one, two, three = (total[:, at * cols : (at + 1) * cols] for at in range(4))
         one = swap(one, "tensor", 1)
         two = swap(two + after(swap(three, "tensor", 1), wait), "tensor", 2)
+        one, two = after((one, two), later)
         return to_core((own + one + two).reshape(2, own_rows, cols))
 
     grad_top = grad_own.astype(jnp.float32)
     grad_all = both_halves(grad_own)
     sum_fc2_bias = jnp.sum(grad_top, axis=0)
-    grad_fc2 = contract(grad_all, act, 0, 0)
-    grad_act = jnp.dot(grad_all, weight_down, preferred_element_type=jnp.float32)
+    parts_fc2 = dealt(contract(grad_all, act, 0, 0))
+    grad_act = jnp.dot(after(grad_all, parts_fc2), weight_down, preferred_element_type=jnp.float32)
     grad_hidden = jax.vjp(exact_gelu, hidden)[1](grad_act)[0].astype(low)
     sum_fc1_bias = jnp.sum(grad_hidden, axis=0, dtype=jnp.float32)
-    grad_fc1 = contract(second_all, grad_hidden, 0, 0)
     grad_second_part = contract(grad_hidden, weight_up, 1, 1)
+    sent_fc2 = first_back(parts_fc2, grad_second_part)
     grad_second = part_sum(grad_second_part)
     second_pull = jax.vjp(norm_rows, resid, mlp_gain, mlp_shift)[1]
     grad_resid_norm, sum_mlp_gain, sum_mlp_shift = second_pull(grad_second)
     grad_resid = grad_top + grad_resid_norm
     sum_out_bias = jnp.sum(grad_resid, axis=0)
     resid_all = both_halves(grad_resid.astype(low))
-    grad_out = contract(resid_all, heads_out, 0, 0)
+    grad_fc1 = contract(after(second_all, sent_fc2[0]), grad_hidden, 0, 0)
+    parts_up = dealt(contract(resid_all, heads_out, 0, 0), grad_fc1)
     grad_heads = jnp.dot(resid_all, weight_out, preferred_element_type=jnp.float32).astype(low)
-    grad_packed, sum_qkv_bias = attend_back(qkv, grad_heads, turned, log_total, cosine, sine)
-    grad_qkv = contract(first_all, grad_packed, 0, 0)
-    grad_first_part = contract(grad_packed, weight_qkv, 1, 1)
-    grad_first = part_sum(grad_first_part)
+    total_fc2 = second_back(*sent_fc2, grad_heads)
+    grad_packed, sum_qkv_bias = attend_back(qkv, after(grad_heads, (parts_up, total_fc2)), turned, log_total, cosine, sine)
+    sent_up = first_back(parts_up, grad_packed)
+    parts_qkv = dealt(contract(after(first_all, sent_up), grad_packed, 0, 0))
+    total_up = second_back(*sent_up, parts_qkv)
+    grad_first_part = contract(after(grad_packed, parts_qkv), weight_qkv, 1, 1)
+    grad_first = part_sum(after(grad_first_part, total_up))
     first_pull = jax.vjp(norm_rows, tokens, attn_gain, attn_shift)[1]
     grad_input_norm, sum_attn_gain, sum_attn_shift = first_pull(grad_first)
     input_grad = from_clips((grad_resid + grad_input_norm).astype(low)).astype(jnp.float32)
 
-    total = over_plane_back([grad_fc2], [grad_second_part, grad_packed])
-    grad_fc2_weight = along_z_back(total, grad_first_part)
-    total = over_plane_back([grad_out, grad_fc1], [grad_packed, grad_first_part])
-    both_weights = along_z_back(total, grad_first)
+    grad_fc2_weight = along_z_back(total_fc2, grad_packed, parts_qkv)
+    both_weights = along_z_back(total_up, grad_first_part, grad_first)
     cuts = both_weights.shape[1] // 2
     both_weights = [both_weights[:, :cuts], both_weights[:, cuts:]]
     grad_out_weight = jnp.concatenate([item[:, :out_cols] for item in both_weights], axis=1)
     grad_fc1_weight = jnp.concatenate([item[:, out_cols:] for item in both_weights], axis=1)
-    total = over_plane_back([grad_qkv], [grad_first_part, grad_first])
-    grad_qkv_weight = by_head(along_z_back(total, grad_first))
+    total = second_back(*first_back(parts_qkv, grad_first_part), grad_first)
+    grad_qkv_weight = by_head(along_z_back(total, grad_first, grad_first))
 
     def by_core(values):
         none = jnp.zeros_like(values)

time: 585 us -> 473 us (0.81)
  waiting for transfers between devices: 217 us -> 136 us
  starting transfers between devices: 101 us -> 89.5 us
  other arithmetic: 58.1 us -> 48.6 us
    ppermute x59, waiting for transfers between devices: 201 us -> 119 us  [swap(): lax.ppermute(values, axis, [(i, i ^ bit) for i in range(4 if axis == 'ten...]
    ppermute x59, starting transfers between devices: 75.1 us -> 64.6 us  [swap(): lax.ppermute(values, axis, [(i, i ^ bit) for i in range(4 if axis == 'ten...]
    unnamed x154 -> x152, local copies, waits for them, and re-layouts: 16 us -> 17.9 us
  transfers between devices with their start and end apart: 67 -> 67, of which waited for: 27 -> 21; matrix products, arithmetic and copies ran while one was open for 19% -> 32% of each run, Pallas kernels for 13% -> 16%
where the time goes in v1:
time: 473 us; the launch traced here: 468 us
  waiting for transfers between devices  136 us (29%)
  starting transfers between devices  89.5 us (19%)
  matrix products  81.3 us (17%)
  Pallas kernels  75.3 us (16%)
  other arithmetic  48.6 us (10%)
  local copies, waits for them, and re-layouts  35.1 us (7%)
    ppermute x59, waiting for transfers between devices, swap(): lax.ppermute(values, axis, [(i, i ^ bit) for i in range(4 if axis == 'ten...  119 us
    ppermute x59, starting transfers between devices, swap(): lax.ppermute(values, axis, [(i, i ^ bit) for i in range(4 if axis == 'ten...  64.6 us
    dot_general x8, matrix products, contract(): lax.dot_general(left, right, (((left_dim,), (right_dim,)), ((), ())), pre...  43.1 us
    pallas_call x1, Pallas kernels, attend_back(): pl.pallas_call(attend_back_kernel, grid=(pairs,), in_specs=[pl.BlockSpec(...  25.7 us
    dot_general x1, matrix products, clip_body(): jnp.dot(after(second_all, pieces[1:3]), weight_up, preferred_element_type...  23.4 us
    pallas_call x1, Pallas kernels, attend(): pl.pallas_call(attend_kernel, grid=(pairs,), in_specs=[pl.BlockSpec((leng...  20.4 us
    unnamed x152, local copies, waits for them, and re-layouts  17.9 us
    pallas_call x3, Pallas kernels, deal(): pl.pallas_call(deal_kernel, grid_spec=pltpu.PrefetchScalarGridSpec(num_sc...  14.6 us
  transfers between devices with their start and end apart: 67, of which 21 were waited for; matrix products, arithmetic and copies ran while one was open for 32% of the time, Pallas kernels for 16%

profile of v1, /device:TPU:1, one launch (start us, length us, event | category | flops | bytes accessed | tf_op | source)
XLA Modules:
  0.0 468.0 jit_solution(13661310211211156452)
XLA Ops:
  12.2 6.5 %collective-permute-done.1 = bf16[272,384]{1,0:T(8,128)(2,1)S(1)} collective-permute-done((bf16[272,384]{1,0:T(8,128)(2,1)S(1)}, bf16[272,384]{1,0:T(8,128)(2,1)S(1)}, u32[]{:S(2)}, u32[]{:S(2)}) %collective-permute-start.1) | collective-permute-done | bytes 208928 | tf_op jit(solution)/shard_map/ppermute | solution.py:556
  27.1 15.3 %collective-permute-done.6 = bf16[272,384]{1,0:T(8,128)(2,1)S(1)} collective-permute-done((bf16[272,384]{1,0:T(8,128)(2,1)S(1)}, bf16[272,384]{1,0:T(8,128)(2,1)S(1)}, u32[]{:S(2)}, u32[]{:S(2)}) %collective-permute-start.6) | collective-permute-done | bytes 208928 | tf_op jit(solution)/shard_map/ppermute | solution.py:556
  51.6 10.4 %collective-permute-done.8.y_ref = bf16[256,1536]{1,0:T(8,128)(2,1)S(1)} collective-permute-done((bf16[256,1536]{1,0:T(8,128)(2,1)S(1)}, bf16[256,1536]{1,0:T(8,128)(2,1)S(1)}, u32[]{:S(2)}, u32[]{:S(2)}) %collective-permute-start.8) | collective-permute-done | bytes 786464 | tf_op jit(solution)/shard_map/ppermute | solution.py:556
  78.2 8.4 %collective-permute-done.11 = bf16[256,640]{1,0:T(8,128)(2,1)S(1)} collective-permute-done((bf16[256,640]{1,0:T(8,128)(2,1)S(1)}, bf16[256,640]{1,0:T(8,128)(2,1)S(1)}, u32[]{:S(2)}, u32[]{:S(2)}) %collective-permute-start.11) | collective-permute-done | bytes 327712 | tf_op jit(solution)/shard_map/ppermute | solution.py:556
  99.8 20.4 %attend.1 = (bf16[1024,1536]{1,0:T(8,128)(2,1)}, bf16[1024,512]{1,0:T(8,128)(2,1)}, f32[4,128,1024]{2,1,0:T(8,128)}, f32[4,2,1024]{2,1,0:T(2,128)}) custom-call(bf16[1024,1024]{1,0:T(8,128)(2,1)} %pad_maximum_fusion.first_ref, bf16[1024,1536]{1,0:T(8,128)(2,1)} %assemble.3.weight_ref, f32[1,1536]{1,0:T(1,128)} %bitcast.110, ...), custom_call_target="tpu_custom_call" | custom-call | flops 20000000000 | bytes 16777216 | tf_op jit(solution)/shard_map/attend/pallas_call | solution.py:389
  124.0 5.5 %collective-permute-done.22 = bf16[256,512]{1,0:T(8,128)(2,1)S(1)} collective-permute-done((bf16[256,512]{1,0:T(8,128)(2,1)S(1)}, bf16[256,512]{1,0:T(8,128)(2,1)S(1)}, u32[]{:S(2)}, u32[]{:S(2)}) %collective-permute-start.22) | collective-permute-done | bytes 262176 | tf_op jit(solution)/shard_map/ppermute | solution.py:556
  130.6 6.3 %collective-permute-start.30 = (bf16[256,1024]{1,0:T(8,128)(2,1)}, bf16[256,1024]{1,0:T(8,128)(2,1)S(1)}, u32[]{:S(2)}, u32[]{:S(2)}) collective-permute-start(bf16[256,1024]{1,0:T(8,128)(2,1)} %get-tuple-element.225), channel_id=1, source_target_pairs={{0,1},{1,0},{2,5},{3,4},{4,3},{5,2},{6,7},{7,6},{8,9},{9,8},{10,13... | collective-permute-start | bytes 1572872 | tf_op jit(solution)/shard_map/ppermute | solution.py:582
  140.7 5.3 %assemble.4 = (bf16[1024,512]{1,0:T(8,128)(2,1)}, bf16[1024,2048]{1,0:T(8,128)(2,1)}) custom-call(s32[1]{0:T(128)} %bitcast.7.place_ref, bf16[256,2560]{1,0:T(8,128)(2,1)} %constant_dynamic-update-slice_fusion.own_ref, bf16[256,2560]{1,0:T(8,128)(2,1)} %collective-permute-done.14.x_ref, bf16[256,2560]{1,0:T(8,128)(2,1)} %collective-permute-done.15.y_ref, ...), custom_call_target="tpu_custom_call" | custom-call | bytes 16777216 | tf_op jit(solution)/shard_map/assemble/pallas_call | solution.py:497
  170.1 19.8 %collective-permute-done.24.y_ref = bf16[256,2048]{1,0:T(8,128)(2,1)S(1)} collective-permute-done((bf16[256,2048]{1,0:T(8,128)(2,1)S(1)}, bf16[256,2048]{1,0:T(8,128)(2,1)S(1)}, u32[]{:S(2)}, u32[]{:S(2)}) %collective-permute-start.24) | collective-permute-done | bytes 1048608 | tf_op jit(solution)/shard_map/ppermute | solution.py:556
  194.0 23.4 %multiply_convert_fusion = (bf16[1024,2048]{1,0:T(8,128)(2,1)S(1)}, f32[1024,2048]{1,0:T(8,128)}, f32[1024,2048]{1,0:T(8,128)}) fusion(f32[2048]{0:T(1024)S(1)} %bitcast.108, bf16[1024,1024]{1,0:T(8,128)(2,1)S(1)} %pad_maximum_fusion.1, bf16[1024,2048]{1,0:T(8,128)(2,1)S(1)} %copy-done.61), kind=kOutput, calls=%fused_computation.4 | convolution fusion | flops 4433379328 | bytes 27271168 | tf_op jit(solution)/shard_map/dot_general | solution.py:713
  219.4 6.3 %convolution_convert_fusion.2.refs_0_ = bf16[1024,2048]{1,0:T(8,128)(2,1)} fusion(bf16[1024,2048]{1,0:T(8,128)(2,1)S(1)} %get-tuple-element.199, bf16[512,1024]{1,0:T(8,128)(2,1)S(1)} %get-tuple-element.210, bf16[512,1024]{1,0:T(8,128)(2,1)S(1)} %get-tuple-element.209), kind=kOutput, calls=%fused_computation.20 | convolution fusion | flops 4301258752 | bytes 10485760 | tf_op jit(solution)/shard_map/dot_general | solution.py:46
  225.7 4.8 %deal.3 = (bf16[2,128,2048]{2,1,0:T(8,128)(2,1)}, bf16[2,128,2048]{2,1,0:T(8,128)(2,1)}, bf16[2,128,2048]{2,1,0:T(8,128)(2,1)}, bf16[2,128,2048]{2,1,0:T(8,128)(2,1)}) custom-call(s32[1]{0:T(128)} %bitcast.7.place_ref, bf16[1024,2048]{1,0:T(8,128)(2,1)} %convolution_convert_fusion.2.refs_0_), custom_call_target="tpu_custom_call" | custom-call | bytes 16777216 | tf_op jit(solution)/shard_map/deal/pallas_call | solution.py:530
  236.1 8.2 %fusion.73 = f32[1024,1024]{1,0:T(8,128)S(1)} fusion(bf16[1024,2048]{1,0:T(8,128)(2,1)} %copy-done.65, bf16[1024,2048]{1,0:T(8,128)(2,1)} %assemble.5), kind=kOutput, calls=%fused_computation.291 | convolution fusion | flops 4294967296 | bytes 12582912 | tf_op jit(solution)/shard_map/dot_general | solution.py:46
  244.3 10.9 %convert_reduce_fusion = (f32[2048]{0:T(1024)S(1)}, bf16[1024,2048]{1,0:T(8,128)(2,1)S(1)}) fusion(f32[1024,2048]{1,0:T(8,128)} %get-tuple-element.200, f32[1024,2048]{1,0:T(8,128)} %get-tuple-element.279, f32[2048]{0:T(1024)S(1)} %bitcast.109, bf16[1024,1024]{1,0:T(8,128)(2,1)S(1)} %copy-done.23, bf16[1024,2048]{1,0:T(8,128)(2,1)S(1)} %copy-done.16), kind=kOutput, calls=%fused_computation.2 | convolution fusion | flops 4330616832 | bytes 27279360 | tf_op jit(solution)/shard_map/dot_general | solution.py:751
  280.4 6.3 %convolution_convert_fusion.1.refs_1_ = bf16[1024,2048]{1,0:T(8,128)(2,1)} fusion(bf16[1024,1024]{1,0:T(8,128)(2,1)S(1)} %copy-done.22, bf16[1024,2048]{1,0:T(8,128)(2,1)S(1)} %get-tuple-element.194), kind=kOutput, calls=%fused_computation.19 | convolution fusion | flops 4297064448 | bytes 10485760 | tf_op jit(solution)/shard_map/dot_general | solution.py:46
  287.9 10.4 %collective-permute-done.29 = bf16[256,1024]{1,0:T(8,128)(2,1)S(1)} collective-permute-done((bf16[256,1024]{1,0:T(8,128)(2,1)S(1)}, bf16[256,1024]{1,0:T(8,128)(2,1)S(1)}, u32[]{:S(2)}, u32[]{:S(2)}) %collective-permute-start.29) | collective-permute-done | bytes 524320 | tf_op jit(solution)/shard_map/ppermute | solution.py:594
  305.1 5.5 %deal.4 = (bf16[2,128,2560]{2,1,0:T(8,128)(2,1)}, bf16[2,128,2560]{2,1,0:T(8,128)(2,1)}, bf16[2,128,2560]{2,1,0:T(8,128)(2,1)}, bf16[2,128,2560]{2,1,0:T(8,128)(2,1)}) custom-call(s32[1]{0:T(128)} %bitcast.7.place_ref, bf16[1024,512]{1,0:T(8,128)(2,1)} %convolution_convert_fusion.3.refs_0_, bf16[1024,2048]{1,0:T(8,128)(2,1)} %convolution_convert_fusion.1.refs_1_), custom_call_target="tpu_custom_call" | custom-call | bytes 16777216 | tf_op jit(solution)/shard_map/deal/pallas_call | solution.py:530
  317.5 25.7 %attend_back.1 = (bf16[1024,1536]{1,0:T(8,128)(2,1)}, f32[1,1536]{1,0:T(1,128)}) custom-call(bf16[1024,1536]{1,0:T(8,128)(2,1)} %get-tuple-element.99.qkv_ref, bf16[1024,512]{1,0:T(8,128)(2,1)} %convolution_convert_fusion.4.grad_ref, f32[4,128,1024]{2,1,0:T(8,128)} %get-tuple-element.110.turned_ref, f32[4,2,1024]{2,1,0:T(2,128)} %get-tuple-element.111.log_ref, ...), custom_call_target="tpu_custom_call" | custom-call | flops 27000000512 | bytes 16777216 | tf_op jit(solution)/shard_map/attend_back/pallas_call | solution.py:457
  354.1 5.2 %convolution_convert_fusion.refs_0_ = bf16[1024,1536]{1,0:T(8,128)(2,1)} fusion(bf16[1024,1024]{1,0:T(8,128)(2,1)S(1)} %copy-done.20, bf16[1024,1536]{1,0:T(8,128)(2,1)S(1)} %copy-done.64), kind=kOutput, calls=%fused_computation.18 | convolution fusion | flops 3222798336 | bytes 8388608 | tf_op jit(solution)/shard_map/dot_general | solution.py:46
  365.4 6.3 %fusion.75 = f32[1024,1024]{1,0:T(8,128)S(1)} fusion(bf16[1024,1536]{1,0:T(8,128)(2,1)} %get-tuple-element.120, bf16[1024,1536]{1,0:T(8,128)(2,1)} %assemble.3.weight_ref), kind=kOutput, calls=%fused_computation.293 | convolution fusion | flops 3221225472 | bytes 10485760 | tf_op jit(solution)/shard_map/dot_general | solution.py:46
  378.9 15.0 %collective-permute-done.42 = bf16[128,2560]{1,0:T(8,128)(2,1)S(1)} collective-permute-done((bf16[128,2560]{1,0:T(8,128)(2,1)}, bf16[128,2560]{1,0:T(8,128)(2,1)S(1)}, u32[]{:S(2)}, u32[]{:S(2)}) %collective-permute-start.42) | collective-permute-done | bytes 655392 | tf_op jit(solution)/shard_map/ppermute | solution.py:556
  401.4 7.0 %collective-permute-start.61 = (bf16[256,640]{1,0:T(8,128)(2,1)S(1)}, bf16[256,640]{1,0:T(8,128)(2,1)S(1)}, u32[]{:S(2)}, u32[]{:S(2)}) collective-permute-start(bf16[256,640]{1,0:T(8,128)(2,1)S(1)} %get-tuple-element.215), channel_id=1, source_target_pairs={{0,2},{1,3},{2,0},{3,1},{4,6},{5,7},{6,4},{7,5},{8,10},{9,11},{10,... | collective-permute-start | bytes 983048 | tf_op jit(solution)/shard_map/ppermute | solution.py:556
  427.5 13.8 %collective-permute-done.49 = f32[13312]{0:T(1024)S(1)} collective-permute-done((f32[13312]{0:T(1024)S(1)}, f32[13312]{0:T(1024)S(1)}, u32[]{:S(2)}, u32[]{:S(2)}) %collective-permute-start.49) | collective-permute-done | bytes 53280 | tf_op jit(solution)/shard_map/ppermute | solution.py:556
  456.1 6.7 %collective-permute-done.57 = bf16[256,384]{1,0:T(8,128)(2,1)S(1)} collective-permute-done((bf16[256,384]{1,0:T(8,128)(2,1)S(1)}, bf16[256,384]{1,0:T(8,128)(2,1)S(1)}, u32[]{:S(2)}, u32[]{:S(2)}) %collective-permute-start.57) | collective-permute-done | bytes 196640 | tf_op jit(solution)/shard_map/ppermute | solution.py:556
  (451 shorter events, 211.9 us)
Async XLA Ops:
  18.8 28.4 %collective-permute-start.2 = (bf16[256,1024]{1,0:T(8,128)(2,1)S(1)}, bf16[256,1024]{1,0:T(8,128)(2,1)S(1)}, u32[]{:S(2)}, u32[]{:S(2)}) collective-permute-start(bf16[256,1024]{1,0:T(8,128)(2,1)S(1)} %get-tuple-element.233), channel_id=1, source_target_pairs={{0,1},{1,0},{2,5},{3,4},{4,3},{5,2},{6,7},{7,6},{8,9},{9,8},{10,13... | collective-permute-start | bytes 1572872 | tf_op jit(solution)/shard_map/ppermute | solution.py:582
  48.5 48.3 %collective-permute-start.4 = (bf16[512,1024]{1,0:T(8,128)(2,1)S(1)}, bf16[512,1024]{1,0:T(8,128)(2,1)}, u32[]{:S(2)}, u32[]{:S(2)}) collective-permute-start(bf16[512,1024]{1,0:T(8,128)(2,1)S(1)} %add_convert_fusion.4), channel_id=1, source_target_pairs={{0,4},{4,0},{1,5},{5,1},{2,6},{6,2},{3,7},{7,3},{8,12},{12,8},{9,1... | collective-permute-start | bytes 3145736 | tf_op jit(solution)/shard_map/ppermute | solution.py:556
  75.4 48.6 %collective-permute-start.21 = (bf16[256,512]{1,0:T(8,128)(2,1)}, bf16[256,512]{1,0:T(8,128)(2,1)S(1)}, u32[]{:S(2)}, u32[]{:S(2)}) collective-permute-start(bf16[256,512]{1,0:T(8,128)(2,1)} %pad_maximum_fusion.18), channel_id=1, source_target_pairs={{0,2},{1,3},{2,0},{3,1},{4,6},{5,7},{6,4},{7,5},{8,10},{9,11},{10,... | collective-permute-start | bytes 786440 | tf_op jit(solution)/shard_map/ppermute | solution.py:556
  91.0 29.1 %collective-permute-start.15 = (bf16[256,2560]{1,0:T(8,128)(2,1)}, bf16[256,2560]{1,0:T(8,128)(2,1)}, u32[]{:S(2)}, u32[]{:S(2)}) collective-permute-start(bf16[256,2560]{1,0:T(8,128)(2,1)} %constant_dynamic-update-slice_fusion.own_ref), channel_id=1, source_target_pairs={{0,16},{16,0},{1,17},{17,1},{2,18},{18,2},{3,19},{19,3},{4,20},{20... | collective-permute-start | bytes 3932168 | tf_op jit(solution)/shard_map/ppermute | solution.py:556
  91.4 28.7 %collective-permute-start.14 = (bf16[256,2560]{1,0:T(8,128)(2,1)}, bf16[256,2560]{1,0:T(8,128)(2,1)}, u32[]{:S(2)}, u32[]{:S(2)}) collective-permute-start(bf16[256,2560]{1,0:T(8,128)(2,1)} %constant_dynamic-update-slice_fusion.own_ref), channel_id=1, source_target_pairs={{0,8},{8,0},{1,9},{9,1},{2,10},{10,2},{3,11},{11,3},{4,12},{12,4},... | collective-permute-start | bytes 3932168 | tf_op jit(solution)/shard_map/ppermute | solution.py:556
  191.7 39.5 %collective-permute-start.25 = (bf16[128,2048]{1,0:T(8,128)(2,1)}, bf16[128,2048]{1,0:T(8,128)(2,1)}, u32[]{:S(2)}, u32[]{:S(2)}) collective-permute-start(bf16[128,2048]{1,0:T(8,128)(2,1)} %slice.385), channel_id=1, source_target_pairs={{0,8},{8,0},{1,9},{9,1},{2,10},{10,2},{3,11},{11,3},{4,12},{12,4},... | collective-permute-start | bytes 1572872 | tf_op jit(solution)/shard_map/ppermute | solution.py:556
  193.1 38.1 %collective-permute-start.26 = (bf16[128,2048]{1,0:T(8,128)(2,1)}, bf16[128,2048]{1,0:T(8,128)(2,1)}, u32[]{:S(2)}, u32[]{:S(2)}) collective-permute-start(bf16[128,2048]{1,0:T(8,128)(2,1)} %slice.386), channel_id=1, source_target_pairs={{0,16},{16,0},{1,17},{17,1},{2,18},{18,2},{3,19},{19,3},{4,20},{20... | collective-permute-start | bytes 1572872 | tf_op jit(solution)/shard_map/ppermute | solution.py:556
  230.5 32.5 %collective-permute-start.35 = (bf16[2,128,2048]{2,1,0:T(8,128)(2,1)}, bf16[2,128,2048]{2,1,0:T(8,128)(2,1)}, u32[]{:S(2)}, u32[]{:S(2)}) collective-permute-start(bf16[2,128,2048]{2,1,0:T(8,128)(2,1)} %get-tuple-element.95), channel_id=1, source_target_pairs={{0,16},{16,0},{1,17},{17,1},{2,18},{18,2},{3,19},{19,3},{4,20},{20... | collective-permute-start | bytes 3145736 | tf_op jit(solution)/shard_map/ppermute | solution.py:556
  231.2 31.8 %collective-permute-start.36 = (bf16[2,128,2048]{2,1,0:T(8,128)(2,1)}, bf16[2,128,2048]{2,1,0:T(8,128)(2,1)}, u32[]{:S(2)}, u32[]{:S(2)}) collective-permute-start(bf16[2,128,2048]{2,1,0:T(8,128)(2,1)} %get-tuple-element.97), channel_id=1, source_target_pairs={{0,8},{8,0},{1,9},{9,1},{2,10},{10,2},{3,11},{11,3},{4,12},{12,4},... | collective-permute-start | bytes 3145736 | tf_op jit(solution)/shard_map/ppermute | solution.py:556
  267.3 48.0 %collective-permute-start.37 = (bf16[128,2048]{1,0:T(8,128)(2,1)}, bf16[128,2048]{1,0:T(8,128)(2,1)}, u32[]{:S(2)}, u32[]{:S(2)}) collective-permute-start(bf16[128,2048]{1,0:T(8,128)(2,1)} %slice_bitcast_fusion.6), channel_id=1, source_target_pairs={{0,8},{8,0},{1,9},{9,1},{2,10},{10,2},{3,11},{11,3},{4,12},{12,4},... | collective-permute-start | bytes 1572872 | tf_op jit(solution)/shard_map/ppermute | solution.py:556
  269.3 45.9 %collective-permute-start.38 = (bf16[128,2048]{1,0:T(8,128)(2,1)}, bf16[128,2048]{1,0:T(8,128)(2,1)}, u32[]{:S(2)}, u32[]{:S(2)}) collective-permute-start(bf16[128,2048]{1,0:T(8,128)(2,1)} %slice_bitcast_fusion.5), channel_id=1, source_target_pairs={{0,16},{16,0},{1,17},{17,1},{2,18},{18,2},{3,19},{19,3},{4,20},{20... | collective-permute-start | bytes 1572872 | tf_op jit(solution)/shard_map/ppermute | solution.py:556
  310.7 35.9 %collective-permute-start.39 = (bf16[2,128,2560]{2,1,0:T(8,128)(2,1)}, bf16[2,128,2560]{2,1,0:T(8,128)(2,1)}, u32[]{:S(2)}, u32[]{:S(2)}) collective-permute-start(bf16[2,128,2560]{2,1,0:T(8,128)(2,1)} %get-tuple-element.103), channel_id=1, source_target_pairs={{0,16},{16,0},{1,17},{17,1},{2,18},{18,2},{3,19},{19,3},{4,20},{20... | collective-permute-start | bytes 3932168 | tf_op jit(solution)/shard_map/ppermute | solution.py:556
  311.1 35.4 %collective-permute-start.40 = (bf16[2,128,2560]{2,1,0:T(8,128)(2,1)}, bf16[2,128,2560]{2,1,0:T(8,128)(2,1)}, u32[]{:S(2)}, u32[]{:S(2)}) collective-permute-start(bf16[2,128,2560]{2,1,0:T(8,128)(2,1)} %get-tuple-element.105), channel_id=1, source_target_pairs={{0,8},{8,0},{1,9},{9,1},{2,10},{10,2},{3,11},{11,3},{4,12},{12,4},... | collective-permute-start | bytes 3932168 | tf_op jit(solution)/shard_map/ppermute | solution.py:556
  317.5 26.7 %collective-permute-start.64 = (bf16[256,512]{1,0:T(8,128)(2,1)S(1)}, bf16[256,512]{1,0:T(8,128)(2,1)S(1)}, u32[]{:S(2)}, u32[]{:S(2)}) collective-permute-start(bf16[256,512]{1,0:T(8,128)(2,1)S(1)} %fusion.25), channel_id=1, source_target_pairs={{0,1},{1,0},{2,3},{3,2},{4,5},{5,4},{6,7},{7,6},{8,9},{9,8},{10,11... | collective-permute-start | bytes 786440 | tf_op jit(solution)/shard_map/ppermute | solution.py:556
  353.0 26.0 %collective-permute-start.41 = (bf16[128,2560]{1,0:T(8,128)(2,1)}, bf16[128,2560]{1,0:T(8,128)(2,1)}, u32[]{:S(2)}, u32[]{:S(2)}) collective-permute-start(bf16[128,2560]{1,0:T(8,128)(2,1)} %slice_bitcast_fusion.2), channel_id=1, source_target_pairs={{0,8},{8,0},{1,9},{9,1},{2,10},{10,2},{3,11},{11,3},{4,12},{12,4},... | collective-permute-start | bytes 1966088 | tf_op jit(solution)/shard_map/ppermute | solution.py:556
  363.6 31.8 %collective-permute-start.51 = (bf16[2,128,1536]{2,1,0:T(8,128)(2,1)}, bf16[2,128,1536]{2,1,0:T(8,128)(2,1)S(1)}, u32[]{:S(2)}, u32[]{:S(2)}) collective-permute-start(bf16[2,128,1536]{2,1,0:T(8,128)(2,1)} %get-tuple-element.117), channel_id=1, source_target_pairs={{0,16},{16,0},{1,17},{17,1},{2,18},{18,2},{3,19},{19,3},{4,20},{20... | collective-permute-start | bytes 2359304 | tf_op jit(solution)/shard_map/ppermute | solution.py:556
  364.6 30.8 %collective-permute-start.52 = (bf16[2,128,1536]{2,1,0:T(8,128)(2,1)}, bf16[2,128,1536]{2,1,0:T(8,128)(2,1)S(1)}, u32[]{:S(2)}, u32[]{:S(2)}) collective-permute-start(bf16[2,128,1536]{2,1,0:T(8,128)(2,1)} %get-tuple-element.119), channel_id=1, source_target_pairs={{0,8},{8,0},{1,9},{9,1},{2,10},{10,2},{3,11},{11,3},{4,12},{12,4},... | collective-permute-start | bytes 2359304 | tf_op jit(solution)/shard_map/ppermute | solution.py:556
  365.0 29.0 %collective-permute-start.42 = (bf16[128,2560]{1,0:T(8,128)(2,1)}, bf16[128,2560]{1,0:T(8,128)(2,1)S(1)}, u32[]{:S(2)}, u32[]{:S(2)}) collective-permute-start(bf16[128,2560]{1,0:T(8,128)(2,1)} %slice_bitcast_fusion.1), channel_id=1, source_target_pairs={{0,16},{16,0},{1,17},{17,1},{2,18},{18,2},{3,19},{19,3},{4,20},{20... | collective-permute-start | bytes 1966088 | tf_op jit(solution)/shard_map/ppermute | solution.py:556
  377.7 30.7 %collective-permute-start.43 = (bf16[512,1024]{1,0:T(8,128)(2,1)S(1)}, bf16[512,1024]{1,0:T(8,128)(2,1)S(1)}, u32[]{:S(2)}, u32[]{:S(2)}) collective-permute-start(bf16[512,1024]{1,0:T(8,128)(2,1)S(1)} %select_convert_fusion), channel_id=1, source_target_pairs={{0,4},{4,0},{1,5},{5,1},{2,6},{6,2},{3,7},{7,3},{8,12},{12,8},{9,1... | collective-permute-start | bytes 3145736 | tf_op jit(solution)/shard_map/ppermute | solution.py:556
  397.2 26.0 %collective-permute-start.54 = (bf16[128,1536]{1,0:T(8,128)(2,1)S(1)}, bf16[128,1536]{1,0:T(8,128)(2,1)S(1)}, u32[]{:S(2)}, u32[]{:S(2)}) collective-permute-start(bf16[128,1536]{1,0:T(8,128)(2,1)S(1)} %slice_bitcast_fusion.9), channel_id=1, source_target_pairs={{0,16},{16,0},{1,17},{17,1},{2,18},{18,2},{3,19},{19,3},{4,20},{20... | collective-permute-start | bytes 1179656 | tf_op jit(solution)/shard_map/ppermute | solution.py:556
  401.4 42.3 %collective-permute-start.61 = (bf16[256,640]{1,0:T(8,128)(2,1)S(1)}, bf16[256,640]{1,0:T(8,128)(2,1)S(1)}, u32[]{:S(2)}, u32[]{:S(2)}) collective-permute-start(bf16[256,640]{1,0:T(8,128)(2,1)S(1)} %get-tuple-element.215), channel_id=1, source_target_pairs={{0,2},{1,3},{2,0},{3,1},{4,6},{5,7},{6,4},{7,5},{8,10},{9,11},{10,... | collective-permute-start | bytes 983048 | tf_op jit(solution)/shard_map/ppermute | solution.py:556
  408.4 35.3 %collective-permute-start.59 = (bf16[256,640]{1,0:T(8,128)(2,1)S(1)}, bf16[256,640]{1,0:T(8,128)(2,1)S(1)}, u32[]{:S(2)}, u32[]{:S(2)}) collective-permute-start(bf16[256,640]{1,0:T(8,128)(2,1)S(1)} %get-tuple-element.216), channel_id=1, source_target_pairs={{0,1},{1,0},{2,3},{3,2},{4,5},{5,4},{6,7},{7,6},{8,9},{9,8},{10,11... | collective-permute-start | bytes 983048 | tf_op jit(solution)/shard_map/ppermute | solution.py:556
  418.3 37.7 %collective-permute-start.44 = (bf16[256,1024]{1,0:T(8,128)(2,1)S(1)}, bf16[256,1024]{1,0:T(8,128)(2,1)S(1)}, u32[]{:S(2)}, u32[]{:S(2)}) collective-permute-start(bf16[256,1024]{1,0:T(8,128)(2,1)S(1)} %get-tuple-element.221), channel_id=1, source_target_pairs={{1,0},{0,1},{5,2},{4,3},{3,4},{2,5},{7,6},{6,7},{9,8},{8,9},{13,10... | collective-permute-start | bytes 1572872 | tf_op jit(solution)/shard_map/ppermute | solution.py:594
  420.7 35.3 %collective-permute-start.45 = (bf16[256,1024]{1,0:T(8,128)(2,1)S(1)}, bf16[256,1024]{1,0:T(8,128)(2,1)S(1)}, u32[]{:S(2)}, u32[]{:S(2)}) collective-permute-start(bf16[256,1024]{1,0:T(8,128)(2,1)S(1)} %get-tuple-element.222), channel_id=1, source_target_pairs={{0,0},{1,1},{4,2},{5,3},{2,4},{3,5},{6,6},{7,7},{8,8},{9,9},{12,10... | collective-permute-start | bytes 1572872 | tf_op jit(solution)/shard_map/ppermute | solution.py:594
  (111 other events, 1319.8 us)

commit v2 on v1

--- a/solution.py
+++ b/solution.py
@@ -674,7 +674,7 @@
     lines = jnp.concatenate([own_half(by_kind(qkv_bias)), own_half(fc1_bias)])
     lines = jnp.pad(three_parts(lines), ((0, 0), (0, 3 * qkv_cols - lines.shape[0]))).reshape(9, qkv_cols)
     blocks = along_z(jnp.concatenate([held[:, :qkv_cols], lines, jnp.zeros((7, qkv_cols), low)], axis=0))
-    tokens = to_clips(after(activations, blocks[2])).astype(jnp.float32)
+    tokens = to_clips(after(activations, (blocks[1], blocks[3]))).astype(jnp.float32)
     lines = jnp.stack([item[2 * own_rows : 2 * own_rows + 9] for item in blocks])
     lines = lines.astype(jnp.float32).reshape(4, 3, 3 * qkv_cols).sum(axis=1)
     bias_qkv = lines[:, :qkv_cols].reshape(-1)
@@ -696,22 +696,26 @@
     first_all = both_halves(norm_rows(tokens, attn_gain, attn_shift).astype(low))
     qkv, heads_out, turned, log_total = attend(first_all, weight_qkv, bias_qkv, cosine, sine)
 
-    own = after(held[:, qkv_cols : qkv_cols + out_cols + unit_cols], (blocks[3], tokens))
+    own = after(held[:, qkv_cols : qkv_cols + out_cols + unit_cols], blocks[3])
     blocks = along_z(own, pieces[1:3])
     blocks[0] = after(blocks[0], pieces[3:])
     pieces = over_plane(blocks, heads_out)
+
+    own = after(held[:, qkv_cols + out_cols + unit_cols :], blocks[3])
+    blocks = along_z(own)
+    pieces = pieces[:3] + after(pieces[3:], blocks[1:])
     weight_out, weight_up = assemble(place, pieces, [out_cols, unit_cols])
     resid = tokens + part_sum(contract(heads_out, weight_out, 1, 1)) + out_bias
     second_all = both_halves(norm_rows(resid, mlp_gain, mlp_shift).astype(low))
 
-    own = after(held[:, qkv_cols + out_cols + unit_cols :], blocks[3])
-    blocks = along_z(own, heads_out)
     blocks[0] = after(blocks[0], pieces[3:])
     pieces = over_plane(blocks, second_all)
-    grad_own = to_clips(after(cotangent, blocks[3]))
+    grad_own = to_clips(after(cotangent, second_all))
 
     hidden = jnp.dot(after(second_all, pieces[1:3]), weight_up, preferred_element_type=jnp.float32) + bias_up
-    act = exact_gelu(hidden).astype(low)
+    share = 0.5 + 0.5 * lax.erf(hidden * math.sqrt(0.5))
+    act = (hidden * share).astype(low)
+    slope = (share + hidden * jnp.exp(-0.5 * hidden * hidden) * (1.0 / math.sqrt(2.0 * math.pi))).astype(low)
     pieces = pieces[:3] + after(pieces[3:], act)
     (weight_down,) = assemble(place, pieces, [unit_cols])
     result = resid + part_sum(contract(act, weight_down, 1, 1)) + fc2_bias
@@ -734,7 +738,7 @@
 
     def second_back(even, odd, wait):
         came = after((swap(even[1], "x"), swap(odd[1], "y")), wait)
-        return jnp.concatenate([even[0] + came[0], odd[0] + came[1]])
+        return jnp.concatenate([even[0] + came[0], odd[0] + came[1]]), came
 
     def along_z_back(total, wait, later):
         cols = total.shape[1] // 4
@@ -749,7 +753,7 @@
     sum_fc2_bias = jnp.sum(grad_top, axis=0)
     parts_fc2 = dealt(contract(grad_all, act, 0, 0))
     grad_act = jnp.dot(after(grad_all, parts_fc2), weight_down, preferred_element_type=jnp.float32)
-    grad_hidden = jax.vjp(exact_gelu, hidden)[1](grad_act)[0].astype(low)
+    grad_hidden = (grad_act * slope.astype(jnp.float32)).astype(low)
     sum_fc1_bias = jnp.sum(grad_hidden, axis=0, dtype=jnp.float32)
     grad_second_part = contract(grad_hidden, weight_up, 1, 1)
     sent_fc2 = first_back(parts_fc2, grad_second_part)
@@ -762,24 +766,26 @@
     grad_fc1 = contract(after(second_all, sent_fc2[0]), grad_hidden, 0, 0)
     parts_up = dealt(contract(resid_all, heads_out, 0, 0), grad_fc1)
     grad_heads = jnp.dot(resid_all, weight_out, preferred_element_type=jnp.float32).astype(low)
-    total_fc2 = second_back(*sent_fc2, grad_heads)
-    grad_packed, sum_qkv_bias = attend_back(qkv, after(grad_heads, (parts_up, total_fc2)), turned, log_total, cosine, sine)
+    total_fc2, came_fc2 = second_back(*sent_fc2, grad_heads)
+    grad_packed, sum_qkv_bias = attend_back(qkv, after(grad_heads, (parts_up, came_fc2)), turned, log_total, cosine, sine)
     sent_up = first_back(parts_up, grad_packed)
     parts_qkv = dealt(contract(after(first_all, sent_up), grad_packed, 0, 0))
-    total_up = second_back(*sent_up, parts_qkv)
-    grad_first_part = contract(after(grad_packed, parts_qkv), weight_qkv, 1, 1)
-    grad_first = part_sum(after(grad_first_part, total_up))
+    total_up, came_up = second_back(*sent_up, parts_qkv)
+    grad_first_part = contract(after(grad_packed, came_up), weight_qkv, 1, 1)
+    grad_first = part_sum(grad_first_part)
     first_pull = jax.vjp(norm_rows, tokens, attn_gain, attn_shift)[1]
     grad_input_norm, sum_attn_gain, sum_attn_shift = first_pull(grad_first)
-    input_grad = from_clips((grad_resid + grad_input_norm).astype(low)).astype(jnp.float32)
+    input_low = from_clips((grad_resid + grad_input_norm).astype(low))
+    input_grad = input_low.astype(jnp.float32)
 
     grad_fc2_weight = along_z_back(total_fc2, grad_packed, parts_qkv)
-    both_weights = along_z_back(total_up, grad_first_part, grad_first)
+    both_weights = along_z_back(total_up, grad_first, input_low)
     cuts = both_weights.shape[1] // 2
     both_weights = [both_weights[:, :cuts], both_weights[:, cuts:]]
     grad_out_weight = jnp.concatenate([item[:, :out_cols] for item in both_weights], axis=1)
     grad_fc1_weight = jnp.concatenate([item[:, out_cols:] for item in both_weights], axis=1)
-    total = second_back(*first_back(parts_qkv, grad_first_part), grad_first)
+    sent_qkv = first_back(parts_qkv, grad_first)
+    total, came_qkv = second_back(*sent_qkv, grad_first)
     grad_qkv_weight = by_head(along_z_back(total, grad_first, grad_first))
 
     def by_core(values):
@@ -797,7 +803,10 @@
 
     sums = [sum_attn_gain, sum_attn_shift, sum_out_bias, sum_mlp_gain, sum_mlp_shift, sum_fc2_bias]
     sums = jnp.concatenate(sums + by_core(by_owner(sum_qkv_bias, qkv_cols)) + by_core(by_owner(sum_fc1_bias, unit_cols)))
-    for axis, bit in (("core", 1), ("x", 1), ("y", 1), ("tensor", 1), ("tensor", 2)):
+    stages = (("core", 1, sent_qkv), ("x", 1, None), ("y", 1, came_qkv), ("tensor", 1, input_low), ("tensor", 2, None))
+    for axis, bit, earlier in stages:
+        if earlier is not None:
+            sums = after(sums, earlier)
         sums = sums + swap(sums, axis, bit)
     vectors = sums[: 6 * width].reshape(6, width)
     qkv_sums = sums[6 * width : 6 * width + 8 * qkv_cols].reshape(2, 4, qkv_cols)

time: 473 us -> 483 us (1.021)
  waiting for transfers between devices: 136 us -> 163 us
  matrix products: 81.3 us -> 61.8 us
  starting transfers between devices: 89.5 us -> 72.9 us
  Pallas kernels: 75.3 us -> 85.5 us
  local copies, waits for them, and re-layouts: 35.1 us -> 41.3 us
    ppermute x4, waiting for transfers between devices: 11.6 us -> 32.2 us  [from_clips(): arrived.append(lax.ppermute(sent, EVERY, pairs))]
    ppermute x4, waiting for transfers between devices: 4.79 us -> 22.2 us  [to_clips(): arrived.append(lax.ppermute(sent, EVERY, pairs))]
    dot_general x1, matrix products: 23.4 us -> 7.81 us  [clip_body(): jnp.dot(after(second_all, pieces[1:3]), weight_up, preferred_element_type...]
    ppermute x59, starting transfers between devices: 64.6 us -> 48.9 us  [swap(): lax.ppermute(values, axis, [(i, i ^ bit) for i in range(4 if axis == 'ten...]
    ppermute x59, waiting for transfers between devices: 119 us -> 109 us  [swap(): lax.ppermute(values, axis, [(i, i ^ bit) for i in range(4 if axis == 'ten...]
    pallas_call x3, Pallas kernels: 14.6 us -> 24.8 us  [assemble(): pl.pallas_call(assemble_kernel, grid_spec=pltpu.PrefetchScalarGridSpec(nu...]
    unnamed x152 -> x146, local copies, waits for them, and re-layouts: 17.9 us -> 18.9 us
  transfers between devices with their start and end apart: 67 -> 67, of which waited for: 21 -> 30; matrix products, arithmetic and copies ran while one was open for 32% -> 27% of each run, Pallas kernels for 16% -> 14%
where the time goes in v2:
time: 483 us; the launch traced here: 476 us
  waiting for transfers between devices  163 us (34%)
  Pallas kernels  85.5 us (18%)
  starting transfers between devices  72.9 us (15%)
  matrix products  61.8 us (13%)
  other arithmetic  49.4 us (10%)
  local copies, waits for them, and re-layouts  41.3 us (9%)
    ppermute x59, waiting for transfers between devices, swap(): lax.ppermute(values, axis, [(i, i ^ bit) for i in range(4 if axis == 'ten...  109 us
    ppermute x59, starting transfers between devices, swap(): lax.ppermute(values, axis, [(i, i ^ bit) for i in range(4 if axis == 'ten...  48.9 us
    dot_general x8, matrix products, contract(): lax.dot_general(left, right, (((left_dim,), (right_dim,)), ((), ())), pre...  40.8 us
    ppermute x4, waiting for transfers between devices, from_clips(): arrived.append(lax.ppermute(sent, EVERY, pairs))  32.2 us
    pallas_call x1, Pallas kernels, attend_back(): pl.pallas_call(attend_back_kernel, grid=(pairs,), in_specs=[pl.BlockSpec(...  25.7 us
    pallas_call x3, Pallas kernels, assemble(): pl.pallas_call(assemble_kernel, grid_spec=pltpu.PrefetchScalarGridSpec(nu...  24.8 us
    ppermute x4, waiting for transfers between devices, to_clips(): arrived.append(lax.ppermute(sent, EVERY, pairs))  22.2 us
    pallas_call x1, Pallas kernels, attend(): pl.pallas_call(attend_kernel, grid=(pairs,), in_specs=[pl.BlockSpec((leng...  20.4 us
  transfers between devices with their start and end apart: 67, of which 30 were waited for; matrix products, arithmetic and copies ran while one was open for 27% of the time, Pallas kernels for 14%

profile of v2, /device:TPU:1, one launch (start us, length us, event | category | flops | bytes accessed | tf_op | source)
XLA Modules:
  0.0 476.2 jit_solution(4859792516585152301)
XLA Ops:
  10.6 8.6 %collective-permute-done.2 = bf16[272,384]{1,0:T(8,128)(2,1)} collective-permute-done((bf16[272,384]{1,0:T(8,128)(2,1)}, bf16[272,384]{1,0:T(8,128)(2,1)}, u32[]{:S(2)}, u32[]{:S(2)}) %collective-permute-start.2) | collective-permute-done | bytes 208928 | tf_op jit(solution)/shard_map/ppermute | solution.py:556
  26.3 5.4 %collective-permute-start.4 = (bf16[256,1024]{1,0:T(8,128)(2,1)}, bf16[256,1024]{1,0:T(8,128)(2,1)}, u32[]{:S(2)}, u32[]{:S(2)}) collective-permute-start(bf16[256,1024]{1,0:T(8,128)(2,1)} %get-tuple-element.237), channel_id=1, source_target_pairs={{0,1},{1,0},{2,5},{3,4},{4,3},{5,2},{6,7},{7,6},{8,9},{9,8},{10,13... | collective-permute-start | bytes 1572872 | tf_op jit(solution)/shard_map/ppermute | solution.py:582
  45.2 9.4 %collective-permute-done.5 = bf16[256,1024]{1,0:T(8,128)(2,1)} collective-permute-done((bf16[256,1024]{1,0:T(8,128)(2,1)}, bf16[256,1024]{1,0:T(8,128)(2,1)}, u32[]{:S(2)}, u32[]{:S(2)}) %collective-permute-start.5) | collective-permute-done | bytes 524320 | tf_op jit(solution)/shard_map/ppermute | solution.py:582
  75.3 8.0 %collective-permute-done.12 = bf16[256,640]{1,0:T(8,128)(2,1)S(1)} collective-permute-done((bf16[256,640]{1,0:T(8,128)(2,1)S(1)}, bf16[256,640]{1,0:T(8,128)(2,1)S(1)}, u32[]{:S(2)}, u32[]{:S(2)}) %collective-permute-start.12) | collective-permute-done | bytes 327712 | tf_op jit(solution)/shard_map/ppermute | solution.py:556
  102.1 20.4 %attend.1 = (bf16[1024,1536]{1,0:T(8,128)(2,1)}, bf16[1024,512]{1,0:T(8,128)(2,1)}, f32[4,128,1024]{2,1,0:T(8,128)}, f32[4,2,1024]{2,1,0:T(2,128)}) custom-call(bf16[1024,1024]{1,0:T(8,128)(2,1)} %pad_maximum_fusion.first_ref, bf16[1024,1536]{1,0:T(8,128)(2,1)} %assemble.3.weight_ref, f32[1,1536]{1,0:T(1,128)} %bitcast.110, ...), custom_call_target="tpu_custom_call" | custom-call | flops 20000000000 | bytes 16777216 | tf_op jit(solution)/shard_map/attend/pallas_call | solution.py:389
  127.8 12.4 %collective-permute-done.19 = bf16[256,512]{1,0:T(8,128)(2,1)S(1)} collective-permute-done((bf16[256,512]{1,0:T(8,128)(2,1)S(1)}, bf16[256,512]{1,0:T(8,128)(2,1)S(1)}, u32[]{:S(2)}, u32[]{:S(2)}) %collective-permute-start.19) | collective-permute-done | bytes 262176 | tf_op jit(solution)/shard_map/ppermute | solution.py:556
  140.2 6.1 %collective-permute-done.20 = bf16[256,512]{1,0:T(8,128)(2,1)S(1)} collective-permute-done((bf16[256,512]{1,0:T(8,128)(2,1)S(1)}, bf16[256,512]{1,0:T(8,128)(2,1)S(1)}, u32[]{:S(2)}, u32[]{:S(2)}) %collective-permute-start.20) | collective-permute-done | bytes 262176 | tf_op jit(solution)/shard_map/ppermute | solution.py:556
  147.9 15.5 %assemble.4 = (bf16[1024,512]{1,0:T(8,128)(2,1)}, bf16[1024,2048]{1,0:T(8,128)(2,1)}) custom-call(s32[1]{0:T(128)} %bitcast.7.place_ref, bf16[256,2560]{1,0:T(8,128)(2,1)} %constant_dynamic-update-slice_fusion.own_ref, bf16[256,2560]{1,0:T(8,128)(2,1)} %collective-permute-done.14.x_ref, bf16[256,2560]{1,0:T(8,128)(2,1)} %collective-permute-done.15.y_ref, ...), custom_call_target="tpu_custom_call" | custom-call | bytes 16777216 | tf_op jit(solution)/shard_map/assemble/pallas_call | solution.py:497
  181.0 21.4 %collective-permute-done.24.y_ref = bf16[256,2048]{1,0:T(8,128)(2,1)} collective-permute-done((bf16[256,2048]{1,0:T(8,128)(2,1)}, bf16[256,2048]{1,0:T(8,128)(2,1)}, u32[]{:S(2)}, u32[]{:S(2)}) %collective-permute-start.24) | collective-permute-done | bytes 1048608 | tf_op jit(solution)/shard_map/ppermute | solution.py:556
  211.0 7.8 %multiply_convert_fusion.1 = (bf16[1024,2048]{1,0:T(8,128)(2,1)}, f32[1024,2048]{1,0:T(8,128)}) fusion(f32[2048]{0:T(1024)S(1)} %bitcast.108, bf16[1024,1024]{1,0:T(8,128)(2,1)S(1)} %pad_maximum_fusion.1, bf16[1024,2048]{1,0:T(8,128)(2,1)S(1)} %copy-done.57), kind=kOutput, calls=%fused_computation.8 | convolution fusion | flops 4307550208 | bytes 18882560 | tf_op jit(solution)/shard_map/dot_general | solution.py:715
  220.3 11.3 %collective-permute-done.31 = bf16[256,1024]{1,0:T(8,128)(2,1)S(1)} collective-permute-done((bf16[256,1024]{1,0:T(8,128)(2,1)S(1)}, bf16[256,1024]{1,0:T(8,128)(2,1)S(1)}, u32[]{:S(2)}, u32[]{:S(2)}) %collective-permute-start.31) | collective-permute-done | bytes 524320 | tf_op jit(solution)/shard_map/ppermute | solution.py:582
  238.4 7.6 %fusion.82 = f32[1024,1024]{1,0:T(8,128)S(1)} fusion(bf16[1024,2048]{1,0:T(8,128)(2,1)} %get-tuple-element.283, bf16[1024,2048]{1,0:T(8,128)(2,1)} %assemble.5), kind=kOutput, calls=%fused_computation.286 | convolution fusion | flops 4294967296 | bytes 12582912 | tf_op jit(solution)/shard_map/dot_general | solution.py:46
  252.9 6.3 %convolution_convert_fusion.2.refs_0_ = bf16[1024,2048]{1,0:T(8,128)(2,1)} fusion(bf16[1024,2048]{1,0:T(8,128)(2,1)S(1)} %copy-done.62, bf16[512,1024]{1,0:T(8,128)(2,1)S(1)} %get-tuple-element.212, bf16[512,1024]{1,0:T(8,128)(2,1)S(1)} %get-tuple-element.211), kind=kOutput, calls=%fused_computation.12 | convolution fusion | flops 4301258752 | bytes 10485760 | tf_op jit(solution)/shard_map/dot_general | solution.py:46
  265.9 11.0 %convert_reduce_fusion = (f32[2048]{0:T(1024)S(1)}, bf16[1024,2048]{1,0:T(8,128)(2,1)S(1)}) fusion(f32[1024,2048]{1,0:T(8,128)} %get-tuple-element.284, f32[2048]{0:T(1024)S(1)} %bitcast.109, bf16[1024,1024]{1,0:T(8,128)(2,1)} %pad_maximum_fusion.2, bf16[1024,2048]{1,0:T(8,128)(2,1)} %assemble.5), kind=kOutput, calls=%fused_computation.6 | convolution fusion | flops 4326422528 | bytes 18890752 | tf_op jit(solution)/shard_map/dot_general | solution.py:755
  282.8 5.7 %collective-permute-done.35 = bf16[2,128,2048]{2,1,0:T(8,128)(2,1)S(1)} collective-permute-done((bf16[2,128,2048]{2,1,0:T(8,128)(2,1)}, bf16[2,128,2048]{2,1,0:T(8,128)(2,1)S(1)}, u32[]{:S(2)}, u32[]{:S(2)}) %collective-permute-start.35) | collective-permute-done | bytes 1048608 | tf_op jit(solution)/shard_map/ppermute | solution.py:556
  304.9 6.8 %convolution_convert_fusion.1.refs_1_ = bf16[1024,2048]{1,0:T(8,128)(2,1)} fusion(bf16[1024,1024]{1,0:T(8,128)(2,1)S(1)} %copy-done.18, bf16[1024,2048]{1,0:T(8,128)(2,1)S(1)} %get-tuple-element.286), kind=kOutput, calls=%fused_computation.11 | convolution fusion | flops 4297064448 | bytes 10485760 | tf_op jit(solution)/shard_map/dot_general | solution.py:46
  312.0 10.3 %collective-permute-done.29 = bf16[256,1024]{1,0:T(8,128)(2,1)S(1)} collective-permute-done((bf16[256,1024]{1,0:T(8,128)(2,1)S(1)}, bf16[256,1024]{1,0:T(8,128)(2,1)S(1)}, u32[]{:S(2)}, u32[]{:S(2)}) %collective-permute-start.29) | collective-permute-done | bytes 524320 | tf_op jit(solution)/shard_map/ppermute | solution.py:594
  329.3 5.5 %deal.4 = (bf16[2,128,2560]{2,1,0:T(8,128)(2,1)}, bf16[2,128,2560]{2,1,0:T(8,128)(2,1)}, bf16[2,128,2560]{2,1,0:T(8,128)(2,1)}, bf16[2,128,2560]{2,1,0:T(8,128)(2,1)}) custom-call(s32[1]{0:T(128)} %bitcast.7.place_ref, bf16[1024,512]{1,0:T(8,128)(2,1)} %convolution_convert_fusion.3.refs_0_, bf16[1024,2048]{1,0:T(8,128)(2,1)} %convolution_convert_fusion.1.refs_1_), custom_call_target="tpu_custom_call" | custom-call | bytes 16777216 | tf_op jit(solution)/shard_map/deal/pallas_call | solution.py:530
  337.0 25.7 %attend_back.1 = (bf16[1024,1536]{1,0:T(8,128)(2,1)}, f32[1,1536]{1,0:T(1,128)}) custom-call(bf16[1024,1536]{1,0:T(8,128)(2,1)} %get-tuple-element.103.qkv_ref, bf16[1024,512]{1,0:T(8,128)(2,1)} %convolution_convert_fusion.4.grad_ref, f32[4,128,1024]{2,1,0:T(8,128)} %get-tuple-element.114.turned_ref, f32[4,2,1024]{2,1,0:T(2,128)} %get-tuple-element.115.log_ref, ...), custom_call_target="tpu_custom_call" | custom-call | flops 27000000512 | bytes 16777216 | tf_op jit(solution)/shard_map/attend_back/pallas_call | solution.py:457
  388.8 5.3 %fusion.84 = f32[1024,1024]{1,0:T(8,128)S(1)} fusion(bf16[1024,1536]{1,0:T(8,128)(2,1)} %get-tuple-element.126, bf16[1024,1536]{1,0:T(8,128)(2,1)S(1)} %copy-done.15), kind=kOutput, calls=%fused_computation.288 | convolution fusion | flops 3221225472 | bytes 10485760 | tf_op jit(solution)/shard_map/dot_general | solution.py:46
  415.9 7.6 %collective-permute-done.49 = f32[13312]{0:T(1024)S(1)} collective-permute-done((f32[13312]{0:T(1024)S(1)}, f32[13312]{0:T(1024)S(1)}, u32[]{:S(2)}, u32[]{:S(2)}) %collective-permute-start.49) | collective-permute-done | bytes 53280 | tf_op jit(solution)/shard_map/ppermute | solution.py:556
  432.6 12.9 %collective-permute-done.44 = bf16[256,1024]{1,0:T(8,128)(2,1)S(1)} collective-permute-done((bf16[256,1024]{1,0:T(8,128)(2,1)S(1)}, bf16[256,1024]{1,0:T(8,128)(2,1)S(1)}, u32[]{:S(2)}, u32[]{:S(2)}) %collective-permute-start.44) | collective-permute-done | bytes 524320 | tf_op jit(solution)/shard_map/ppermute | solution.py:594
  445.6 8.6 %collective-permute-done.45 = bf16[256,1024]{1,0:T(8,128)(2,1)S(1)} collective-permute-done((bf16[256,1024]{1,0:T(8,128)(2,1)S(1)}, bf16[256,1024]{1,0:T(8,128)(2,1)S(1)}, u32[]{:S(2)}, u32[]{:S(2)}) %collective-permute-start.45) | collective-permute-done | bytes 524320 | tf_op jit(solution)/shard_map/ppermute | solution.py:594
  461.2 5.5 %collective-permute-done.54 = f32[13312]{0:T(1024)S(1)} collective-permute-done((f32[13312]{0:T(1024)S(1)}, f32[13312]{0:T(1024)S(1)}, u32[]{:S(2)}, u32[]{:S(2)}) %collective-permute-start.54) | collective-permute-done | bytes 53280 | tf_op jit(solution)/shard_map/ppermute | solution.py:556
  (443 shorter events, 228.8 us)
Async XLA Ops:
  31.8 22.9 %collective-permute-start.5 = (bf16[256,1024]{1,0:T(8,128)(2,1)}, bf16[256,1024]{1,0:T(8,128)(2,1)}, u32[]{:S(2)}, u32[]{:S(2)}) collective-permute-start(bf16[256,1024]{1,0:T(8,128)(2,1)} %get-tuple-element.238), channel_id=1, source_target_pairs={{0,0},{1,1},{2,4},{3,5},{4,2},{5,3},{6,6},{7,7},{8,8},{9,9},{10,12... | collective-permute-start | bytes 1572872 | tf_op jit(solution)/shard_map/ppermute | solution.py:582
  57.6 41.6 %collective-permute-start.6 = (bf16[512,1024]{1,0:T(8,128)(2,1)S(1)}, bf16[512,1024]{1,0:T(8,128)(2,1)}, u32[]{:S(2)}, u32[]{:S(2)}) collective-permute-start(bf16[512,1024]{1,0:T(8,128)(2,1)S(1)} %fusion.12), channel_id=1, source_target_pairs={{0,4},{4,0},{1,5},{5,1},{2,6},{6,2},{3,7},{7,3},{8,12},{12,8},{9,1... | collective-permute-start | bytes 3145736 | tf_op jit(solution)/shard_map/ppermute | solution.py:556
  61.7 21.6 %collective-permute-start.9 = (bf16[128,1536]{1,0:T(8,128)(2,1)}, bf16[128,1536]{1,0:T(8,128)(2,1)}, u32[]{:S(2)}, u32[]{:S(2)}) collective-permute-start(bf16[128,1536]{1,0:T(8,128)(2,1)} %slice.456), channel_id=1, source_target_pairs={{0,8},{8,0},{1,9},{9,1},{2,10},{10,2},{3,11},{11,3},{4,12},{12,4},... | collective-permute-start | bytes 1179656 | tf_op jit(solution)/shard_map/ppermute | solution.py:556
  94.6 28.7 %collective-permute-start.15 = (bf16[256,2560]{1,0:T(8,128)(2,1)}, bf16[256,2560]{1,0:T(8,128)(2,1)}, u32[]{:S(2)}, u32[]{:S(2)}) collective-permute-start(bf16[256,2560]{1,0:T(8,128)(2,1)} %constant_dynamic-update-slice_fusion.own_ref), channel_id=1, source_target_pairs={{0,16},{16,0},{1,17},{17,1},{2,18},{18,2},{3,19},{19,3},{4,20},{20... | collective-permute-start | bytes 3932168 | tf_op jit(solution)/shard_map/ppermute | solution.py:556
  94.8 28.5 %collective-permute-start.14 = (bf16[256,2560]{1,0:T(8,128)(2,1)}, bf16[256,2560]{1,0:T(8,128)(2,1)}, u32[]{:S(2)}, u32[]{:S(2)}) collective-permute-start(bf16[256,2560]{1,0:T(8,128)(2,1)} %constant_dynamic-update-slice_fusion.own_ref), channel_id=1, source_target_pairs={{0,8},{8,0},{1,9},{9,1},{2,10},{10,2},{3,11},{11,3},{4,12},{12,4},... | collective-permute-start | bytes 3932168 | tf_op jit(solution)/shard_map/ppermute | solution.py:556
  126.3 21.5 %collective-permute-start.17 = (bf16[128,2560]{1,0:T(8,128)(2,1)S(1)}, bf16[128,2560]{1,0:T(8,128)(2,1)}, u32[]{:S(2)}, u32[]{:S(2)}) collective-permute-start(bf16[128,2560]{1,0:T(8,128)(2,1)S(1)} %slice.380), channel_id=1, source_target_pairs={{0,16},{16,0},{1,17},{17,1},{2,18},{18,2},{3,19},{19,3},{4,20},{20... | collective-permute-start | bytes 1966088 | tf_op jit(solution)/shard_map/ppermute | solution.py:556
  177.5 24.9 %collective-permute-start.24 = (bf16[256,2048]{1,0:T(8,128)(2,1)}, bf16[256,2048]{1,0:T(8,128)(2,1)}, u32[]{:S(2)}, u32[]{:S(2)}) collective-permute-start(bf16[256,2048]{1,0:T(8,128)(2,1)} %constant_dynamic-update-slice_fusion.4.own_ref), channel_id=1, source_target_pairs={{0,16},{16,0},{1,17},{17,1},{2,18},{18,2},{3,19},{19,3},{4,20},{20... | collective-permute-start | bytes 3145736 | tf_op jit(solution)/shard_map/ppermute | solution.py:556
  177.8 24.6 %collective-permute-start.23 = (bf16[256,2048]{1,0:T(8,128)(2,1)}, bf16[256,2048]{1,0:T(8,128)(2,1)}, u32[]{:S(2)}, u32[]{:S(2)}) collective-permute-start(bf16[256,2048]{1,0:T(8,128)(2,1)} %constant_dynamic-update-slice_fusion.4.own_ref), channel_id=1, source_target_pairs={{0,8},{8,0},{1,9},{9,1},{2,10},{10,2},{3,11},{11,3},{4,12},{12,4},... | collective-permute-start | bytes 3145736 | tf_op jit(solution)/shard_map/ppermute | solution.py:556
  204.5 29.0 %collective-permute-start.25 = (bf16[128,2048]{1,0:T(8,128)(2,1)S(1)}, bf16[128,2048]{1,0:T(8,128)(2,1)}, u32[]{:S(2)}, u32[]{:S(2)}) collective-permute-start(bf16[128,2048]{1,0:T(8,128)(2,1)S(1)} %slice.385), channel_id=1, source_target_pairs={{0,8},{8,0},{1,9},{9,1},{2,10},{10,2},{3,11},{11,3},{4,12},{12,4},... | collective-permute-start | bytes 1572872 | tf_op jit(solution)/shard_map/ppermute | solution.py:556
  205.0 28.6 %collective-permute-start.26 = (bf16[128,2048]{1,0:T(8,128)(2,1)S(1)}, bf16[128,2048]{1,0:T(8,128)(2,1)}, u32[]{:S(2)}, u32[]{:S(2)}) collective-permute-start(bf16[128,2048]{1,0:T(8,128)(2,1)S(1)} %slice.386), channel_id=1, source_target_pairs={{0,16},{16,0},{1,17},{17,1},{2,18},{18,2},{3,19},{19,3},{4,20},{20... | collective-permute-start | bytes 1572872 | tf_op jit(solution)/shard_map/ppermute | solution.py:556
  209.1 22.5 %collective-permute-start.31 = (bf16[256,1024]{1,0:T(8,128)(2,1)S(1)}, bf16[256,1024]{1,0:T(8,128)(2,1)S(1)}, u32[]{:S(2)}, u32[]{:S(2)}) collective-permute-start(bf16[256,1024]{1,0:T(8,128)(2,1)S(1)} %get-tuple-element.230), channel_id=1, source_target_pairs={{0,0},{1,1},{2,4},{3,5},{4,2},{5,3},{6,6},{7,7},{8,8},{9,9},{10,12... | collective-permute-start | bytes 1572872 | tf_op jit(solution)/shard_map/ppermute | solution.py:582
  247.2 45.6 %collective-permute-start.27 = (bf16[512,1024]{1,0:T(8,128)(2,1)}, bf16[512,1024]{1,0:T(8,128)(2,1)}, u32[]{:S(2)}, u32[]{:S(2)}) collective-permute-start(bf16[512,1024]{1,0:T(8,128)(2,1)} %select_convert_fusion.2), channel_id=1, source_target_pairs={{0,4},{4,0},{1,5},{5,1},{2,6},{6,2},{3,7},{7,3},{8,12},{12,8},{9,1... | collective-permute-start | bytes 3145736 | tf_op jit(solution)/shard_map/ppermute | solution.py:556
  264.0 24.4 %collective-permute-start.35 = (bf16[2,128,2048]{2,1,0:T(8,128)(2,1)}, bf16[2,128,2048]{2,1,0:T(8,128)(2,1)S(1)}, u32[]{:S(2)}, u32[]{:S(2)}) collective-permute-start(bf16[2,128,2048]{2,1,0:T(8,128)(2,1)} %get-tuple-element.99), channel_id=1, source_target_pairs={{0,16},{16,0},{1,17},{17,1},{2,18},{18,2},{3,19},{19,3},{4,20},{20... | collective-permute-start | bytes 3145736 | tf_op jit(solution)/shard_map/ppermute | solution.py:556
  265.0 24.2 %collective-permute-start.36 = (bf16[2,128,2048]{2,1,0:T(8,128)(2,1)}, bf16[2,128,2048]{2,1,0:T(8,128)(2,1)S(1)}, u32[]{:S(2)}, u32[]{:S(2)}) collective-permute-start(bf16[2,128,2048]{2,1,0:T(8,128)(2,1)} %get-tuple-element.101), channel_id=1, source_target_pairs={{0,8},{8,0},{1,9},{9,1},{2,10},{10,2},{3,11},{11,3},{4,12},{12,4},... | collective-permute-start | bytes 3145736 | tf_op jit(solution)/shard_map/ppermute | solution.py:556
  290.0 39.1 %collective-permute-start.37 = (bf16[128,2048]{1,0:T(8,128)(2,1)S(1)}, bf16[128,2048]{1,0:T(8,128)(2,1)S(1)}, u32[]{:S(2)}, u32[]{:S(2)}) collective-permute-start(bf16[128,2048]{1,0:T(8,128)(2,1)S(1)} %slice_bitcast_fusion.7), channel_id=1, source_target_pairs={{0,8},{8,0},{1,9},{9,1},{2,10},{10,2},{3,11},{11,3},{4,12},{12,4},... | collective-permute-start | bytes 1572872 | tf_op jit(solution)/shard_map/ppermute | solution.py:556
  291.0 38.1 %collective-permute-start.38 = (bf16[128,2048]{1,0:T(8,128)(2,1)S(1)}, bf16[128,2048]{1,0:T(8,128)(2,1)S(1)}, u32[]{:S(2)}, u32[]{:S(2)}) collective-permute-start(bf16[128,2048]{1,0:T(8,128)(2,1)S(1)} %slice_bitcast_fusion.6), channel_id=1, source_target_pairs={{0,16},{16,0},{1,17},{17,1},{2,18},{18,2},{3,19},{19,3},{4,20},{20... | collective-permute-start | bytes 1572872 | tf_op jit(solution)/shard_map/ppermute | solution.py:556
  334.8 30.3 %collective-permute-start.39 = (bf16[2,128,2560]{2,1,0:T(8,128)(2,1)}, bf16[2,128,2560]{2,1,0:T(8,128)(2,1)}, u32[]{:S(2)}, u32[]{:S(2)}) collective-permute-start(bf16[2,128,2560]{2,1,0:T(8,128)(2,1)} %get-tuple-element.107), channel_id=1, source_target_pairs={{0,16},{16,0},{1,17},{17,1},{2,18},{18,2},{3,19},{19,3},{4,20},{20... | collective-permute-start | bytes 3932168 | tf_op jit(solution)/shard_map/ppermute | solution.py:556
  335.7 29.4 %collective-permute-start.40 = (bf16[2,128,2560]{2,1,0:T(8,128)(2,1)}, bf16[2,128,2560]{2,1,0:T(8,128)(2,1)}, u32[]{:S(2)}, u32[]{:S(2)}) collective-permute-start(bf16[2,128,2560]{2,1,0:T(8,128)(2,1)} %get-tuple-element.109), channel_id=1, source_target_pairs={{0,8},{8,0},{1,9},{9,1},{2,10},{10,2},{3,11},{11,3},{4,12},{12,4},... | collective-permute-start | bytes 3932168 | tf_op jit(solution)/shard_map/ppermute | solution.py:556
  337.0 25.7 %collective-permute-start.64 = (bf16[256,512]{1,0:T(8,128)(2,1)}, bf16[256,512]{1,0:T(8,128)(2,1)S(1)}, u32[]{:S(2)}, u32[]{:S(2)}) collective-permute-start(bf16[256,512]{1,0:T(8,128)(2,1)} %pad_maximum_fusion.18), channel_id=1, source_target_pairs={{0,1},{1,0},{2,3},{3,2},{4,5},{5,4},{6,7},{7,6},{8,9},{9,8},{10,11... | collective-permute-start | bytes 786440 | tf_op jit(solution)/shard_map/ppermute | solution.py:556
  414.0 41.6 %collective-permute-start.61 = (bf16[256,640]{1,0:T(8,128)(2,1)S(1)}, bf16[256,640]{1,0:T(8,128)(2,1)S(1)}, u32[]{:S(2)}, u32[]{:S(2)}) collective-permute-start(bf16[256,640]{1,0:T(8,128)(2,1)S(1)} %get-tuple-element.217), channel_id=1, source_target_pairs={{0,2},{1,3},{2,0},{3,1},{4,6},{5,7},{6,4},{7,5},{8,10},{9,11},{10,... | collective-permute-start | bytes 983048 | tf_op jit(solution)/shard_map/ppermute | solution.py:556
  414.9 40.8 %collective-permute-start.59 = (bf16[256,640]{1,0:T(8,128)(2,1)S(1)}, bf16[256,640]{1,0:T(8,128)(2,1)S(1)}, u32[]{:S(2)}, u32[]{:S(2)}) collective-permute-start(bf16[256,640]{1,0:T(8,128)(2,1)S(1)} %get-tuple-element.218), channel_id=1, source_target_pairs={{0,1},{1,0},{2,3},{3,2},{4,5},{5,4},{6,7},{7,6},{8,9},{9,8},{10,11... | collective-permute-start | bytes 983048 | tf_op jit(solution)/shard_map/ppermute | solution.py:556
  423.5 22.1 %collective-permute-start.44 = (bf16[256,1024]{1,0:T(8,128)(2,1)S(1)}, bf16[256,1024]{1,0:T(8,128)(2,1)S(1)}, u32[]{:S(2)}, u32[]{:S(2)}) collective-permute-start(bf16[256,1024]{1,0:T(8,128)(2,1)S(1)} %get-tuple-element.225), channel_id=1, source_target_pairs={{1,0},{0,1},{5,2},{4,3},{3,4},{2,5},{7,6},{6,7},{9,8},{8,9},{13,10... | collective-permute-start | bytes 1572872 | tf_op jit(solution)/shard_map/ppermute | solution.py:594
  425.5 28.6 %collective-permute-start.45 = (bf16[256,1024]{1,0:T(8,128)(2,1)S(1)}, bf16[256,1024]{1,0:T(8,128)(2,1)S(1)}, u32[]{:S(2)}, u32[]{:S(2)}) collective-permute-start(bf16[256,1024]{1,0:T(8,128)(2,1)S(1)} %get-tuple-element.226), channel_id=1, source_target_pairs={{0,0},{1,1},{4,2},{5,3},{2,4},{3,5},{6,6},{7,7},{8,8},{9,9},{12,10... | collective-permute-start | bytes 1572872 | tf_op jit(solution)/shard_map/ppermute | solution.py:594
  432.0 26.7 %collective-permute-start.56 = (bf16[256,384]{1,0:T(8,128)(2,1)S(1)}, bf16[256,384]{1,0:T(8,128)(2,1)S(1)}, u32[]{:S(2)}, u32[]{:S(2)}) collective-permute-start(bf16[256,384]{1,0:T(8,128)(2,1)S(1)} %pad_maximum_fusion.20), channel_id=1, source_target_pairs={{0,1},{1,0},{2,3},{3,2},{4,5},{5,4},{6,7},{7,6},{8,9},{9,8},{10,11... | collective-permute-start | bytes 589832 | tf_op jit(solution)/shard_map/ppermute | solution.py:556
  (106 other events, 923.7 us)

commit v3 on v2

--- a/solution.py
+++ b/solution.py
@@ -580,7 +580,7 @@
     for turn, pairs in enumerate(clip_routes(False)):
         sent = pick(odd, values[turn], values[1 - turn])
         arrived.append(lax.ppermute(sent, EVERY, pairs))
-    return jnp.concatenate(
+    return arrived, jnp.concatenate(
         [pick(odd, arrived[0], arrived[1]), pick(odd, arrived[1], arrived[0])], axis=0
     )
 
@@ -674,13 +674,16 @@
     lines = jnp.concatenate([own_half(by_kind(qkv_bias)), own_half(fc1_bias)])
     lines = jnp.pad(three_parts(lines), ((0, 0), (0, 3 * qkv_cols - lines.shape[0]))).reshape(9, qkv_cols)
     blocks = along_z(jnp.concatenate([held[:, :qkv_cols], lines, jnp.zeros((7, qkv_cols), low)], axis=0))
-    tokens = to_clips(after(activations, (blocks[1], blocks[3]))).astype(jnp.float32)
+    tokens = to_clips(after(activations, (blocks[1], blocks[3])))[1].astype(jnp.float32)
     lines = jnp.stack([item[2 * own_rows : 2 * own_rows + 9] for item in blocks])
     lines = lines.astype(jnp.float32).reshape(4, 3, 3 * qkv_cols).sum(axis=1)
     bias_qkv = lines[:, :qkv_cols].reshape(-1)
     bias_up = lines[:, qkv_cols : qkv_cols + unit_cols].reshape(-1)
-    pieces = over_plane([item[: 2 * own_rows] for item in blocks])
+    blocks_up = along_z(after(held[:, qkv_cols : qkv_cols + out_cols + unit_cols], blocks[3]))
+    pieces = over_plane([item[: 2 * own_rows] for item in blocks], blocks_up[1:3])
     (weight_qkv,) = assemble(place, pieces, [qkv_cols])
+    blocks_down = along_z(after(held[:, qkv_cols + out_cols + unit_cols :], blocks_up[3]))
+    weight_qkv = after(weight_qkv, blocks_down[1:3])
 
     def both_halves(values):
         other = swap(values, "core")
@@ -696,23 +699,19 @@
     first_all = both_halves(norm_rows(tokens, attn_gain, attn_shift).astype(low))
     qkv, heads_out, turned, log_total = attend(first_all, weight_qkv, bias_qkv, cosine, sine)
 
-    own = after(held[:, qkv_cols : qkv_cols + out_cols + unit_cols], blocks[3])
-    blocks = along_z(own, pieces[1:3])
-    blocks[0] = after(blocks[0], pieces[3:])
-    pieces = over_plane(blocks, heads_out)
-
-    own = after(held[:, qkv_cols + out_cols + unit_cols :], blocks[3])
-    blocks = along_z(own)
-    pieces = pieces[:3] + after(pieces[3:], blocks[1:])
+    blocks_up[0] = after(blocks_up[0], pieces[3:])
+    pieces = over_plane(blocks_up, heads_out)
+    pieces = pieces[:3] + after(pieces[3:], blocks_down[3])
     weight_out, weight_up = assemble(place, pieces, [out_cols, unit_cols])
     resid = tokens + part_sum(contract(heads_out, weight_out, 1, 1)) + out_bias
     second_all = both_halves(norm_rows(resid, mlp_gain, mlp_shift).astype(low))
 
-    blocks[0] = after(blocks[0], pieces[3:])
-    pieces = over_plane(blocks, second_all)
-    grad_own = to_clips(after(cotangent, second_all))
-
-    hidden = jnp.dot(after(second_all, pieces[1:3]), weight_up, preferred_element_type=jnp.float32) + bias_up
+    blocks_down[0] = after(blocks_down[0], pieces[3:])
+    arrived, grad_own = to_clips(after(cotangent, blocks_down[3]))
+    pieces = over_plane(blocks_down, second_all)
+
+    second_all = after(second_all, (pieces[1:3], arrived))
+    hidden = jnp.dot(second_all, weight_up, preferred_element_type=jnp.float32) + bias_up
     share = 0.5 + 0.5 * lax.erf(hidden * math.sqrt(0.5))
     act = (hidden * share).astype(low)
     slope = (share + hidden * jnp.exp(-0.5 * hidden * hidden) * (1.0 / math.sqrt(2.0 * math.pi))).astype(low)
@@ -803,7 +802,7 @@
 
     sums = [sum_attn_gain, sum_attn_shift, sum_out_bias, sum_mlp_gain, sum_mlp_shift, sum_fc2_bias]
     sums = jnp.concatenate(sums + by_core(by_owner(sum_qkv_bias, qkv_cols)) + by_core(by_owner(sum_fc1_bias, unit_cols)))
-    stages = (("core", 1, sent_qkv), ("x", 1, None), ("y", 1, came_qkv), ("tensor", 1, input_low), ("tensor", 2, None))
+    stages = (("core", 1, sent_qkv), ("x", 1, None), ("y", 1, (came_qkv, input_low)), ("tensor", 1, None), ("tensor", 2, None))
     for axis, bit, earlier in stages:
         if earlier is not None:
             sums = after(sums, earlier)

time: 483 us -> 438 us (0.907)
  waiting for transfers between devices: 163 us -> 137 us
  Pallas kernels: 85.5 us -> 75.4 us
  local copies, waits for them, and re-layouts: 41.3 us -> 31.5 us
  starting transfers between devices: 72.9 us -> 81.9 us
  other arithmetic: 49.4 us -> 43.8 us
    ppermute x59, waiting for transfers between devices: 109 us -> 68 us  [swap(): lax.ppermute(values, axis, [(i, i ^ bit) for i in range(4 if axis == 'ten...]
    ppermute x4, waiting for transfers between devices: 22.2 us -> 33.8 us  [to_clips(): arrived.append(lax.ppermute(sent, EVERY, pairs))]
    pallas_call x3, Pallas kernels: 24.8 us -> 14.7 us  [assemble(): pl.pallas_call(assemble_kernel, grid_spec=pltpu.PrefetchScalarGridSpec(nu...]
    ppermute x59, starting transfers between devices: 48.9 us -> 56.5 us  [swap(): lax.ppermute(values, axis, [(i, i ^ bit) for i in range(4 if axis == 'ten...]
    unnamed x146 -> x154, local copies, waits for them, and re-layouts: 18.9 us -> 16.2 us
  transfers between devices with their start and end apart: 67 -> 67, of which waited for: 30 -> 24; matrix products, arithmetic and copies ran while one was open for 27% -> 27% of each run, Pallas kernels for 14% -> 16%
where the time goes in v3:
time: 438 us; the launch traced here: 432 us
  waiting for transfers between devices  137 us (31%)
  starting transfers between devices  81.9 us (19%)
  Pallas kernels  75.4 us (17%)
  matrix products  59.8 us (14%)
  other arithmetic  43.8 us (10%)
  local copies, waits for them, and re-layouts  31.5 us (7%)
    ppermute x59, waiting for transfers between devices, swap(): lax.ppermute(values, axis, [(i, i ^ bit) for i in range(4 if axis == 'ten...  68 us
    ppermute x59, starting transfers between devices, swap(): lax.ppermute(values, axis, [(i, i ^ bit) for i in range(4 if axis == 'ten...  56.5 us
    dot_general x8, matrix products, contract(): lax.dot_general(left, right, (((left_dim,), (right_dim,)), ((), ())), pre...  40.7 us
    ppermute x4, waiting for transfers between devices, from_clips(): arrived.append(lax.ppermute(sent, EVERY, pairs))  35.3 us
    ppermute x4, waiting for transfers between devices, to_clips(): arrived.append(lax.ppermute(sent, EVERY, pairs))  33.8 us
    pallas_call x1, Pallas kernels, attend_back(): pl.pallas_call(attend_back_kernel, grid=(pairs,), in_specs=[pl.BlockSpec(...  25.7 us
    pallas_call x1, Pallas kernels, attend(): pl.pallas_call(attend_kernel, grid=(pairs,), in_specs=[pl.BlockSpec((leng...  20.4 us
    unnamed x154, local copies, waits for them, and re-layouts  16.2 us
  transfers between devices with their start and end apart: 67, of which 24 were waited for; matrix products, arithmetic and copies ran while one was open for 27% of the time, Pallas kernels for 16%

profile of v3, /device:TPU:1, one launch (start us, length us, event | category | flops | bytes accessed | tf_op | source)
XLA Modules:
  0.0 432.4 jit_solution(14169118228180659191)
XLA Ops:
  11.1 7.2 %collective-permute-done.2 = bf16[272,384]{1,0:T(8,128)(2,1)S(1)} collective-permute-done((bf16[272,384]{1,0:T(8,128)(2,1)S(1)}, bf16[272,384]{1,0:T(8,128)(2,1)S(1)}, u32[]{:S(2)}, u32[]{:S(2)}) %collective-permute-start.2) | collective-permute-done | bytes 208928 | tf_op jit(solution)/shard_map/ppermute | solution.py:556
  24.1 5.5 %collective-permute-start.4 = (bf16[256,1024]{1,0:T(8,128)(2,1)S(1)}, bf16[256,1024]{1,0:T(8,128)(2,1)S(1)}, u32[]{:S(2)}, u32[]{:S(2)}) collective-permute-start(bf16[256,1024]{1,0:T(8,128)(2,1)S(1)} %get-tuple-element.239), channel_id=1, source_target_pairs={{0,1},{1,0},{2,5},{3,4},{4,3},{5,2},{6,7},{7,6},{8,9},{9,8},{10,13... | collective-permute-start | bytes 1572872 | tf_op jit(solution)/shard_map/ppermute | solution.py:582
  33.9 8.3 %collective-permute-done.4 = bf16[256,1024]{1,0:T(8,128)(2,1)S(1)} collective-permute-done((bf16[256,1024]{1,0:T(8,128)(2,1)S(1)}, bf16[256,1024]{1,0:T(8,128)(2,1)S(1)}, u32[]{:S(2)}, u32[]{:S(2)}) %collective-permute-start.4) | collective-permute-done | bytes 524320 | tf_op jit(solution)/shard_map/ppermute | solution.py:582
  43.5 19.3 %collective-permute-done.5 = bf16[256,1024]{1,0:T(8,128)(2,1)S(1)} collective-permute-done((bf16[256,1024]{1,0:T(8,128)(2,1)S(1)}, bf16[256,1024]{1,0:T(8,128)(2,1)S(1)}, u32[]{:S(2)}, u32[]{:S(2)}) %collective-permute-start.5) | collective-permute-done | bytes 524320 | tf_op jit(solution)/shard_map/ppermute | solution.py:582
  77.4 5.0 %collective-permute-start.15 = (bf16[256,512]{1,0:T(8,128)(2,1)S(1)}, bf16[256,512]{1,0:T(8,128)(2,1)S(1)}, u32[]{:S(2)}, u32[]{:S(2)}) collective-permute-start(bf16[256,512]{1,0:T(8,128)(2,1)S(1)} %pad_maximum_fusion.19), channel_id=1, source_target_pairs={{0,2},{1,3},{2,0},{3,1},{4,6},{5,7},{6,4},{7,5},{8,10},{9,11},{10,... | collective-permute-start | bytes 786440 | tf_op jit(solution)/shard_map/ppermute | solution.py:556
  97.8 20.4 %attend.1 = (bf16[1024,1536]{1,0:T(8,128)(2,1)}, bf16[1024,512]{1,0:T(8,128)(2,1)}, f32[4,128,1024]{2,1,0:T(8,128)}, f32[4,2,1024]{2,1,0:T(2,128)}) custom-call(bf16[1024,1024]{1,0:T(8,128)(2,1)} %pad_maximum_fusion.first_ref, bf16[1024,1536]{1,0:T(8,128)(2,1)} %assemble.3.weight_ref, f32[1,1536]{1,0:T(1,128)} %bitcast.110, ...), custom_call_target="tpu_custom_call" | custom-call | flops 20000000000 | bytes 16777216 | tf_op jit(solution)/shard_map/attend/pallas_call | solution.py:389
  123.4 5.3 %collective-permute-done.20 = bf16[256,512]{1,0:T(8,128)(2,1)S(1)} collective-permute-done((bf16[256,512]{1,0:T(8,128)(2,1)S(1)}, bf16[256,512]{1,0:T(8,128)(2,1)S(1)}, u32[]{:S(2)}, u32[]{:S(2)}) %collective-permute-start.20) | collective-permute-done | bytes 262176 | tf_op jit(solution)/shard_map/ppermute | solution.py:556
  137.5 5.4 %assemble.4 = (bf16[1024,512]{1,0:T(8,128)(2,1)}, bf16[1024,2048]{1,0:T(8,128)(2,1)}) custom-call(s32[1]{0:T(128)} %bitcast.7.place_ref, bf16[256,2560]{1,0:T(8,128)(2,1)} %constant_dynamic-update-slice_fusion.own_ref, bf16[256,2560]{1,0:T(8,128)(2,1)} %collective-permute-done.16.x_ref, bf16[256,2560]{1,0:T(8,128)(2,1)} %collective-permute-done.17.y_ref, ...), custom_call_target="tpu_custom_call" | custom-call | bytes 16777216 | tf_op jit(solution)/shard_map/assemble/pallas_call | solution.py:497
  151.0 6.2 %collective-permute-done.25 = bf16[256,1024]{1,0:T(8,128)(2,1)} collective-permute-done((bf16[256,1024]{1,0:T(8,128)(2,1)}, bf16[256,1024]{1,0:T(8,128)(2,1)}, u32[]{:S(2)}, u32[]{:S(2)}) %collective-permute-start.25) | collective-permute-done | bytes 524320 | tf_op jit(solution)/shard_map/ppermute | solution.py:582
  167.7 19.0 %collective-permute-done.24.y_ref = bf16[256,2048]{1,0:T(8,128)(2,1)S(1)} collective-permute-done((bf16[256,2048]{1,0:T(8,128)(2,1)S(1)}, bf16[256,2048]{1,0:T(8,128)(2,1)S(1)}, u32[]{:S(2)}, u32[]{:S(2)}) %collective-permute-start.24) | collective-permute-done | bytes 1048608 | tf_op jit(solution)/shard_map/ppermute | solution.py:556
  191.1 7.2 %multiply_convert_fusion.1 = (bf16[1024,2048]{1,0:T(8,128)(2,1)S(1)}, f32[1024,2048]{1,0:T(8,128)}) fusion(f32[2048]{0:T(1024)S(1)} %bitcast.108, bf16[1024,1024]{1,0:T(8,128)(2,1)S(1)} %pad_maximum_fusion.1, bf16[1024,2048]{1,0:T(8,128)(2,1)S(1)} %copy-done.61), kind=kOutput, calls=%fused_computation.8 | convolution fusion | flops 4307550208 | bytes 18882560 | tf_op jit(solution)/shard_map/dot_general | solution.py:714
  200.3 6.3 %convolution_convert_fusion.2.refs_0_ = bf16[1024,2048]{1,0:T(8,128)(2,1)} fusion(bf16[1024,2048]{1,0:T(8,128)(2,1)S(1)} %get-tuple-element.285, bf16[512,1024]{1,0:T(8,128)(2,1)S(1)} %get-tuple-element.214, bf16[512,1024]{1,0:T(8,128)(2,1)S(1)} %get-tuple-element.213), kind=kOutput, calls=%fused_computation.12 | convolution fusion | flops 4301258752 | bytes 10485760 | tf_op jit(solution)/shard_map/dot_general | solution.py:46
  217.4 7.7 %fusion.82 = f32[1024,1024]{1,0:T(8,128)S(1)} fusion(bf16[1024,2048]{1,0:T(8,128)(2,1)} %copy-done.66, bf16[1024,2048]{1,0:T(8,128)(2,1)} %assemble.5), kind=kOutput, calls=%fused_computation.286 | convolution fusion | flops 4294967296 | bytes 12582912 | tf_op jit(solution)/shard_map/dot_general | solution.py:46
  225.2 9.6 %convert_reduce_fusion = (f32[2048]{0:T(1024)S(1)}, bf16[1024,2048]{1,0:T(8,128)(2,1)S(1)}) fusion(f32[1024,2048]{1,0:T(8,128)} %get-tuple-element.286, f32[2048]{0:T(1024)S(1)} %bitcast.109, bf16[1024,1024]{1,0:T(8,128)(2,1)S(1)} %copy-done.20, bf16[1024,2048]{1,0:T(8,128)(2,1)S(1)} %copy-done.12), kind=kOutput, calls=%fused_computation.6 | convolution fusion | flops 4326422528 | bytes 18890752 | tf_op jit(solution)/shard_map/dot_general | solution.py:754
  257.8 6.6 %convolution_convert_fusion.1.refs_1_ = bf16[1024,2048]{1,0:T(8,128)(2,1)} fusion(bf16[1024,1024]{1,0:T(8,128)(2,1)S(1)} %copy-done.19, bf16[1024,2048]{1,0:T(8,128)(2,1)S(1)} %get-tuple-element.288), kind=kOutput, calls=%fused_computation.11 | convolution fusion | flops 4297064448 | bytes 10485760 | tf_op jit(solution)/shard_map/dot_general | solution.py:46
  265.4 9.9 %collective-permute-done.31 = bf16[256,1024]{1,0:T(8,128)(2,1)S(1)} collective-permute-done((bf16[256,1024]{1,0:T(8,128)(2,1)S(1)}, bf16[256,1024]{1,0:T(8,128)(2,1)S(1)}, u32[]{:S(2)}, u32[]{:S(2)}) %collective-permute-start.31) | collective-permute-done | bytes 524320 | tf_op jit(solution)/shard_map/ppermute | solution.py:594
  282.2 5.5 %deal.4 = (bf16[2,128,2560]{2,1,0:T(8,128)(2,1)}, bf16[2,128,2560]{2,1,0:T(8,128)(2,1)}, bf16[2,128,2560]{2,1,0:T(8,128)(2,1)}, bf16[2,128,2560]{2,1,0:T(8,128)(2,1)}) custom-call(s32[1]{0:T(128)} %bitcast.7.place_ref, bf16[1024,512]{1,0:T(8,128)(2,1)} %convolution_convert_fusion.3.refs_0_, bf16[1024,2048]{1,0:T(8,128)(2,1)} %convolution_convert_fusion.1.refs_1_), custom_call_target="tpu_custom_call" | custom-call | bytes 16777216 | tf_op jit(solution)/shard_map/deal/pallas_call | solution.py:530
  289.8 25.7 %attend_back.1 = (bf16[1024,1536]{1,0:T(8,128)(2,1)}, f32[1,1536]{1,0:T(1,128)}) custom-call(bf16[1024,1536]{1,0:T(8,128)(2,1)} %get-tuple-element.106.qkv_ref, bf16[1024,512]{1,0:T(8,128)(2,1)} %convolution_convert_fusion.4.grad_ref, f32[4,128,1024]{2,1,0:T(8,128)} %get-tuple-element.117.turned_ref, f32[4,2,1024]{2,1,0:T(2,128)} %get-tuple-element.118.log_ref, ...), custom_call_target="tpu_custom_call" | custom-call | flops 27000000512 | bytes 16777216 | tf_op jit(solution)/shard_map/attend_back/pallas_call | solution.py:457
  325.2 5.2 %convolution_convert_fusion.refs_0_ = bf16[1024,1536]{1,0:T(8,128)(2,1)} fusion(bf16[1024,1024]{1,0:T(8,128)(2,1)S(1)} %copy-done.17, bf16[1024,1536]{1,0:T(8,128)(2,1)S(1)} %copy-done.65), kind=kOutput, calls=%fused_computation.10 | convolution fusion | flops 3222798336 | bytes 8388608 | tf_op jit(solution)/shard_map/dot_general | solution.py:46
  341.6 5.3 %fusion.84 = f32[1024,1024]{1,0:T(8,128)S(1)} fusion(bf16[1024,1536]{1,0:T(8,128)(2,1)} %get-tuple-element.129, bf16[1024,1536]{1,0:T(8,128)(2,1)S(1)} %copy-done.14), kind=kOutput, calls=%fused_computation.288 | convolution fusion | flops 3221225472 | bytes 10485760 | tf_op jit(solution)/shard_map/dot_general | solution.py:46
  353.2 5.4 %collective-permute-done.46 = bf16[2,128,1536]{2,1,0:T(8,128)(2,1)S(1)} collective-permute-done((bf16[2,128,1536]{2,1,0:T(8,128)(2,1)}, bf16[2,128,1536]{2,1,0:T(8,128)(2,1)S(1)}, u32[]{:S(2)}, u32[]{:S(2)}) %collective-permute-start.46) | collective-permute-done | bytes 786464 | tf_op jit(solution)/shard_map/ppermute | solution.py:556
  368.8 7.8 %collective-permute-done.49 = f32[13312]{0:T(1024)S(1)} collective-permute-done((f32[13312]{0:T(1024)S(1)}, f32[13312]{0:T(1024)S(1)}, u32[]{:S(2)}, u32[]{:S(2)}) %collective-permute-start.49) | collective-permute-done | bytes 53280 | tf_op jit(solution)/shard_map/ppermute | solution.py:556
  382.5 15.9 %collective-permute-done.44 = bf16[256,1024]{1,0:T(8,128)(2,1)S(1)} collective-permute-done((bf16[256,1024]{1,0:T(8,128)(2,1)S(1)}, bf16[256,1024]{1,0:T(8,128)(2,1)S(1)}, u32[]{:S(2)}, u32[]{:S(2)}) %collective-permute-start.44) | collective-permute-done | bytes 524320 | tf_op jit(solution)/shard_map/ppermute | solution.py:594
  398.4 8.5 %collective-permute-done.45 = bf16[256,1024]{1,0:T(8,128)(2,1)S(1)} collective-permute-done((bf16[256,1024]{1,0:T(8,128)(2,1)S(1)}, bf16[256,1024]{1,0:T(8,128)(2,1)S(1)}, u32[]{:S(2)}, u32[]{:S(2)}) %collective-permute-start.45) | collective-permute-done | bytes 524320 | tf_op jit(solution)/shard_map/ppermute | solution.py:594
  (453 shorter events, 201.2 us)
Async XLA Ops:
  29.7 33.1 %collective-permute-start.5 = (bf16[256,1024]{1,0:T(8,128)(2,1)S(1)}, bf16[256,1024]{1,0:T(8,128)(2,1)S(1)}, u32[]{:S(2)}, u32[]{:S(2)}) collective-permute-start(bf16[256,1024]{1,0:T(8,128)(2,1)S(1)} %get-tuple-element.240), channel_id=1, source_target_pairs={{0,0},{1,1},{2,4},{3,5},{4,2},{5,3},{6,6},{7,7},{8,8},{9,9},{10,12... | collective-permute-start | bytes 1572872 | tf_op jit(solution)/shard_map/ppermute | solution.py:582
  32.0 33.1 %collective-permute-start.10 = (bf16[256,640]{1,0:T(8,128)(2,1)S(1)}, bf16[256,640]{1,0:T(8,128)(2,1)}, u32[]{:S(2)}, u32[]{:S(2)}) collective-permute-start(bf16[256,640]{1,0:T(8,128)(2,1)S(1)} %pad_maximum_fusion.17), channel_id=1, source_target_pairs={{0,2},{1,3},{2,0},{3,1},{4,6},{5,7},{6,4},{7,5},{8,10},{9,11},{10,... | collective-permute-start | bytes 983048 | tf_op jit(solution)/shard_map/ppermute | solution.py:556
  32.1 33.0 %collective-permute-start.9 = (bf16[256,640]{1,0:T(8,128)(2,1)S(1)}, bf16[256,640]{1,0:T(8,128)(2,1)S(1)}, u32[]{:S(2)}, u32[]{:S(2)}) collective-permute-start(bf16[256,640]{1,0:T(8,128)(2,1)S(1)} %pad_maximum_fusion.17), channel_id=1, source_target_pairs={{0,1},{1,0},{2,3},{3,2},{4,5},{5,4},{6,7},{7,6},{8,9},{9,8},{10,11... | collective-permute-start | bytes 983048 | tf_op jit(solution)/shard_map/ppermute | solution.py:556
  32.6 32.5 %collective-permute-start.8 = (bf16[256,1536]{1,0:T(8,128)(2,1)S(1)}, bf16[256,1536]{1,0:T(8,128)(2,1)S(1)}, u32[]{:S(2)}, u32[]{:S(2)}) collective-permute-start(bf16[256,1536]{1,0:T(8,128)(2,1)S(1)} %pad_maximum_fusion.10.own_ref), channel_id=1, source_target_pairs={{0,16},{16,0},{1,17},{17,1},{2,18},{18,2},{3,19},{19,3},{4,20},{20... | collective-permute-start | bytes 2359304 | tf_op jit(solution)/shard_map/ppermute | solution.py:556
  42.2 22.9 %collective-permute-start.7 = (bf16[256,1536]{1,0:T(8,128)(2,1)S(1)}, bf16[256,1536]{1,0:T(8,128)(2,1)S(1)}, u32[]{:S(2)}, u32[]{:S(2)}) collective-permute-start(bf16[256,1536]{1,0:T(8,128)(2,1)S(1)} %pad_maximum_fusion.10.own_ref), channel_id=1, source_target_pairs={{0,8},{8,0},{1,9},{9,1},{2,10},{10,2},{3,11},{11,3},{4,12},{12,4},... | collective-permute-start | bytes 2359304 | tf_op jit(solution)/shard_map/ppermute | solution.py:556
  64.0 30.8 %collective-permute-start.6 = (bf16[512,1024]{1,0:T(8,128)(2,1)S(1)}, bf16[512,1024]{1,0:T(8,128)(2,1)}, u32[]{:S(2)}, u32[]{:S(2)}) collective-permute-start(bf16[512,1024]{1,0:T(8,128)(2,1)S(1)} %fusion.12), channel_id=1, source_target_pairs={{0,4},{4,0},{1,5},{5,1},{2,6},{6,2},{3,7},{7,3},{8,12},{12,8},{9,1... | collective-permute-start | bytes 3145736 | tf_op jit(solution)/shard_map/ppermute | solution.py:556
  89.7 29.3 %collective-permute-start.17 = (bf16[256,2560]{1,0:T(8,128)(2,1)}, bf16[256,2560]{1,0:T(8,128)(2,1)}, u32[]{:S(2)}, u32[]{:S(2)}) collective-permute-start(bf16[256,2560]{1,0:T(8,128)(2,1)} %constant_dynamic-update-slice_fusion.own_ref), channel_id=1, source_target_pairs={{0,16},{16,0},{1,17},{17,1},{2,18},{18,2},{3,19},{19,3},{4,20},{20... | collective-permute-start | bytes 3932168 | tf_op jit(solution)/shard_map/ppermute | solution.py:556
  90.0 29.1 %collective-permute-start.16 = (bf16[256,2560]{1,0:T(8,128)(2,1)}, bf16[256,2560]{1,0:T(8,128)(2,1)}, u32[]{:S(2)}, u32[]{:S(2)}) collective-permute-start(bf16[256,2560]{1,0:T(8,128)(2,1)} %constant_dynamic-update-slice_fusion.own_ref), channel_id=1, source_target_pairs={{0,8},{8,0},{1,9},{9,1},{2,10},{10,2},{3,11},{11,3},{4,12},{12,4},... | collective-permute-start | bytes 3932168 | tf_op jit(solution)/shard_map/ppermute | solution.py:556
  134.2 23.0 %collective-permute-start.25 = (bf16[256,1024]{1,0:T(8,128)(2,1)}, bf16[256,1024]{1,0:T(8,128)(2,1)}, u32[]{:S(2)}, u32[]{:S(2)}) collective-permute-start(bf16[256,1024]{1,0:T(8,128)(2,1)} %get-tuple-element.236), channel_id=1, source_target_pairs={{0,0},{1,1},{2,4},{3,5},{4,2},{5,3},{6,6},{7,7},{8,8},{9,9},{10,12... | collective-permute-start | bytes 1572872 | tf_op jit(solution)/shard_map/ppermute | solution.py:582
  162.3 24.4 %collective-permute-start.24 = (bf16[256,2048]{1,0:T(8,128)(2,1)S(1)}, bf16[256,2048]{1,0:T(8,128)(2,1)S(1)}, u32[]{:S(2)}, u32[]{:S(2)}) collective-permute-start(bf16[256,2048]{1,0:T(8,128)(2,1)S(1)} %constant_dynamic-update-slice_fusion.4.own_ref), channel_id=1, source_target_pairs={{0,16},{16,0},{1,17},{17,1},{2,18},{18,2},{3,19},{19,3},{4,20},{20... | collective-permute-start | bytes 3145736 | tf_op jit(solution)/shard_map/ppermute | solution.py:556
  163.5 24.1 %collective-permute-start.23 = (bf16[256,2048]{1,0:T(8,128)(2,1)S(1)}, bf16[256,2048]{1,0:T(8,128)(2,1)S(1)}, u32[]{:S(2)}, u32[]{:S(2)}) collective-permute-start(bf16[256,2048]{1,0:T(8,128)(2,1)S(1)} %constant_dynamic-update-slice_fusion.4.own_ref), channel_id=1, source_target_pairs={{0,8},{8,0},{1,9},{9,1},{2,10},{10,2},{3,11},{11,3},{4,12},{12,4},... | collective-permute-start | bytes 3145736 | tf_op jit(solution)/shard_map/ppermute | solution.py:556
  189.3 23.3 %collective-permute-start.27 = (bf16[128,2048]{1,0:T(8,128)(2,1)}, bf16[128,2048]{1,0:T(8,128)(2,1)}, u32[]{:S(2)}, u32[]{:S(2)}) collective-permute-start(bf16[128,2048]{1,0:T(8,128)(2,1)} %slice.387), channel_id=1, source_target_pairs={{0,8},{8,0},{1,9},{9,1},{2,10},{10,2},{3,11},{11,3},{4,12},{12,4},... | collective-permute-start | bytes 1572872 | tf_op jit(solution)/shard_map/ppermute | solution.py:556
  190.6 22.0 %collective-permute-start.28 = (bf16[128,2048]{1,0:T(8,128)(2,1)}, bf16[128,2048]{1,0:T(8,128)(2,1)}, u32[]{:S(2)}, u32[]{:S(2)}) collective-permute-start(bf16[128,2048]{1,0:T(8,128)(2,1)} %slice.388), channel_id=1, source_target_pairs={{0,16},{16,0},{1,17},{17,1},{2,18},{18,2},{3,19},{19,3},{4,20},{20... | collective-permute-start | bytes 1572872 | tf_op jit(solution)/shard_map/ppermute | solution.py:556
  211.4 31.2 %collective-permute-start.35 = (bf16[2,128,2048]{2,1,0:T(8,128)(2,1)}, bf16[2,128,2048]{2,1,0:T(8,128)(2,1)}, u32[]{:S(2)}, u32[]{:S(2)}) collective-permute-start(bf16[2,128,2048]{2,1,0:T(8,128)(2,1)} %get-tuple-element.102), channel_id=1, source_target_pairs={{0,16},{16,0},{1,17},{17,1},{2,18},{18,2},{3,19},{19,3},{4,20},{20... | collective-permute-start | bytes 3145736 | tf_op jit(solution)/shard_map/ppermute | solution.py:556
  212.4 30.2 %collective-permute-start.36 = (bf16[2,128,2048]{2,1,0:T(8,128)(2,1)}, bf16[2,128,2048]{2,1,0:T(8,128)(2,1)}, u32[]{:S(2)}, u32[]{:S(2)}) collective-permute-start(bf16[2,128,2048]{2,1,0:T(8,128)(2,1)} %get-tuple-element.104), channel_id=1, source_target_pairs={{0,8},{8,0},{1,9},{9,1},{2,10},{10,2},{3,11},{11,3},{4,12},{12,4},... | collective-permute-start | bytes 3145736 | tf_op jit(solution)/shard_map/ppermute | solution.py:556
  246.0 36.1 %collective-permute-start.37 = (bf16[128,2048]{1,0:T(8,128)(2,1)S(1)}, bf16[128,2048]{1,0:T(8,128)(2,1)S(1)}, u32[]{:S(2)}, u32[]{:S(2)}) collective-permute-start(bf16[128,2048]{1,0:T(8,128)(2,1)S(1)} %slice_bitcast_fusion.7), channel_id=1, source_target_pairs={{0,8},{8,0},{1,9},{9,1},{2,10},{10,2},{3,11},{11,3},{4,12},{12,4},... | collective-permute-start | bytes 1572872 | tf_op jit(solution)/shard_map/ppermute | solution.py:556
  247.4 34.7 %collective-permute-start.38 = (bf16[128,2048]{1,0:T(8,128)(2,1)S(1)}, bf16[128,2048]{1,0:T(8,128)(2,1)S(1)}, u32[]{:S(2)}, u32[]{:S(2)}) collective-permute-start(bf16[128,2048]{1,0:T(8,128)(2,1)S(1)} %slice_bitcast_fusion.6), channel_id=1, source_target_pairs={{0,16},{16,0},{1,17},{17,1},{2,18},{18,2},{3,19},{19,3},{4,20},{20... | collective-permute-start | bytes 1572872 | tf_op jit(solution)/shard_map/ppermute | solution.py:556
  287.7 30.2 %collective-permute-start.39 = (bf16[2,128,2560]{2,1,0:T(8,128)(2,1)}, bf16[2,128,2560]{2,1,0:T(8,128)(2,1)}, u32[]{:S(2)}, u32[]{:S(2)}) collective-permute-start(bf16[2,128,2560]{2,1,0:T(8,128)(2,1)} %get-tuple-element.110), channel_id=1, source_target_pairs={{0,16},{16,0},{1,17},{17,1},{2,18},{18,2},{3,19},{19,3},{4,20},{20... | collective-permute-start | bytes 3932168 | tf_op jit(solution)/shard_map/ppermute | solution.py:556
  288.8 29.1 %collective-permute-start.40 = (bf16[2,128,2560]{2,1,0:T(8,128)(2,1)}, bf16[2,128,2560]{2,1,0:T(8,128)(2,1)}, u32[]{:S(2)}, u32[]{:S(2)}) collective-permute-start(bf16[2,128,2560]{2,1,0:T(8,128)(2,1)} %get-tuple-element.112), channel_id=1, source_target_pairs={{0,8},{8,0},{1,9},{9,1},{2,10},{10,2},{3,11},{11,3},{4,12},{12,4},... | collective-permute-start | bytes 3932168 | tf_op jit(solution)/shard_map/ppermute | solution.py:556
  289.8 25.8 %collective-permute-start.64 = (bf16[256,512]{1,0:T(8,128)(2,1)}, bf16[256,512]{1,0:T(8,128)(2,1)S(1)}, u32[]{:S(2)}, u32[]{:S(2)}) collective-permute-start(bf16[256,512]{1,0:T(8,128)(2,1)} %pad_maximum_fusion.18), channel_id=1, source_target_pairs={{0,1},{1,0},{2,3},{3,2},{4,5},{5,4},{6,7},{7,6},{8,9},{9,8},{10,11... | collective-permute-start | bytes 786440 | tf_op jit(solution)/shard_map/ppermute | solution.py:556
  366.9 41.6 %collective-permute-start.61 = (bf16[256,640]{1,0:T(8,128)(2,1)S(1)}, bf16[256,640]{1,0:T(8,128)(2,1)S(1)}, u32[]{:S(2)}, u32[]{:S(2)}) collective-permute-start(bf16[256,640]{1,0:T(8,128)(2,1)S(1)} %get-tuple-element.219), channel_id=1, source_target_pairs={{0,2},{1,3},{2,0},{3,1},{4,6},{5,7},{6,4},{7,5},{8,10},{9,11},{10,... | collective-permute-start | bytes 983048 | tf_op jit(solution)/shard_map/ppermute | solution.py:556
  367.8 40.7 %collective-permute-start.59 = (bf16[256,640]{1,0:T(8,128)(2,1)S(1)}, bf16[256,640]{1,0:T(8,128)(2,1)S(1)}, u32[]{:S(2)}, u32[]{:S(2)}) collective-permute-start(bf16[256,640]{1,0:T(8,128)(2,1)S(1)} %get-tuple-element.220), channel_id=1, source_target_pairs={{0,1},{1,0},{2,3},{3,2},{4,5},{5,4},{6,7},{7,6},{8,9},{9,8},{10,11... | collective-permute-start | bytes 983048 | tf_op jit(solution)/shard_map/ppermute | solution.py:556
  378.5 28.4 %collective-permute-start.45 = (bf16[256,1024]{1,0:T(8,128)(2,1)S(1)}, bf16[256,1024]{1,0:T(8,128)(2,1)S(1)}, u32[]{:S(2)}, u32[]{:S(2)}) collective-permute-start(bf16[256,1024]{1,0:T(8,128)(2,1)S(1)} %get-tuple-element.228), channel_id=1, source_target_pairs={{0,0},{1,1},{4,2},{5,3},{2,4},{3,5},{6,6},{7,7},{8,8},{9,9},{12,10... | collective-permute-start | bytes 1572872 | tf_op jit(solution)/shard_map/ppermute | solution.py:594
  381.8 29.8 %collective-permute-start.56 = (bf16[256,384]{1,0:T(8,128)(2,1)S(1)}, bf16[256,384]{1,0:T(8,128)(2,1)S(1)}, u32[]{:S(2)}, u32[]{:S(2)}) collective-permute-start(bf16[256,384]{1,0:T(8,128)(2,1)S(1)} %pad_maximum_fusion.20), channel_id=1, source_target_pairs={{0,1},{1,0},{2,3},{3,2},{4,5},{5,4},{6,7},{7,6},{8,9},{9,8},{10,11... | collective-permute-start | bytes 589832 | tf_op jit(solution)/shard_map/ppermute | solution.py:556
  (112 other events, 942.4 us)

commit v4 on v3

--- a/solution.py
+++ b/solution.py
@@ -585,13 +585,15 @@
     )
 
 
-def from_clips(values):
+def from_clips(values, wait=None):
     odd = lax.axis_index("tensor") % 2 == 1
     rows = values.shape[0] // 2
     arrived = []
     for turn, pairs in enumerate(clip_routes(True)):
         sent = pick(odd, values[turn * rows : (turn + 1) * rows], values[(1 - turn) * rows : (2 - turn) * rows])
         arrived.append(lax.ppermute(sent, EVERY, pairs))
+    if wait is not None:
+        arrived = after(arrived, wait)
     return jnp.stack([pick(odd, arrived[0], arrived[1]), pick(odd, arrived[1], arrived[0])])
 
 
@@ -718,7 +720,6 @@
     pieces = pieces[:3] + after(pieces[3:], act)
     (weight_down,) = assemble(place, pieces, [unit_cols])
     result = resid + part_sum(contract(act, weight_down, 1, 1)) + fc2_bias
-    output = from_clips(result.astype(low))
 
     def to_core(total):
         kept = pick(core == 1, total[0], total[1])
@@ -767,6 +768,7 @@
     grad_heads = jnp.dot(resid_all, weight_out, preferred_element_type=jnp.float32).astype(low)
     total_fc2, came_fc2 = second_back(*sent_fc2, grad_heads)
     grad_packed, sum_qkv_bias = attend_back(qkv, after(grad_heads, (parts_up, came_fc2)), turned, log_total, cosine, sine)
+    output = from_clips(result.astype(low), grad_packed)
     sent_up = first_back(parts_up, grad_packed)
     parts_qkv = dealt(contract(after(first_all, sent_up), grad_packed, 0, 0))
     total_up, came_up = second_back(*sent_up, parts_qkv)
@@ -777,7 +779,7 @@
     input_low = from_clips((grad_resid + grad_input_norm).astype(low))
     input_grad = input_low.astype(jnp.float32)
 
-    grad_fc2_weight = along_z_back(total_fc2, grad_packed, parts_qkv)
+    grad_fc2_weight = along_z_back(total_fc2, parts_qkv, grad_first)
     both_weights = along_z_back(total_up, grad_first, input_low)
     cuts = both_weights.shape[1] // 2
     both_weights = [both_weights[:, :cuts], both_weights[:, cuts:]]

time: 438 us -> 434 us (level)
  waiting for transfers between devices: 137 us -> 115 us
  starting transfers between devices: 81.9 us -> 95.4 us
    ppermute x59, starting transfers between devices: 56.5 us -> 69.9 us  [swap(): lax.ppermute(values, axis, [(i, i ^ bit) for i in range(4 if axis == 'ten...]
    ppermute x4, waiting for transfers between devices: 35.3 us -> 22.9 us  [from_clips(): arrived.append(lax.ppermute(sent, EVERY, pairs))]
    ppermute x59, waiting for transfers between devices: 68 us -> 58.1 us  [swap(): lax.ppermute(values, axis, [(i, i ^ bit) for i in range(4 if axis == 'ten...]
    unnamed x154 -> x166, local copies, waits for them, and re-layouts: 16.2 us -> 17.3 us
  transfers between devices with their start and end apart: 67 -> 67, of which waited for: 24 -> 18; matrix products, arithmetic and copies ran while one was open for 27% -> 28% of each run, Pallas kernels for 16% -> 18%
where the time goes in v4:
time: 434 us; the launch traced here: 428 us
  waiting for transfers between devices  115 us (26%)
  starting transfers between devices  95.4 us (22%)
  Pallas kernels  75.6 us (17%)
  matrix products  60.3 us (14%)
  other arithmetic  48 us (11%)
  local copies, waits for them, and re-layouts  31 us (7%)
    ppermute x59, starting transfers between devices, swap(): lax.ppermute(values, axis, [(i, i ^ bit) for i in range(4 if axis == 'ten...  69.9 us
    ppermute x59, waiting for transfers between devices, swap(): lax.ppermute(values, axis, [(i, i ^ bit) for i in range(4 if axis == 'ten...  58.1 us
    dot_general x8, matrix products, contract(): lax.dot_general(left, right, (((left_dim,), (right_dim,)), ((), ())), pre...  41.2 us
    ppermute x4, waiting for transfers between devices, to_clips(): arrived.append(lax.ppermute(sent, EVERY, pairs))  33.8 us
    pallas_call x1, Pallas kernels, attend_back(): pl.pallas_call(attend_back_kernel, grid=(pairs,), in_specs=[pl.BlockSpec(...  25.8 us
    ppermute x4, waiting for transfers between devices, from_clips(): arrived.append(lax.ppermute(sent, EVERY, pairs))  22.9 us
    pallas_call x1, Pallas kernels, attend(): pl.pallas_call(attend_kernel, grid=(pairs,), in_specs=[pl.BlockSpec((leng...  20.4 us
    unnamed x166, local copies, waits for them, and re-layouts  17.3 us
  transfers between devices with their start and end apart: 67, of which 18 were waited for; matrix products, arithmetic and copies ran while one was open for 28% of the time, Pallas kernels for 18%

profile of v4, /device:TPU:1, one launch (start us, length us, event | category | flops | bytes accessed | tf_op | source)
XLA Modules:
  0.0 427.9 jit_solution(4322459211310053162)
XLA Ops:
  11.1 7.2 %collective-permute-done.2 = bf16[272,384]{1,0:T(8,128)(2,1)S(1)} collective-permute-done((bf16[272,384]{1,0:T(8,128)(2,1)S(1)}, bf16[272,384]{1,0:T(8,128)(2,1)S(1)}, u32[]{:S(2)}, u32[]{:S(2)}) %collective-permute-start.2) | collective-permute-done | bytes 208928 | tf_op jit(solution)/shard_map/ppermute | solution.py:556
  24.1 5.5 %collective-permute-start.4 = (bf16[256,1024]{1,0:T(8,128)(2,1)S(1)}, bf16[256,1024]{1,0:T(8,128)(2,1)S(1)}, u32[]{:S(2)}, u32[]{:S(2)}) collective-permute-start(bf16[256,1024]{1,0:T(8,128)(2,1)S(1)} %get-tuple-element.243), channel_id=1, source_target_pairs={{0,1},{1,0},{2,5},{3,4},{4,3},{5,2},{6,7},{7,6},{8,9},{9,8},{10,13... | collective-permute-start | bytes 1572872 | tf_op jit(solution)/shard_map/ppermute | solution.py:582
  33.9 8.4 %collective-permute-done.4 = bf16[256,1024]{1,0:T(8,128)(2,1)S(1)} collective-permute-done((bf16[256,1024]{1,0:T(8,128)(2,1)S(1)}, bf16[256,1024]{1,0:T(8,128)(2,1)S(1)}, u32[]{:S(2)}, u32[]{:S(2)}) %collective-permute-start.4) | collective-permute-done | bytes 524320 | tf_op jit(solution)/shard_map/ppermute | solution.py:582
  43.5 19.3 %collective-permute-done.5 = bf16[256,1024]{1,0:T(8,128)(2,1)S(1)} collective-permute-done((bf16[256,1024]{1,0:T(8,128)(2,1)S(1)}, bf16[256,1024]{1,0:T(8,128)(2,1)S(1)}, u32[]{:S(2)}, u32[]{:S(2)}) %collective-permute-start.5) | collective-permute-done | bytes 524320 | tf_op jit(solution)/shard_map/ppermute | solution.py:582
  77.4 5.0 %collective-permute-start.15 = (bf16[256,512]{1,0:T(8,128)(2,1)S(1)}, bf16[256,512]{1,0:T(8,128)(2,1)S(1)}, u32[]{:S(2)}, u32[]{:S(2)}) collective-permute-start(bf16[256,512]{1,0:T(8,128)(2,1)S(1)} %pad_maximum_fusion.19), channel_id=1, source_target_pairs={{0,2},{1,3},{2,0},{3,1},{4,6},{5,7},{6,4},{7,5},{8,10},{9,11},{10,... | collective-permute-start | bytes 786440 | tf_op jit(solution)/shard_map/ppermute | solution.py:556
  97.7 20.4 %attend.1 = (bf16[1024,1536]{1,0:T(8,128)(2,1)}, bf16[1024,512]{1,0:T(8,128)(2,1)}, f32[4,128,1024]{2,1,0:T(8,128)}, f32[4,2,1024]{2,1,0:T(2,128)}) custom-call(bf16[1024,1024]{1,0:T(8,128)(2,1)} %pad_maximum_fusion.first_ref, bf16[1024,1536]{1,0:T(8,128)(2,1)} %assemble.3.weight_ref, f32[1,1536]{1,0:T(1,128)} %bitcast.110, ...), custom_call_target="tpu_custom_call" | custom-call | flops 20000000000 | bytes 16777216 | tf_op jit(solution)/shard_map/attend/pallas_call | solution.py:389
  123.3 5.3 %collective-permute-done.20 = bf16[256,512]{1,0:T(8,128)(2,1)S(1)} collective-permute-done((bf16[256,512]{1,0:T(8,128)(2,1)S(1)}, bf16[256,512]{1,0:T(8,128)(2,1)S(1)}, u32[]{:S(2)}, u32[]{:S(2)}) %collective-permute-start.20) | collective-permute-done | bytes 262176 | tf_op jit(solution)/shard_map/ppermute | solution.py:556
  137.5 5.4 %assemble.4 = (bf16[1024,512]{1,0:T(8,128)(2,1)}, bf16[1024,2048]{1,0:T(8,128)(2,1)}) custom-call(s32[1]{0:T(128)} %bitcast.7.place_ref, bf16[256,2560]{1,0:T(8,128)(2,1)} %constant_dynamic-update-slice_fusion.own_ref, bf16[256,2560]{1,0:T(8,128)(2,1)} %collective-permute-done.16.x_ref, bf16[256,2560]{1,0:T(8,128)(2,1)} %collective-permute-done.17.y_ref, ...), custom_call_target="tpu_custom_call" | custom-call | bytes 16777216 | tf_op jit(solution)/shard_map/assemble/pallas_call | solution.py:497
  151.0 6.1 %collective-permute-done.25 = bf16[256,1024]{1,0:T(8,128)(2,1)} collective-permute-done((bf16[256,1024]{1,0:T(8,128)(2,1)}, bf16[256,1024]{1,0:T(8,128)(2,1)}, u32[]{:S(2)}, u32[]{:S(2)}) %collective-permute-start.25) | collective-permute-done | bytes 524320 | tf_op jit(solution)/shard_map/ppermute | solution.py:582
  167.6 19.1 %collective-permute-done.24.y_ref = bf16[256,2048]{1,0:T(8,128)(2,1)S(1)} collective-permute-done((bf16[256,2048]{1,0:T(8,128)(2,1)S(1)}, bf16[256,2048]{1,0:T(8,128)(2,1)S(1)}, u32[]{:S(2)}, u32[]{:S(2)}) %collective-permute-start.24) | collective-permute-done | bytes 1048608 | tf_op jit(solution)/shard_map/ppermute | solution.py:556
  191.0 7.2 %multiply_convert_fusion.1 = (bf16[1024,2048]{1,0:T(8,128)(2,1)S(1)}, f32[1024,2048]{1,0:T(8,128)}) fusion(f32[2048]{0:T(1024)S(1)} %bitcast.108, bf16[1024,1024]{1,0:T(8,128)(2,1)S(1)} %pad_maximum_fusion.1, bf16[1024,2048]{1,0:T(8,128)(2,1)S(1)} %copy-done.67), kind=kOutput, calls=%fused_computation.8 | convolution fusion | flops 4307550208 | bytes 18882560 | tf_op jit(solution)/shard_map/dot_general | solution.py:716
  200.2 6.2 %convolution_convert_fusion.2.refs_0_ = bf16[1024,2048]{1,0:T(8,128)(2,1)} fusion(bf16[1024,2048]{1,0:T(8,128)(2,1)S(1)} %get-tuple-element.289, bf16[512,1024]{1,0:T(8,128)(2,1)S(1)} %get-tuple-element.218, bf16[512,1024]{1,0:T(8,128)(2,1)S(1)} %get-tuple-element.217), kind=kOutput, calls=%fused_computation.12 | convolution fusion | flops 4301258752 | bytes 10485760 | tf_op jit(solution)/shard_map/dot_general | solution.py:46
  217.2 7.7 %fusion.82 = f32[1024,1024]{1,0:T(8,128)S(1)} fusion(bf16[1024,2048]{1,0:T(8,128)(2,1)} %copy-done.72, bf16[1024,2048]{1,0:T(8,128)(2,1)} %assemble.5), kind=kOutput, calls=%fused_computation.286 | convolution fusion | flops 4294967296 | bytes 12582912 | tf_op jit(solution)/shard_map/dot_general | solution.py:46
  225.0 9.6 %convert_reduce_fusion = (f32[2048]{0:T(1024)S(1)}, bf16[1024,2048]{1,0:T(8,128)(2,1)S(1)}) fusion(f32[1024,2048]{1,0:T(8,128)} %get-tuple-element.290, f32[2048]{0:T(1024)S(1)} %bitcast.109, bf16[1024,1024]{1,0:T(8,128)(2,1)S(1)} %copy-done.24, bf16[1024,2048]{1,0:T(8,128)(2,1)S(1)} %copy-done.17), kind=kOutput, calls=%fused_computation.6 | convolution fusion | flops 4326422528 | bytes 18890752 | tf_op jit(solution)/shard_map/dot_general | solution.py:755
  253.3 6.4 %convolution_convert_fusion.1.refs_1_ = bf16[1024,2048]{1,0:T(8,128)(2,1)} fusion(bf16[1024,1024]{1,0:T(8,128)(2,1)S(1)} %copy-done.23, bf16[1024,2048]{1,0:T(8,128)(2,1)S(1)} %get-tuple-element.292), kind=kOutput, calls=%fused_computation.11 | convolution fusion | flops 4297064448 | bytes 10485760 | tf_op jit(solution)/shard_map/dot_general | solution.py:46
  271.1 5.5 %deal.4 = (bf16[2,128,2560]{2,1,0:T(8,128)(2,1)}, bf16[2,128,2560]{2,1,0:T(8,128)(2,1)}, bf16[2,128,2560]{2,1,0:T(8,128)(2,1)}, bf16[2,128,2560]{2,1,0:T(8,128)(2,1)}) custom-call(s32[1]{0:T(128)} %bitcast.7.place_ref, bf16[1024,512]{1,0:T(8,128)(2,1)} %convolution_convert_fusion.3.refs_0_, bf16[1024,2048]{1,0:T(8,128)(2,1)} %convolution_convert_fusion.1.refs_1_), custom_call_target="tpu_custom_call" | custom-call | bytes 16777216 | tf_op jit(solution)/shard_map/deal/pallas_call | solution.py:530
  277.9 25.8 %attend_back.1 = (bf16[1024,1536]{1,0:T(8,128)(2,1)}, f32[1,1536]{1,0:T(1,128)}) custom-call(bf16[1024,1536]{1,0:T(8,128)(2,1)} %get-tuple-element.103.qkv_ref, bf16[1024,512]{1,0:T(8,128)(2,1)} %convolution_convert_fusion.4.grad_ref, f32[4,128,1024]{2,1,0:T(8,128)} %get-tuple-element.119.turned_ref, f32[4,2,1024]{2,1,0:T(2,128)} %get-tuple-element.120.log_ref, ...), custom_call_target="tpu_custom_call" | custom-call | flops 27000000512 | bytes 16777216 | tf_op jit(solution)/shard_map/attend_back/pallas_call | solution.py:457
  317.2 5.0 %convolution_convert_fusion.refs_0_ = bf16[1024,1536]{1,0:T(8,128)(2,1)} fusion(bf16[1024,1024]{1,0:T(8,128)(2,1)S(1)} %copy-done.21, bf16[1024,1536]{1,0:T(8,128)(2,1)S(1)} %copy-done.71), kind=kOutput, calls=%fused_computation.10 | convolution fusion | flops 3222798336 | bytes 8388608 | tf_op jit(solution)/shard_map/dot_general | solution.py:46
  333.1 6.3 %fusion.84 = f32[1024,1024]{1,0:T(8,128)S(1)} fusion(bf16[1024,1536]{1,0:T(8,128)(2,1)} %get-tuple-element.133, bf16[1024,1536]{1,0:T(8,128)(2,1)} %assemble.3.weight_ref), kind=kOutput, calls=%fused_computation.288 | convolution fusion | flops 3221225472 | bytes 10485760 | tf_op jit(solution)/shard_map/dot_general | solution.py:46
  339.6 4.9 %collective-permute-start.43 = (bf16[512,1024]{1,0:T(8,128)(2,1)S(1)}, bf16[512,1024]{1,0:T(8,128)(2,1)S(1)}, u32[]{:S(2)}, u32[]{:S(2)}) collective-permute-start(bf16[512,1024]{1,0:T(8,128)(2,1)S(1)} %select_convert_fusion), channel_id=1, source_target_pairs={{0,4},{4,0},{1,5},{5,1},{2,6},{6,2},{3,7},{7,3},{8,12},{12,8},{9,1... | collective-permute-start | bytes 3145736 | tf_op jit(solution)/shard_map/ppermute | solution.py:556
  360.0 9.0 %collective-permute-done.49 = f32[13312]{0:T(1024)S(1)} collective-permute-done((f32[13312]{0:T(1024)S(1)}, f32[13312]{0:T(1024)S(1)}, u32[]{:S(2)}, u32[]{:S(2)}) %collective-permute-start.49) | collective-permute-done | bytes 53280 | tf_op jit(solution)/shard_map/ppermute | solution.py:556
  376.0 15.6 %collective-permute-done.44 = bf16[256,1024]{1,0:T(8,128)(2,1)S(1)} collective-permute-done((bf16[256,1024]{1,0:T(8,128)(2,1)S(1)}, bf16[256,1024]{1,0:T(8,128)(2,1)S(1)}, u32[]{:S(2)}, u32[]{:S(2)}) %collective-permute-start.44) | collective-permute-done | bytes 524320 | tf_op jit(solution)/shard_map/ppermute | solution.py:594
  391.5 7.3 %collective-permute-done.45 = bf16[256,1024]{1,0:T(8,128)(2,1)S(1)} collective-permute-done((bf16[256,1024]{1,0:T(8,128)(2,1)S(1)}, bf16[256,1024]{1,0:T(8,128)(2,1)S(1)}, u32[]{:S(2)}, u32[]{:S(2)}) %collective-permute-start.45) | collective-permute-done | bytes 524320 | tf_op jit(solution)/shard_map/ppermute | solution.py:594
  416.0 6.2 %collective-permute-done.57 = bf16[256,384]{1,0:T(8,128)(2,1)S(1)} collective-permute-done((bf16[256,384]{1,0:T(8,128)(2,1)S(1)}, bf16[256,384]{1,0:T(8,128)(2,1)S(1)}, u32[]{:S(2)}, u32[]{:S(2)}) %collective-permute-start.57) | collective-permute-done | bytes 196640 | tf_op jit(solution)/shard_map/ppermute | solution.py:556
  (465 shorter events, 200.5 us)
Async XLA Ops:
  29.7 33.1 %collective-permute-start.5 = (bf16[256,1024]{1,0:T(8,128)(2,1)S(1)}, bf16[256,1024]{1,0:T(8,128)(2,1)S(1)}, u32[]{:S(2)}, u32[]{:S(2)}) collective-permute-start(bf16[256,1024]{1,0:T(8,128)(2,1)S(1)} %get-tuple-element.244), channel_id=1, source_target_pairs={{0,0},{1,1},{2,4},{3,5},{4,2},{5,3},{6,6},{7,7},{8,8},{9,9},{10,12... | collective-permute-start | bytes 1572872 | tf_op jit(solution)/shard_map/ppermute | solution.py:582
  32.0 33.1 %collective-permute-start.10 = (bf16[256,640]{1,0:T(8,128)(2,1)S(1)}, bf16[256,640]{1,0:T(8,128)(2,1)}, u32[]{:S(2)}, u32[]{:S(2)}) collective-permute-start(bf16[256,640]{1,0:T(8,128)(2,1)S(1)} %pad_maximum_fusion.17), channel_id=1, source_target_pairs={{0,2},{1,3},{2,0},{3,1},{4,6},{5,7},{6,4},{7,5},{8,10},{9,11},{10,... | collective-permute-start | bytes 983048 | tf_op jit(solution)/shard_map/ppermute | solution.py:556
  32.1 33.0 %collective-permute-start.9 = (bf16[256,640]{1,0:T(8,128)(2,1)S(1)}, bf16[256,640]{1,0:T(8,128)(2,1)S(1)}, u32[]{:S(2)}, u32[]{:S(2)}) collective-permute-start(bf16[256,640]{1,0:T(8,128)(2,1)S(1)} %pad_maximum_fusion.17), channel_id=1, source_target_pairs={{0,1},{1,0},{2,3},{3,2},{4,5},{5,4},{6,7},{7,6},{8,9},{9,8},{10,11... | collective-permute-start | bytes 983048 | tf_op jit(solution)/shard_map/ppermute | solution.py:556
  32.6 32.5 %collective-permute-start.8 = (bf16[256,1536]{1,0:T(8,128)(2,1)S(1)}, bf16[256,1536]{1,0:T(8,128)(2,1)S(1)}, u32[]{:S(2)}, u32[]{:S(2)}) collective-permute-start(bf16[256,1536]{1,0:T(8,128)(2,1)S(1)} %pad_maximum_fusion.10.own_ref), channel_id=1, source_target_pairs={{0,16},{16,0},{1,17},{17,1},{2,18},{18,2},{3,19},{19,3},{4,20},{20... | collective-permute-start | bytes 2359304 | tf_op jit(solution)/shard_map/ppermute | solution.py:556
  42.2 22.9 %collective-permute-start.7 = (bf16[256,1536]{1,0:T(8,128)(2,1)S(1)}, bf16[256,1536]{1,0:T(8,128)(2,1)S(1)}, u32[]{:S(2)}, u32[]{:S(2)}) collective-permute-start(bf16[256,1536]{1,0:T(8,128)(2,1)S(1)} %pad_maximum_fusion.10.own_ref), channel_id=1, source_target_pairs={{0,8},{8,0},{1,9},{9,1},{2,10},{10,2},{3,11},{11,3},{4,12},{12,4},... | collective-permute-start | bytes 2359304 | tf_op jit(solution)/shard_map/ppermute | solution.py:556
  64.0 30.7 %collective-permute-start.6 = (bf16[512,1024]{1,0:T(8,128)(2,1)S(1)}, bf16[512,1024]{1,0:T(8,128)(2,1)}, u32[]{:S(2)}, u32[]{:S(2)}) collective-permute-start(bf16[512,1024]{1,0:T(8,128)(2,1)S(1)} %fusion.12), channel_id=1, source_target_pairs={{0,4},{4,0},{1,5},{5,1},{2,6},{6,2},{3,7},{7,3},{8,12},{12,8},{9,1... | collective-permute-start | bytes 3145736 | tf_op jit(solution)/shard_map/ppermute | solution.py:556
  89.6 29.3 %collective-permute-start.17 = (bf16[256,2560]{1,0:T(8,128)(2,1)}, bf16[256,2560]{1,0:T(8,128)(2,1)}, u32[]{:S(2)}, u32[]{:S(2)}) collective-permute-start(bf16[256,2560]{1,0:T(8,128)(2,1)} %constant_dynamic-update-slice_fusion.own_ref), channel_id=1, source_target_pairs={{0,16},{16,0},{1,17},{17,1},{2,18},{18,2},{3,19},{19,3},{4,20},{20... | collective-permute-start | bytes 3932168 | tf_op jit(solution)/shard_map/ppermute | solution.py:556
  89.9 29.0 %collective-permute-start.16 = (bf16[256,2560]{1,0:T(8,128)(2,1)}, bf16[256,2560]{1,0:T(8,128)(2,1)}, u32[]{:S(2)}, u32[]{:S(2)}) collective-permute-start(bf16[256,2560]{1,0:T(8,128)(2,1)} %constant_dynamic-update-slice_fusion.own_ref), channel_id=1, source_target_pairs={{0,8},{8,0},{1,9},{9,1},{2,10},{10,2},{3,11},{11,3},{4,12},{12,4},... | collective-permute-start | bytes 3932168 | tf_op jit(solution)/shard_map/ppermute | solution.py:556
  134.2 23.0 %collective-permute-start.25 = (bf16[256,1024]{1,0:T(8,128)(2,1)}, bf16[256,1024]{1,0:T(8,128)(2,1)}, u32[]{:S(2)}, u32[]{:S(2)}) collective-permute-start(bf16[256,1024]{1,0:T(8,128)(2,1)} %get-tuple-element.240), channel_id=1, source_target_pairs={{0,0},{1,1},{2,4},{3,5},{4,2},{5,3},{6,6},{7,7},{8,8},{9,9},{10,12... | collective-permute-start | bytes 1572872 | tf_op jit(solution)/shard_map/ppermute | solution.py:582
  162.3 24.4 %collective-permute-start.24 = (bf16[256,2048]{1,0:T(8,128)(2,1)S(1)}, bf16[256,2048]{1,0:T(8,128)(2,1)S(1)}, u32[]{:S(2)}, u32[]{:S(2)}) collective-permute-start(bf16[256,2048]{1,0:T(8,128)(2,1)S(1)} %constant_dynamic-update-slice_fusion.4.own_ref), channel_id=1, source_target_pairs={{0,16},{16,0},{1,17},{17,1},{2,18},{18,2},{3,19},{19,3},{4,20},{20... | collective-permute-start | bytes 3145736 | tf_op jit(solution)/shard_map/ppermute | solution.py:556
  163.5 24.1 %collective-permute-start.23 = (bf16[256,2048]{1,0:T(8,128)(2,1)S(1)}, bf16[256,2048]{1,0:T(8,128)(2,1)S(1)}, u32[]{:S(2)}, u32[]{:S(2)}) collective-permute-start(bf16[256,2048]{1,0:T(8,128)(2,1)S(1)} %constant_dynamic-update-slice_fusion.4.own_ref), channel_id=1, source_target_pairs={{0,8},{8,0},{1,9},{9,1},{2,10},{10,2},{3,11},{11,3},{4,12},{12,4},... | collective-permute-start | bytes 3145736 | tf_op jit(solution)/shard_map/ppermute | solution.py:556
  189.3 23.2 %collective-permute-start.27 = (bf16[128,2048]{1,0:T(8,128)(2,1)}, bf16[128,2048]{1,0:T(8,128)(2,1)}, u32[]{:S(2)}, u32[]{:S(2)}) collective-permute-start(bf16[128,2048]{1,0:T(8,128)(2,1)} %slice.387), channel_id=1, source_target_pairs={{0,8},{8,0},{1,9},{9,1},{2,10},{10,2},{3,11},{11,3},{4,12},{12,4},... | collective-permute-start | bytes 1572872 | tf_op jit(solution)/shard_map/ppermute | solution.py:556
  211.3 31.1 %collective-permute-start.35 = (bf16[2,128,2048]{2,1,0:T(8,128)(2,1)}, bf16[2,128,2048]{2,1,0:T(8,128)(2,1)}, u32[]{:S(2)}, u32[]{:S(2)}) collective-permute-start(bf16[2,128,2048]{2,1,0:T(8,128)(2,1)} %get-tuple-element.105), channel_id=1, source_target_pairs={{0,16},{16,0},{1,17},{17,1},{2,18},{18,2},{3,19},{19,3},{4,20},{20... | collective-permute-start | bytes 3145736 | tf_op jit(solution)/shard_map/ppermute | solution.py:556
  212.2 30.2 %collective-permute-start.36 = (bf16[2,128,2048]{2,1,0:T(8,128)(2,1)}, bf16[2,128,2048]{2,1,0:T(8,128)(2,1)}, u32[]{:S(2)}, u32[]{:S(2)}) collective-permute-start(bf16[2,128,2048]{2,1,0:T(8,128)(2,1)} %get-tuple-element.107), channel_id=1, source_target_pairs={{0,8},{8,0},{1,9},{9,1},{2,10},{10,2},{3,11},{11,3},{4,12},{12,4},... | collective-permute-start | bytes 3145736 | tf_op jit(solution)/shard_map/ppermute | solution.py:556
  246.2 24.9 %collective-permute-start.37 = (bf16[128,2048]{1,0:T(8,128)(2,1)S(1)}, bf16[128,2048]{1,0:T(8,128)(2,1)}, u32[]{:S(2)}, u32[]{:S(2)}) collective-permute-start(bf16[128,2048]{1,0:T(8,128)(2,1)S(1)} %slice_bitcast_fusion.7), channel_id=1, source_target_pairs={{0,8},{8,0},{1,9},{9,1},{2,10},{10,2},{3,11},{11,3},{4,12},{12,4},... | collective-permute-start | bytes 1572872 | tf_op jit(solution)/shard_map/ppermute | solution.py:556
  247.6 23.5 %collective-permute-start.38 = (bf16[128,2048]{1,0:T(8,128)(2,1)S(1)}, bf16[128,2048]{1,0:T(8,128)(2,1)}, u32[]{:S(2)}, u32[]{:S(2)}) collective-permute-start(bf16[128,2048]{1,0:T(8,128)(2,1)S(1)} %slice_bitcast_fusion.6), channel_id=1, source_target_pairs={{0,16},{16,0},{1,17},{17,1},{2,18},{18,2},{3,19},{19,3},{4,20},{20... | collective-permute-start | bytes 1572872 | tf_op jit(solution)/shard_map/ppermute | solution.py:556
  260.7 44.4 %collective-permute-start.31 = (bf16[256,1024]{1,0:T(8,128)(2,1)}, bf16[256,1024]{1,0:T(8,128)(2,1)S(1)}, u32[]{:S(2)}, u32[]{:S(2)}) collective-permute-start(bf16[256,1024]{1,0:T(8,128)(2,1)} %get-tuple-element.237), channel_id=1, source_target_pairs={{1,0},{0,1},{5,2},{4,3},{3,4},{2,5},{7,6},{6,7},{9,8},{8,9},{13,10... | collective-permute-start | bytes 1572872 | tf_op jit(solution)/shard_map/ppermute | solution.py:594
  264.2 40.9 %collective-permute-start.30 = (bf16[256,1024]{1,0:T(8,128)(2,1)}, bf16[256,1024]{1,0:T(8,128)(2,1)}, u32[]{:S(2)}, u32[]{:S(2)}) collective-permute-start(bf16[256,1024]{1,0:T(8,128)(2,1)} %get-tuple-element.238), channel_id=1, source_target_pairs={{0,0},{1,1},{4,2},{5,3},{2,4},{3,5},{6,6},{7,7},{8,8},{9,9},{12,10... | collective-permute-start | bytes 1572872 | tf_op jit(solution)/shard_map/ppermute | solution.py:594
  276.6 33.8 %collective-permute-start.39 = (bf16[2,128,2560]{2,1,0:T(8,128)(2,1)}, bf16[2,128,2560]{2,1,0:T(8,128)(2,1)}, u32[]{:S(2)}, u32[]{:S(2)}) collective-permute-start(bf16[2,128,2560]{2,1,0:T(8,128)(2,1)} %get-tuple-element.112), channel_id=1, source_target_pairs={{0,16},{16,0},{1,17},{17,1},{2,18},{18,2},{3,19},{19,3},{4,20},{20... | collective-permute-start | bytes 3932168 | tf_op jit(solution)/shard_map/ppermute | solution.py:556
  277.7 32.7 %collective-permute-start.40 = (bf16[2,128,2560]{2,1,0:T(8,128)(2,1)}, bf16[2,128,2560]{2,1,0:T(8,128)(2,1)}, u32[]{:S(2)}, u32[]{:S(2)}) collective-permute-start(bf16[2,128,2560]{2,1,0:T(8,128)(2,1)} %get-tuple-element.114), channel_id=1, source_target_pairs={{0,8},{8,0},{1,9},{9,1},{2,10},{10,2},{3,11},{11,3},{4,12},{12,4},... | collective-permute-start | bytes 3932168 | tf_op jit(solution)/shard_map/ppermute | solution.py:556
  358.9 41.5 %collective-permute-start.61 = (bf16[256,640]{1,0:T(8,128)(2,1)S(1)}, bf16[256,640]{1,0:T(8,128)(2,1)S(1)}, u32[]{:S(2)}, u32[]{:S(2)}) collective-permute-start(bf16[256,640]{1,0:T(8,128)(2,1)S(1)} %get-tuple-element.223), channel_id=1, source_target_pairs={{0,2},{1,3},{2,0},{3,1},{4,6},{5,7},{6,4},{7,5},{8,10},{9,11},{10,... | collective-permute-start | bytes 983048 | tf_op jit(solution)/shard_map/ppermute | solution.py:556
  369.0 31.3 %collective-permute-start.59 = (bf16[256,640]{1,0:T(8,128)(2,1)S(1)}, bf16[256,640]{1,0:T(8,128)(2,1)S(1)}, u32[]{:S(2)}, u32[]{:S(2)}) collective-permute-start(bf16[256,640]{1,0:T(8,128)(2,1)S(1)} %get-tuple-element.224), channel_id=1, source_target_pairs={{0,1},{1,0},{2,3},{3,2},{4,5},{5,4},{6,7},{7,6},{8,9},{9,8},{10,11... | collective-permute-start | bytes 983048 | tf_op jit(solution)/shard_map/ppermute | solution.py:556
  372.9 25.9 %collective-permute-start.45 = (bf16[256,1024]{1,0:T(8,128)(2,1)S(1)}, bf16[256,1024]{1,0:T(8,128)(2,1)S(1)}, u32[]{:S(2)}, u32[]{:S(2)}) collective-permute-start(bf16[256,1024]{1,0:T(8,128)(2,1)S(1)} %get-tuple-element.232), channel_id=1, source_target_pairs={{0,0},{1,1},{4,2},{5,3},{2,4},{3,5},{6,6},{7,7},{8,8},{9,9},{12,10... | collective-permute-start | bytes 1572872 | tf_op jit(solution)/shard_map/ppermute | solution.py:594
  375.3 33.4 %collective-permute-start.56 = (bf16[256,384]{1,0:T(8,128)(2,1)S(1)}, bf16[256,384]{1,0:T(8,128)(2,1)S(1)}, u32[]{:S(2)}, u32[]{:S(2)}) collective-permute-start(bf16[256,384]{1,0:T(8,128)(2,1)S(1)} %pad_maximum_fusion.20), channel_id=1, source_target_pairs={{0,1},{1,0},{2,3},{3,2},{4,5},{5,4},{6,7},{7,6},{8,9},{9,8},{10,11... | collective-permute-start | bytes 589832 | tf_op jit(solution)/shard_map/ppermute | solution.py:556
  (118 other events, 957.4 us)

commit v5 on v4

--- a/solution.py
+++ b/solution.py
@@ -766,8 +766,8 @@
     grad_fc1 = contract(after(second_all, sent_fc2[0]), grad_hidden, 0, 0)
     parts_up = dealt(contract(resid_all, heads_out, 0, 0), grad_fc1)
     grad_heads = jnp.dot(resid_all, weight_out, preferred_element_type=jnp.float32).astype(low)
-    total_fc2, came_fc2 = second_back(*sent_fc2, grad_heads)
-    grad_packed, sum_qkv_bias = attend_back(qkv, after(grad_heads, (parts_up, came_fc2)), turned, log_total, cosine, sine)
+    total_fc2, _ = second_back(*sent_fc2, grad_heads)
+    grad_packed, sum_qkv_bias = attend_back(qkv, after(grad_heads, parts_up), turned, log_total, cosine, sine)
     output = from_clips(result.astype(low), grad_packed)
     sent_up = first_back(parts_up, grad_packed)
     parts_qkv = dealt(contract(after(first_all, sent_up), grad_packed, 0, 0))

time: 434 us -> 456 us (1.051)
  waiting for transfers between devices: 115 us -> 135 us
    ppermute x59, waiting for transfers between devices: 58.1 us -> 78.8 us  [swap(): lax.ppermute(values, axis, [(i, i ^ bit) for i in range(4 if axis == 'ten...]
  transfers between devices with their start and end apart: 67 -> 67, of which waited for: 18 -> 19; matrix products, arithmetic and copies ran while one was open for 28% -> 27% of each run, Pallas kernels for 18% -> 17%
where the time goes in v5:
time: 456 us; the launch traced here: 450 us
  waiting for transfers between devices  135 us (30%)
  starting transfers between devices  96.3 us (21%)
  Pallas kernels  75.6 us (17%)
  matrix products  60.3 us (13%)
  other arithmetic  46 us (10%)
  local copies, waits for them, and re-layouts  33.9 us (7%)
    ppermute x59, waiting for transfers between devices, swap(): lax.ppermute(values, axis, [(i, i ^ bit) for i in range(4 if axis == 'ten...  78.8 us
    ppermute x59, starting transfers between devices, swap(): lax.ppermute(values, axis, [(i, i ^ bit) for i in range(4 if axis == 'ten...  69.9 us
    dot_general x8, matrix products, contract(): lax.dot_general(left, right, (((left_dim,), (right_dim,)), ((), ())), pre...  41.2 us
    ppermute x4, waiting for transfers between devices, to_clips(): arrived.append(lax.ppermute(sent, EVERY, pairs))  33.8 us
    pallas_call x1, Pallas kernels, attend_back(): pl.pallas_call(attend_back_kernel, grid=(pairs,), in_specs=[pl.BlockSpec(...  25.8 us
    ppermute x4, waiting for transfers between devices, from_clips(): arrived.append(lax.ppermute(sent, EVERY, pairs))  22.3 us
    pallas_call x1, Pallas kernels, attend(): pl.pallas_call(attend_kernel, grid=(pairs,), in_specs=[pl.BlockSpec((leng...  20.4 us
    unnamed x166, local copies, waits for them, and re-layouts  18.6 us
  transfers between devices with their start and end apart: 67, of which 19 were waited for; matrix products, arithmetic and copies ran while one was open for 27% of the time, Pallas kernels for 17%

profile of v5, /device:TPU:1, one launch (start us, length us, event | category | flops | bytes accessed | tf_op | source)
XLA Modules:
  0.0 449.9 jit_solution(3499476637576397036)
XLA Ops:
  11.1 7.2 %collective-permute-done.2 = bf16[272,384]{1,0:T(8,128)(2,1)S(1)} collective-permute-done((bf16[272,384]{1,0:T(8,128)(2,1)S(1)}, bf16[272,384]{1,0:T(8,128)(2,1)S(1)}, u32[]{:S(2)}, u32[]{:S(2)}) %collective-permute-start.2) | collective-permute-done | bytes 208928 | tf_op jit(solution)/shard_map/ppermute | solution.py:556
  24.1 5.5 %collective-permute-start.4 = (bf16[256,1024]{1,0:T(8,128)(2,1)S(1)}, bf16[256,1024]{1,0:T(8,128)(2,1)S(1)}, u32[]{:S(2)}, u32[]{:S(2)}) collective-permute-start(bf16[256,1024]{1,0:T(8,128)(2,1)S(1)} %get-tuple-element.243), channel_id=1, source_target_pairs={{0,1},{1,0},{2,5},{3,4},{4,3},{5,2},{6,7},{7,6},{8,9},{9,8},{10,13... | collective-permute-start | bytes 1572872 | tf_op jit(solution)/shard_map/ppermute | solution.py:582
  33.9 8.4 %collective-permute-done.4 = bf16[256,1024]{1,0:T(8,128)(2,1)S(1)} collective-permute-done((bf16[256,1024]{1,0:T(8,128)(2,1)S(1)}, bf16[256,1024]{1,0:T(8,128)(2,1)S(1)}, u32[]{:S(2)}, u32[]{:S(2)}) %collective-permute-start.4) | collective-permute-done | bytes 524320 | tf_op jit(solution)/shard_map/ppermute | solution.py:582
  43.5 19.3 %collective-permute-done.5 = bf16[256,1024]{1,0:T(8,128)(2,1)S(1)} collective-permute-done((bf16[256,1024]{1,0:T(8,128)(2,1)S(1)}, bf16[256,1024]{1,0:T(8,128)(2,1)S(1)}, u32[]{:S(2)}, u32[]{:S(2)}) %collective-permute-start.5) | collective-permute-done | bytes 524320 | tf_op jit(solution)/shard_map/ppermute | solution.py:582
  77.4 5.0 %collective-permute-start.15 = (bf16[256,512]{1,0:T(8,128)(2,1)S(1)}, bf16[256,512]{1,0:T(8,128)(2,1)S(1)}, u32[]{:S(2)}, u32[]{:S(2)}) collective-permute-start(bf16[256,512]{1,0:T(8,128)(2,1)S(1)} %pad_maximum_fusion.19), channel_id=1, source_target_pairs={{0,2},{1,3},{2,0},{3,1},{4,6},{5,7},{6,4},{7,5},{8,10},{9,11},{10,... | collective-permute-start | bytes 786440 | tf_op jit(solution)/shard_map/ppermute | solution.py:556
  97.7 20.4 %attend.1 = (bf16[1024,1536]{1,0:T(8,128)(2,1)}, bf16[1024,512]{1,0:T(8,128)(2,1)}, f32[4,128,1024]{2,1,0:T(8,128)}, f32[4,2,1024]{2,1,0:T(2,128)}) custom-call(bf16[1024,1024]{1,0:T(8,128)(2,1)} %pad_maximum_fusion.first_ref, bf16[1024,1536]{1,0:T(8,128)(2,1)} %assemble.3.weight_ref, f32[1,1536]{1,0:T(1,128)} %bitcast.110, ...), custom_call_target="tpu_custom_call" | custom-call | flops 20000000000 | bytes 16777216 | tf_op jit(solution)/shard_map/attend/pallas_call | solution.py:389
  123.3 5.3 %collective-permute-done.20 = bf16[256,512]{1,0:T(8,128)(2,1)S(1)} collective-permute-done((bf16[256,512]{1,0:T(8,128)(2,1)S(1)}, bf16[256,512]{1,0:T(8,128)(2,1)S(1)}, u32[]{:S(2)}, u32[]{:S(2)}) %collective-permute-start.20) | collective-permute-done | bytes 262176 | tf_op jit(solution)/shard_map/ppermute | solution.py:556
  137.5 5.4 %assemble.4 = (bf16[1024,512]{1,0:T(8,128)(2,1)}, bf16[1024,2048]{1,0:T(8,128)(2,1)}) custom-call(s32[1]{0:T(128)} %bitcast.7.place_ref, bf16[256,2560]{1,0:T(8,128)(2,1)} %constant_dynamic-update-slice_fusion.own_ref, bf16[256,2560]{1,0:T(8,128)(2,1)} %collective-permute-done.16.x_ref, bf16[256,2560]{1,0:T(8,128)(2,1)} %collective-permute-done.17.y_ref, ...), custom_call_target="tpu_custom_call" | custom-call | bytes 16777216 | tf_op jit(solution)/shard_map/assemble/pallas_call | solution.py:497
  151.0 6.1 %collective-permute-done.25 = bf16[256,1024]{1,0:T(8,128)(2,1)} collective-permute-done((bf16[256,1024]{1,0:T(8,128)(2,1)}, bf16[256,1024]{1,0:T(8,128)(2,1)}, u32[]{:S(2)}, u32[]{:S(2)}) %collective-permute-start.25) | collective-permute-done | bytes 524320 | tf_op jit(solution)/shard_map/ppermute | solution.py:582
  167.6 19.1 %collective-permute-done.24.y_ref = bf16[256,2048]{1,0:T(8,128)(2,1)S(1)} collective-permute-done((bf16[256,2048]{1,0:T(8,128)(2,1)S(1)}, bf16[256,2048]{1,0:T(8,128)(2,1)S(1)}, u32[]{:S(2)}, u32[]{:S(2)}) %collective-permute-start.24) | collective-permute-done | bytes 1048608 | tf_op jit(solution)/shard_map/ppermute | solution.py:556
  191.0 7.2 %multiply_convert_fusion.1 = (bf16[1024,2048]{1,0:T(8,128)(2,1)S(1)}, f32[1024,2048]{1,0:T(8,128)}) fusion(f32[2048]{0:T(1024)S(1)} %bitcast.108, bf16[1024,1024]{1,0:T(8,128)(2,1)S(1)} %pad_maximum_fusion.1, bf16[1024,2048]{1,0:T(8,128)(2,1)S(1)} %copy-done.67), kind=kOutput, calls=%fused_computation.8 | convolution fusion | flops 4307550208 | bytes 18882560 | tf_op jit(solution)/shard_map/dot_general | solution.py:716
  200.2 6.2 %convolution_convert_fusion.2.refs_0_ = bf16[1024,2048]{1,0:T(8,128)(2,1)} fusion(bf16[1024,2048]{1,0:T(8,128)(2,1)S(1)} %get-tuple-element.289, bf16[512,1024]{1,0:T(8,128)(2,1)S(1)} %get-tuple-element.218, bf16[512,1024]{1,0:T(8,128)(2,1)S(1)} %get-tuple-element.217), kind=kOutput, calls=%fused_computation.12 | convolution fusion | flops 4301258752 | bytes 10485760 | tf_op jit(solution)/shard_map/dot_general | solution.py:46
  217.2 7.7 %fusion.82 = f32[1024,1024]{1,0:T(8,128)S(1)} fusion(bf16[1024,2048]{1,0:T(8,128)(2,1)} %copy-done.72, bf16[1024,2048]{1,0:T(8,128)(2,1)} %assemble.5), kind=kOutput, calls=%fused_computation.286 | convolution fusion | flops 4294967296 | bytes 12582912 | tf_op jit(solution)/shard_map/dot_general | solution.py:46
  225.0 9.6 %convert_reduce_fusion = (f32[2048]{0:T(1024)S(1)}, bf16[1024,2048]{1,0:T(8,128)(2,1)S(1)}) fusion(f32[1024,2048]{1,0:T(8,128)} %get-tuple-element.290, f32[2048]{0:T(1024)S(1)} %bitcast.109, bf16[1024,1024]{1,0:T(8,128)(2,1)S(1)} %copy-done.24, bf16[1024,2048]{1,0:T(8,128)(2,1)S(1)} %copy-done.17), kind=kOutput, calls=%fused_computation.6 | convolution fusion | flops 4326422528 | bytes 18890752 | tf_op jit(solution)/shard_map/dot_general | solution.py:755
  254.9 6.4 %convolution_convert_fusion.1.refs_1_ = bf16[1024,2048]{1,0:T(8,128)(2,1)} fusion(bf16[1024,1024]{1,0:T(8,128)(2,1)S(1)} %copy-done.23, bf16[1024,2048]{1,0:T(8,128)(2,1)S(1)} %get-tuple-element.292), kind=kOutput, calls=%fused_computation.11 | convolution fusion | flops 4297064448 | bytes 10485760 | tf_op jit(solution)/shard_map/dot_general | solution.py:46
  272.7 5.5 %deal.4 = (bf16[2,128,2560]{2,1,0:T(8,128)(2,1)}, bf16[2,128,2560]{2,1,0:T(8,128)(2,1)}, bf16[2,128,2560]{2,1,0:T(8,128)(2,1)}, bf16[2,128,2560]{2,1,0:T(8,128)(2,1)}) custom-call(s32[1]{0:T(128)} %bitcast.7.place_ref, bf16[1024,512]{1,0:T(8,128)(2,1)} %convolution_convert_fusion.3.refs_0_, bf16[1024,2048]{1,0:T(8,128)(2,1)} %convolution_convert_fusion.1.refs_1_), custom_call_target="tpu_custom_call" | custom-call | bytes 16777216 | tf_op jit(solution)/shard_map/deal/pallas_call | solution.py:530
  279.2 25.8 %attend_back.1 = (bf16[1024,1536]{1,0:T(8,128)(2,1)}, f32[1,1536]{1,0:T(1,128)}) custom-call(bf16[1024,1536]{1,0:T(8,128)(2,1)} %get-tuple-element.103.qkv_ref, bf16[1024,512]{1,0:T(8,128)(2,1)} %convolution_convert_fusion.4.grad_ref, f32[4,128,1024]{2,1,0:T(8,128)} %get-tuple-element.116.turned_ref, f32[4,2,1024]{2,1,0:T(2,128)} %get-tuple-element.117.log_ref, ...), custom_call_target="tpu_custom_call" | custom-call | flops 27000000512 | bytes 16777216 | tf_op jit(solution)/shard_map/attend_back/pallas_call | solution.py:457
  312.0 22.5 %collective-permute-done.38 = bf16[2,128,2560]{2,1,0:T(8,128)(2,1)S(1)} collective-permute-done((bf16[2,128,2560]{2,1,0:T(8,128)(2,1)}, bf16[2,128,2560]{2,1,0:T(8,128)(2,1)S(1)}, u32[]{:S(2)}, u32[]{:S(2)}) %collective-permute-start.38) | collective-permute-done | bytes 1310752 | tf_op jit(solution)/shard_map/ppermute | solution.py:556
  339.7 5.0 %convolution_convert_fusion.refs_0_ = bf16[1024,1536]{1,0:T(8,128)(2,1)} fusion(bf16[1024,1024]{1,0:T(8,128)(2,1)S(1)} %copy-done.21, bf16[1024,1536]{1,0:T(8,128)(2,1)S(1)} %copy-done.71), kind=kOutput, calls=%fused_computation.10 | convolution fusion | flops 3222798336 | bytes 8388608 | tf_op jit(solution)/shard_map/dot_general | solution.py:46
  355.1 6.3 %fusion.84 = f32[1024,1024]{1,0:T(8,128)S(1)} fusion(bf16[1024,1536]{1,0:T(8,128)(2,1)} %get-tuple-element.130, bf16[1024,1536]{1,0:T(8,128)(2,1)} %assemble.3.weight_ref), kind=kOutput, calls=%fused_computation.288 | convolution fusion | flops 3221225472 | bytes 10485760 | tf_op jit(solution)/shard_map/dot_general | solution.py:46
  382.5 6.4 %collective-permute-done.47 = f32[13312]{0:T(1024)S(1)} collective-permute-done((f32[13312]{0:T(1024)S(1)}, f32[13312]{0:T(1024)S(1)}, u32[]{:S(2)}, u32[]{:S(2)}) %collective-permute-start.47) | collective-permute-done | bytes 53280 | tf_op jit(solution)/shard_map/ppermute | solution.py:556
  397.9 16.2 %collective-permute-done.42 = bf16[256,1024]{1,0:T(8,128)(2,1)S(1)} collective-permute-done((bf16[256,1024]{1,0:T(8,128)(2,1)S(1)}, bf16[256,1024]{1,0:T(8,128)(2,1)S(1)}, u32[]{:S(2)}, u32[]{:S(2)}) %collective-permute-start.42) | collective-permute-done | bytes 524320 | tf_op jit(solution)/shard_map/ppermute | solution.py:594
  414.0 6.2 %collective-permute-done.43 = bf16[256,1024]{1,0:T(8,128)(2,1)S(1)} collective-permute-done((bf16[256,1024]{1,0:T(8,128)(2,1)S(1)}, bf16[256,1024]{1,0:T(8,128)(2,1)S(1)}, u32[]{:S(2)}, u32[]{:S(2)}) %collective-permute-start.43) | collective-permute-done | bytes 524320 | tf_op jit(solution)/shard_map/ppermute | solution.py:594
  437.4 6.8 %collective-permute-done.55 = bf16[256,384]{1,0:T(8,128)(2,1)S(1)} collective-permute-done((bf16[256,384]{1,0:T(8,128)(2,1)S(1)}, bf16[256,384]{1,0:T(8,128)(2,1)S(1)}, u32[]{:S(2)}, u32[]{:S(2)}) %collective-permute-start.55) | collective-permute-done | bytes 196640 | tf_op jit(solution)/shard_map/ppermute | solution.py:556
  (465 shorter events, 207.6 us)
Async XLA Ops:
  29.7 33.1 %collective-permute-start.5 = (bf16[256,1024]{1,0:T(8,128)(2,1)S(1)}, bf16[256,1024]{1,0:T(8,128)(2,1)S(1)}, u32[]{:S(2)}, u32[]{:S(2)}) collective-permute-start(bf16[256,1024]{1,0:T(8,128)(2,1)S(1)} %get-tuple-element.244), channel_id=1, source_target_pairs={{0,0},{1,1},{2,4},{3,5},{4,2},{5,3},{6,6},{7,7},{8,8},{9,9},{10,12... | collective-permute-start | bytes 1572872 | tf_op jit(solution)/shard_map/ppermute | solution.py:582
  32.0 33.1 %collective-permute-start.10 = (bf16[256,640]{1,0:T(8,128)(2,1)S(1)}, bf16[256,640]{1,0:T(8,128)(2,1)}, u32[]{:S(2)}, u32[]{:S(2)}) collective-permute-start(bf16[256,640]{1,0:T(8,128)(2,1)S(1)} %pad_maximum_fusion.17), channel_id=1, source_target_pairs={{0,2},{1,3},{2,0},{3,1},{4,6},{5,7},{6,4},{7,5},{8,10},{9,11},{10,... | collective-permute-start | bytes 983048 | tf_op jit(solution)/shard_map/ppermute | solution.py:556
  32.1 33.0 %collective-permute-start.9 = (bf16[256,640]{1,0:T(8,128)(2,1)S(1)}, bf16[256,640]{1,0:T(8,128)(2,1)S(1)}, u32[]{:S(2)}, u32[]{:S(2)}) collective-permute-start(bf16[256,640]{1,0:T(8,128)(2,1)S(1)} %pad_maximum_fusion.17), channel_id=1, source_target_pairs={{0,1},{1,0},{2,3},{3,2},{4,5},{5,4},{6,7},{7,6},{8,9},{9,8},{10,11... | collective-permute-start | bytes 983048 | tf_op jit(solution)/shard_map/ppermute | solution.py:556
  32.6 32.5 %collective-permute-start.8 = (bf16[256,1536]{1,0:T(8,128)(2,1)S(1)}, bf16[256,1536]{1,0:T(8,128)(2,1)S(1)}, u32[]{:S(2)}, u32[]{:S(2)}) collective-permute-start(bf16[256,1536]{1,0:T(8,128)(2,1)S(1)} %pad_maximum_fusion.10.own_ref), channel_id=1, source_target_pairs={{0,16},{16,0},{1,17},{17,1},{2,18},{18,2},{3,19},{19,3},{4,20},{20... | collective-permute-start | bytes 2359304 | tf_op jit(solution)/shard_map/ppermute | solution.py:556
  64.0 30.7 %collective-permute-start.6 = (bf16[512,1024]{1,0:T(8,128)(2,1)S(1)}, bf16[512,1024]{1,0:T(8,128)(2,1)}, u32[]{:S(2)}, u32[]{:S(2)}) collective-permute-start(bf16[512,1024]{1,0:T(8,128)(2,1)S(1)} %fusion.12), channel_id=1, source_target_pairs={{0,4},{4,0},{1,5},{5,1},{2,6},{6,2},{3,7},{7,3},{8,12},{12,8},{9,1... | collective-permute-start | bytes 3145736 | tf_op jit(solution)/shard_map/ppermute | solution.py:556
  89.6 29.3 %collective-permute-start.17 = (bf16[256,2560]{1,0:T(8,128)(2,1)}, bf16[256,2560]{1,0:T(8,128)(2,1)}, u32[]{:S(2)}, u32[]{:S(2)}) collective-permute-start(bf16[256,2560]{1,0:T(8,128)(2,1)} %constant_dynamic-update-slice_fusion.own_ref), channel_id=1, source_target_pairs={{0,16},{16,0},{1,17},{17,1},{2,18},{18,2},{3,19},{19,3},{4,20},{20... | collective-permute-start | bytes 3932168 | tf_op jit(solution)/shard_map/ppermute | solution.py:556
  89.9 29.0 %collective-permute-start.16 = (bf16[256,2560]{1,0:T(8,128)(2,1)}, bf16[256,2560]{1,0:T(8,128)(2,1)}, u32[]{:S(2)}, u32[]{:S(2)}) collective-permute-start(bf16[256,2560]{1,0:T(8,128)(2,1)} %constant_dynamic-update-slice_fusion.own_ref), channel_id=1, source_target_pairs={{0,8},{8,0},{1,9},{9,1},{2,10},{10,2},{3,11},{11,3},{4,12},{12,4},... | collective-permute-start | bytes 3932168 | tf_op jit(solution)/shard_map/ppermute | solution.py:556
  162.3 24.4 %collective-permute-start.24 = (bf16[256,2048]{1,0:T(8,128)(2,1)S(1)}, bf16[256,2048]{1,0:T(8,128)(2,1)S(1)}, u32[]{:S(2)}, u32[]{:S(2)}) collective-permute-start(bf16[256,2048]{1,0:T(8,128)(2,1)S(1)} %constant_dynamic-update-slice_fusion.4.own_ref), channel_id=1, source_target_pairs={{0,16},{16,0},{1,17},{17,1},{2,18},{18,2},{3,19},{19,3},{4,20},{20... | collective-permute-start | bytes 3145736 | tf_op jit(solution)/shard_map/ppermute | solution.py:556
  163.5 24.1 %collective-permute-start.23 = (bf16[256,2048]{1,0:T(8,128)(2,1)S(1)}, bf16[256,2048]{1,0:T(8,128)(2,1)S(1)}, u32[]{:S(2)}, u32[]{:S(2)}) collective-permute-start(bf16[256,2048]{1,0:T(8,128)(2,1)S(1)} %constant_dynamic-update-slice_fusion.4.own_ref), channel_id=1, source_target_pairs={{0,8},{8,0},{1,9},{9,1},{2,10},{10,2},{3,11},{11,3},{4,12},{12,4},... | collective-permute-start | bytes 3145736 | tf_op jit(solution)/shard_map/ppermute | solution.py:556
  189.3 23.2 %collective-permute-start.27 = (bf16[128,2048]{1,0:T(8,128)(2,1)}, bf16[128,2048]{1,0:T(8,128)(2,1)}, u32[]{:S(2)}, u32[]{:S(2)}) collective-permute-start(bf16[128,2048]{1,0:T(8,128)(2,1)} %slice.387), channel_id=1, source_target_pairs={{0,8},{8,0},{1,9},{9,1},{2,10},{10,2},{3,11},{11,3},{4,12},{12,4},... | collective-permute-start | bytes 1572872 | tf_op jit(solution)/shard_map/ppermute | solution.py:556
  211.3 31.1 %collective-permute-start.35 = (bf16[2,128,2048]{2,1,0:T(8,128)(2,1)}, bf16[2,128,2048]{2,1,0:T(8,128)(2,1)}, u32[]{:S(2)}, u32[]{:S(2)}) collective-permute-start(bf16[2,128,2048]{2,1,0:T(8,128)(2,1)} %get-tuple-element.105), channel_id=1, source_target_pairs={{0,16},{16,0},{1,17},{17,1},{2,18},{18,2},{3,19},{19,3},{4,20},{20... | collective-permute-start | bytes 3145736 | tf_op jit(solution)/shard_map/ppermute | solution.py:556
  212.2 30.2 %collective-permute-start.36 = (bf16[2,128,2048]{2,1,0:T(8,128)(2,1)}, bf16[2,128,2048]{2,1,0:T(8,128)(2,1)}, u32[]{:S(2)}, u32[]{:S(2)}) collective-permute-start(bf16[2,128,2048]{2,1,0:T(8,128)(2,1)} %get-tuple-element.107), channel_id=1, source_target_pairs={{0,8},{8,0},{1,9},{9,1},{2,10},{10,2},{3,11},{11,3},{4,12},{12,4},... | collective-permute-start | bytes 3145736 | tf_op jit(solution)/shard_map/ppermute | solution.py:556
  247.1 58.0 %collective-permute-start.61 = (bf16[128,2048]{1,0:T(8,128)(2,1)}, bf16[128,2048]{1,0:T(8,128)(2,1)}, u32[]{:S(2)}, u32[]{:S(2)}) collective-permute-start(bf16[128,2048]{1,0:T(8,128)(2,1)} %slice_bitcast_fusion.6), channel_id=1, source_target_pairs={{0,8},{8,0},{1,9},{9,1},{2,10},{10,2},{3,11},{11,3},{4,12},{12,4},... | collective-permute-start | bytes 1572872 | tf_op jit(solution)/shard_map/ppermute | solution.py:556
  249.2 56.3 %collective-permute-start.62 = (bf16[128,2048]{1,0:T(8,128)(2,1)}, bf16[128,2048]{1,0:T(8,128)(2,1)}, u32[]{:S(2)}, u32[]{:S(2)}) collective-permute-start(bf16[128,2048]{1,0:T(8,128)(2,1)} %slice_bitcast_fusion.5), channel_id=1, source_target_pairs={{0,16},{16,0},{1,17},{17,1},{2,18},{18,2},{3,19},{19,3},{4,20},{20... | collective-permute-start | bytes 1572872 | tf_op jit(solution)/shard_map/ppermute | solution.py:556
  262.2 44.4 %collective-permute-start.31 = (bf16[256,1024]{1,0:T(8,128)(2,1)}, bf16[256,1024]{1,0:T(8,128)(2,1)S(1)}, u32[]{:S(2)}, u32[]{:S(2)}) collective-permute-start(bf16[256,1024]{1,0:T(8,128)(2,1)} %get-tuple-element.237), channel_id=1, source_target_pairs={{1,0},{0,1},{5,2},{4,3},{3,4},{2,5},{7,6},{6,7},{9,8},{8,9},{13,10... | collective-permute-start | bytes 1572872 | tf_op jit(solution)/shard_map/ppermute | solution.py:594
  265.7 41.0 %collective-permute-start.30 = (bf16[256,1024]{1,0:T(8,128)(2,1)}, bf16[256,1024]{1,0:T(8,128)(2,1)}, u32[]{:S(2)}, u32[]{:S(2)}) collective-permute-start(bf16[256,1024]{1,0:T(8,128)(2,1)} %get-tuple-element.238), channel_id=1, source_target_pairs={{0,0},{1,1},{4,2},{5,3},{2,4},{3,5},{6,6},{7,7},{8,8},{9,9},{12,10... | collective-permute-start | bytes 1572872 | tf_op jit(solution)/shard_map/ppermute | solution.py:594
  278.1 33.9 %collective-permute-start.37 = (bf16[2,128,2560]{2,1,0:T(8,128)(2,1)}, bf16[2,128,2560]{2,1,0:T(8,128)(2,1)}, u32[]{:S(2)}, u32[]{:S(2)}) collective-permute-start(bf16[2,128,2560]{2,1,0:T(8,128)(2,1)} %get-tuple-element.112), channel_id=1, source_target_pairs={{0,16},{16,0},{1,17},{17,1},{2,18},{18,2},{3,19},{19,3},{4,20},{20... | collective-permute-start | bytes 3932168 | tf_op jit(solution)/shard_map/ppermute | solution.py:556
  305.1 29.4 %collective-permute-start.38 = (bf16[2,128,2560]{2,1,0:T(8,128)(2,1)}, bf16[2,128,2560]{2,1,0:T(8,128)(2,1)S(1)}, u32[]{:S(2)}, u32[]{:S(2)}) collective-permute-start(bf16[2,128,2560]{2,1,0:T(8,128)(2,1)} %get-tuple-element.114), channel_id=1, source_target_pairs={{0,8},{8,0},{1,9},{9,1},{2,10},{10,2},{3,11},{11,3},{4,12},{12,4},... | collective-permute-start | bytes 3932168 | tf_op jit(solution)/shard_map/ppermute | solution.py:556
  309.4 40.8 %collective-permute-start.64 = (bf16[256,512]{1,0:T(8,128)(2,1)}, bf16[256,512]{1,0:T(8,128)(2,1)}, u32[]{:S(2)}, u32[]{:S(2)}) collective-permute-start(bf16[256,512]{1,0:T(8,128)(2,1)} %pad_maximum_fusion.18), channel_id=1, source_target_pairs={{0,1},{1,0},{2,3},{3,2},{4,5},{5,4},{6,7},{7,6},{8,9},{9,8},{10,11... | collective-permute-start | bytes 786440 | tf_op jit(solution)/shard_map/ppermute | solution.py:556
  379.2 42.5 %collective-permute-start.59 = (bf16[256,640]{1,0:T(8,128)(2,1)S(1)}, bf16[256,640]{1,0:T(8,128)(2,1)S(1)}, u32[]{:S(2)}, u32[]{:S(2)}) collective-permute-start(bf16[256,640]{1,0:T(8,128)(2,1)S(1)} %get-tuple-element.223), channel_id=1, source_target_pairs={{0,2},{1,3},{2,0},{3,1},{4,6},{5,7},{6,4},{7,5},{8,10},{9,11},{10,... | collective-permute-start | bytes 983048 | tf_op jit(solution)/shard_map/ppermute | solution.py:556
  388.9 32.8 %collective-permute-start.57 = (bf16[256,640]{1,0:T(8,128)(2,1)S(1)}, bf16[256,640]{1,0:T(8,128)(2,1)S(1)}, u32[]{:S(2)}, u32[]{:S(2)}) collective-permute-start(bf16[256,640]{1,0:T(8,128)(2,1)S(1)} %get-tuple-element.224), channel_id=1, source_target_pairs={{0,1},{1,0},{2,3},{3,2},{4,5},{5,4},{6,7},{7,6},{8,9},{9,8},{10,11... | collective-permute-start | bytes 983048 | tf_op jit(solution)/shard_map/ppermute | solution.py:556
  390.4 23.6 %collective-permute-start.42 = (bf16[256,1024]{1,0:T(8,128)(2,1)S(1)}, bf16[256,1024]{1,0:T(8,128)(2,1)S(1)}, u32[]{:S(2)}, u32[]{:S(2)}) collective-permute-start(bf16[256,1024]{1,0:T(8,128)(2,1)S(1)} %get-tuple-element.231), channel_id=1, source_target_pairs={{1,0},{0,1},{5,2},{4,3},{3,4},{2,5},{7,6},{6,7},{9,8},{8,9},{13,10... | collective-permute-start | bytes 1572872 | tf_op jit(solution)/shard_map/ppermute | solution.py:594
  395.4 24.7 %collective-permute-start.43 = (bf16[256,1024]{1,0:T(8,128)(2,1)S(1)}, bf16[256,1024]{1,0:T(8,128)(2,1)S(1)}, u32[]{:S(2)}, u32[]{:S(2)}) collective-permute-start(bf16[256,1024]{1,0:T(8,128)(2,1)S(1)} %get-tuple-element.232), channel_id=1, source_target_pairs={{0,0},{1,1},{4,2},{5,3},{2,4},{3,5},{6,6},{7,7},{8,8},{9,9},{12,10... | collective-permute-start | bytes 1572872 | tf_op jit(solution)/shard_map/ppermute | solution.py:594
  397.5 32.6 %collective-permute-start.54 = (bf16[256,384]{1,0:T(8,128)(2,1)S(1)}, bf16[256,384]{1,0:T(8,128)(2,1)S(1)}, u32[]{:S(2)}, u32[]{:S(2)}) collective-permute-start(bf16[256,384]{1,0:T(8,128)(2,1)S(1)} %pad_maximum_fusion.20), channel_id=1, source_target_pairs={{0,1},{1,0},{2,3},{3,2},{4,5},{5,4},{6,7},{7,6},{8,9},{9,8},{10,11... | collective-permute-start | bytes 589832 | tf_op jit(solution)/shard_map/ppermute | solution.py:556
  (118 other events, 1007.9 us)
